TPU v7x, 128 devices: a whole 4x4x4 slice. The times are simulated.
128 devices in a mesh: seq: 128 (over x, y, z, core).
Axes of the slice: x: 4, y: 4, z: 4, core: 2. Of those that a mesh axis runs over, the one named last changes fastest.
Arguments:
- tokens: bfloat16 [65536, 2048], P('seq'), may hold values from -48 to 48
- w_row: bfloat16 [2048, 3072], replicated, may hold values from -0.21875 to 0.21875
- w_column: bfloat16 [2048, 3072], replicated, may hold values from -0.21875 to 0.21875
Outputs:
- attended: bfloat16 [65536, 2048], P('seq')
All inputs are finite; a program needn't handle non-finite values.
Results may differ from a plain program's by a relative error of at most 0.011.
The roundings to bfloat16 on the way count: a program that leaves them out, or rounds other values in their place, can miss the bound.
Values may be sent and summed in bfloat16 or wider, within the bound.
No kernel may reach another device: no remote copies, remote signals or barrier semaphores. Data moves between devices by JAX's collectives and lax.ppermute only.
A program may use at most 128 MiB of HBM per device.

v0:
```python
import jax
import jax.numpy as jnp
from jax import lax
from jax.sharding import PartitionSpec as P

HEAD = 128
HEADS = 8
STRIDE = 1024


def passed_along(value, axis, steps):
    count = lax.axis_size(axis)
    leading, last = (max(0, -steps), min(count, count - steps))
    return lax.ppermute(value, axis, [(source, source + steps) for source in range(leading, last)])


def softmax_rounded(scores):
    top = jnp.max(scores, axis=-1, keepdims=True)
    expd = jnp.exp(scores - top)
    return (expd / jnp.sum(expd, axis=-1, keepdims=True)).astype(jnp.bfloat16)


def band_attention(row_proj, rank, tok):
    width = HEADS * HEAD
    scale = 1.0 / HEAD**0.5
    keyval = row_proj[:, width:]
    reach = STRIDE // tok
    pieces = []
    for step in range(reach, 0, -1):
        pieces.append(passed_along(keyval, "seq", step))
    pieces.append(keyval)
    gathered = jnp.concatenate(pieces, axis=0)
    keys = gathered[:, :width].reshape(-1, HEADS, HEAD)
    values = gathered[:, width:].reshape(-1, HEADS, HEAD)
    query = row_proj[:, :width].reshape(tok, HEADS, HEAD)
    scores = jnp.einsum("thd,uhd->htu", query, keys, preferred_element_type=jnp.float32) * scale
    tpos = jnp.arange(tok, dtype=jnp.int32)[:, None]
    upos = jnp.arange(STRIDE + tok, dtype=jnp.int32)[None, :]
    diff = tpos + STRIDE - upos
    keypos = rank * tok - STRIDE + upos
    allowed = (diff >= 0) & (diff <= STRIDE - 1) & (keypos >= 0)
    scores = jnp.where(allowed[None], scores, -jnp.inf)
    weights = softmax_rounded(scores)
    out = jnp.einsum("htu,uhd->thd", weights, values, preferred_element_type=jnp.float32)
    return out.astype(jnp.bfloat16).reshape(tok, width)


def column_attend(projected, rows, blocks):
    width = HEADS * HEAD
    scale = 1.0 / HEAD**0.5
    items = projected.shape[0]
    shaped = projected.reshape(items, rows, blocks, 3 * width)
    query = shaped[..., :width].reshape(items, rows, blocks, HEADS, HEAD)
    keys = shaped[..., width : 2 * width].reshape(items, rows, blocks, HEADS, HEAD)
    values = shaped[..., 2 * width :].reshape(items, rows, blocks, HEADS, HEAD)
    scores = (
        jnp.einsum("jrbhd,jsbhd->jbhrs", query, keys, preferred_element_type=jnp.float32) * scale
    )
    rpos = jnp.arange(rows, dtype=jnp.int32)
    allowed = rpos[None, :] <= rpos[:, None]
    scores = jnp.where(allowed[None, None, None], scores, -jnp.inf)
    weights = softmax_rounded(scores)
    out = jnp.einsum("jbhrs,jsbhd->jrbhd", weights, values, preferred_element_type=jnp.float32)
    out = out.astype(jnp.bfloat16).reshape(items, rows * blocks, width)
    return lax.all_to_all(out, "seq", split_axis=1, concat_axis=1, tiled=True)


def on_device(tokens, w_row, w_column):
    count = lax.axis_size("seq")
    rank = lax.axis_index("seq")
    tok = tokens.shape[0]
    width = HEADS * HEAD
    rows = count * tok // STRIDE
    blocks = STRIDE // tok
    row_proj = jnp.dot(tokens, w_row, preferred_element_type=jnp.float32).astype(jnp.bfloat16)
    col_proj = jnp.dot(tokens, w_column, preferred_element_type=jnp.float32).astype(jnp.bfloat16)
    col_proj = col_proj.reshape(tok // count, count, 3 * width)
    col_out = column_attend(
        lax.all_to_all(col_proj, "seq", split_axis=1, concat_axis=1, tiled=True), rows, blocks
    )
    band_out = band_attention(row_proj, rank, tok)
    return jnp.concatenate([band_out, col_out.reshape(tok, width)], axis=1)


def solution(mesh):
    in_specs = (P("seq", None), P(), P())
    out_specs = P("seq", None)
    return jax.shard_map(
        on_device, mesh=mesh, in_specs=in_specs, out_specs=out_specs, check_vma=False
    )
```

profile of v0, /device:TPU:0, one launch (start us, length us, event | category | flops | bytes accessed | tf_op | source)
XLA Modules:
  0.0 205.4 jit_solution(15935761213858890006)
XLA Ops:
  0.0 0.0 copy-start
  0.0 1.6 copy-done
  1.6 0.0 copy-start.6
  1.6 9.8 %convolution_convert_fusion.1 = bf16[512,3072]{1,0:T(8,128)(2,1)S(1)} fusion(bf16[512,2048]{1,0:T(8,128)(2,1)S(1)} %copy-done, bf16[2048,3072]{1,0:T(8,128)(2,1)} %param.4), kind=kOutput, calls=%fused_computation.12 | convolution fusion | flops 6444023808 | bytes 17825792 | tf_op jit(solution)/shard_map/dot_general | solution.py:75
  11.4 0.0 copy-start.4
  11.4 1.6 slice.28
  12.9 5.3 %collective-permute-start = (bf16[512,2048]{1,0:T(8,128)(2,1)}, bf16[512,2048]{1,0:T(8,128)(2,1)}, u32[]{:S(2)}, u32[]{:S(2)}) collective-permute-start(bf16[512,2048]{1,0:T(8,128)(2,1)} %slice.28), channel_id=1, source_target_pairs={{0,2},{1,3},{2,4},{3,5},{4,6},{5,7},{6,8},{7,9},{8,10},{9,11},{10,... | collective-permute-start | bytes 6291464 | tf_op jit(solution)/shard_map/ppermute | solution.py:14
  18.2 0.0 copy-done.4
  18.2 2.8 %collective-permute-start.1 = (bf16[512,2048]{1,0:T(8,128)(2,1)}, bf16[512,2048]{1,0:T(8,128)(2,1)}, u32[]{:S(2)}, u32[]{:S(2)}) collective-permute-start(bf16[512,2048]{1,0:T(8,128)(2,1)} %slice.28), channel_id=1, source_target_pairs={{0,1},{1,2},{2,3},{3,4},{4,5},{5,6},{6,7},{7,8},{8,9},{9,10},{10,1... | collective-permute-start | bytes 6291464 | tf_op jit(solution)/shard_map/ppermute | solution.py:14
  21.0 0.0 copy-done.6
  21.0 6.9 %convolution_convert_fusion = bf16[512,3072]{1,0:T(8,128)(2,1)S(1)} fusion(bf16[512,2048]{1,0:T(8,128)(2,1)S(1)} %copy-done, bf16[2048,3072]{1,0:T(8,128)(2,1)S(1)} %copy-done.6), kind=kOutput, calls=%fused_computation.11 | convolution fusion | flops 6444023808 | bytes 17825792 | tf_op jit(solution)/shard_map/dot_general | solution.py:76
  28.0 4.1 %copy.48 = bf16[4,128,3072]{2,0,1:T(4,128)(2,1)} copy(bf16[4,128,3072]{2,1,0:T(8,128)(2,1)S(1)} %bitcast.65) | data formatting | bytes 6291456 | tf_op jit(solution)/shard_map/reshape | solution.py:77
  32.0 8.6 %all-to-all-start = ((bf16[4,128,3072]{2,0,1:T(4,128)(2,1)}), bf16[4,128,3072]{2,0,1:T(4,128)(2,1)S(1)}, u32[]{:S(2)}, u32[]{:S(2)}) async-start(bf16[4,128,3072]{2,0,1:T(4,128)(2,1)} %copy.48), calls=%async_computation | async-start | bytes 6291456 | tf_op jit(solution)/shard_map/all_to_all | solution.py:79
  40.7 1.8 fusion.16
  42.5 52.3 %collective-permute-done = bf16[512,2048]{1,0:T(8,128)(2,1)} collective-permute-done((bf16[512,2048]{1,0:T(8,128)(2,1)}, bf16[512,2048]{1,0:T(8,128)(2,1)}, u32[]{:S(2)}, u32[]{:S(2)}) %collective-permute-start) | collective-permute-done | bytes 2097184 | tf_op jit(solution)/shard_map/ppermute | solution.py:14
  94.8 0.0 collective-permute-done.1
  94.8 3.8 %pad_maximum_fusion = bf16[1536,2048]{1,0:T(8,128)(2,1)S(1)} fusion(bf16[512,2048]{1,0:T(8,128)(2,1)} %slice.28, bf16[512,2048]{1,0:T(8,128)(2,1)} %collective-permute-done.1, bf16[512,2048]{1,0:T(8,128)(2,1)} %collective-permute-done), kind=kLoop, calls=%fused_computation.10 | loop fusion | flops 18874368 | bytes 12582912 | tf_op jit(solution)/shard_map/concatenate | solution.py:32
  98.6 4.1 %slice_bitcast_fusion = (bf16[192,8,8,128]{3,2,1,0:T(8,128)(2,1)}, bf16[1536,1024]{1,0:T(8,128)(2,1)}) fusion(bf16[1536,2048]{1,0:T(8,128)(2,1)S(1)} %pad_maximum_fusion), kind=kLoop, calls=%fused_computation.15 | loop fusion | bytes 12582912
  102.8 39.7 %all-to-all-done = bf16[4,128,3072]{2,0,1:T(4,128)(2,1)S(1)} async-done(((bf16[4,128,3072]{2,0,1:T(4,128)(2,1)}), bf16[4,128,3072]{2,0,1:T(4,128)(2,1)S(1)}, u32[]{:S(2)}, u32[]{:S(2)}) %all-to-all-start) | async-done | bytes 3145760 | tf_op jit(solution)/shard_map/all_to_all | solution.py:79
  142.5 2.9 %fusion.67 = (bf16[4,64,2,1024]{3,0,2,1:T(4,128)(2,1)}, bf16[4,64,2,1024]{3,0,2,1:T(4,128)(2,1)}, bf16[4,64,2,1024]{3,0,2,1:T(4,128)(2,1)}) fusion(bf16[4,64,2,3072]{3,0,2,1:T(4,128)(2,1)S(1)} %bitcast.62), kind=kLoop, calls=%fused_computation.53 | loop fusion | bytes 6291456 | tf_op jit(solution)/shard_map/slice | solution.py:55
  145.4 0.0 copy-start.3
  145.4 1.6 reshape.110
  147.0 1.5 reshape.111
  148.5 0.0 copy-done.3
  148.5 1.2 reshape.109
  149.7 0.0 copy-start.5
  149.7 3.2 %fusion.68 = (f32[4,2,8,64]{3,2,1,0:T(8,128)S(1)}, f32[4,2,8,64,64]{3,4,2,1,0:T(8,128)}) fusion(pred[64,64]{0,1:T(8,128)(4,1)S(1)} %iota_compare_fusion, bf16[4,64,2,8,128]{4,3,0,2,1:T(8,128)(2,1)S(1)} %reshape.111, bf16[4,64,2,8,128]{4,3,0,2,1:T(8,128)(2,1)S(1)} %reshape.110), kind=kOutput, calls=%fused_computation.54 | convolution fusion | flops 68157504 | bytes 3166208 | tf_op jit(solution)/shard_map/sub | solution.py:19
  153.0 0.0 copy-done.5
  153.0 2.9 %fusion.24 = bf16[4,64,2,8,128]{4,1,3,2,0:T(8,128)(2,1)S(1)} fusion(f32[4,2,8,64,64]{3,4,2,1,0:T(8,128)} %get-tuple-element.11, bf16[4,64,2,8,128]{4,3,0,2,1:T(8,128)(2,1)S(1)} %copy-done.5, f32[4,2,8,64]{3,2,1,0:T(8,128)S(1)} %get-tuple-element.10), kind=kOutput, calls=%fused_computation.30 | convolution fusion | flops 68157440 | bytes 3162112 | tf_op jit(solution)/shard_map/jbhrs,jsbhd->jrbhd/dot_general | solution.py:63
  155.8 0.7 copy.68
  156.5 1.1 reshape.112
  157.6 15.7 %all-to-all-start.1 = ((bf16[4,128,1024]{2,0,1:T(4,128)(2,1)}), bf16[4,128,1024]{2,0,1:T(4,128)(2,1)}, u32[]{:S(2)}, u32[]{:S(2)}) async-start(bf16[4,128,1024]{2,0,1:T(4,128)(2,1)} %reshape.112), calls=%async_computation.1 | async-start | bytes 2097152 | tf_op jit(solution)/shard_map/all_to_all | solution.py:65
  173.4 0.0 copy-start.2
  173.4 10.6 %fusion.73 = f32[8,512]{1,0:T(8,128)S(1)} fusion(pred[512,1536]{1,0:T(8,128)(4,1)} %fusion.16, bf16[192,8,8,128]{3,2,1,0:T(8,128)(2,1)} %get-tuple-element.5, bf16[512,3072]{1,0:T(8,128)(2,1)} %copy-done.4), kind=kOutput, calls=%fused_computation.55 | convolution fusion | flops 1635780096 | bytes 4997120 | tf_op jit(solution)/shard_map/sub | solution.py:19
  184.0 0.0 copy-done.2
  184.0 3.0 %copy.61 = bf16[1536,1024]{0,1:T(8,128)(2,1)} copy(bf16[1536,1024]{1,0:T(8,128)(2,1)S(1)} %copy-done.2) | data formatting | bytes 6291456 | tf_op jit(solution)/shard_map/reshape | solution.py:34
  187.0 13.7 %fusion.23 = bf16[8,128,512]{2,1,0:T(8,128)(2,1)} fusion(bf16[1536,8,128]{0,2,1:T(8,128)(2,1)} %bitcast.64, f32[8,512]{1,0:T(8,128)S(1)} %fusion.73, pred[512,1536]{1,0:T(8,128)(4,1)} %fusion.16, bf16[192,8,8,128]{3,2,1,0:T(8,128)(2,1)} %get-tuple-element.5, bf16[512,3072]{1,0:T(8,128)(2,1)} %copy-done.4), kind=kOutput, calls=%fused_computation.28 | convolution fusion | flops 3253212672 | bytes 9191424 | tf_op jit(solution)/shard_map/htu,uhd->thd/dot_general | solution.py:44
  200.7 0.0 copy-start.1
  200.7 1.6 copy.59
  202.4 0.0 all-to-all-done.1
  202.4 1.5 copy.58
  203.9 1.5 pad_maximum_fusion.1
  205.4 0.0 copy-done.1
  (3 shorter events, 0.0 us)
Async XLA Ops:
  0.0 1.6 copy-start
  1.6 19.5 %copy-start.6 = (bf16[2048,3072]{1,0:T(8,128)(2,1)S(1)}, bf16[2048,3072]{1,0:T(8,128)(2,1)}, u32[]{:S(2)}) copy-start(bf16[2048,3072]{1,0:T(8,128)(2,1)} %param.5) | copy-start | bytes 37748740
  11.4 6.8 %copy-start.4 = (bf16[512,3072]{1,0:T(8,128)(2,1)}, bf16[512,3072]{1,0:T(8,128)(2,1)S(1)}, u32[]{:S(2)}) copy-start(bf16[512,3072]{1,0:T(8,128)(2,1)S(1)} %convolution_convert_fusion.1) | copy-start | bytes 9437188
  12.9 81.8 %collective-permute-start = (bf16[512,2048]{1,0:T(8,128)(2,1)}, bf16[512,2048]{1,0:T(8,128)(2,1)}, u32[]{:S(2)}, u32[]{:S(2)}) collective-permute-start(bf16[512,2048]{1,0:T(8,128)(2,1)} %slice.28), channel_id=1, source_target_pairs={{0,2},{1,3},{2,4},{3,5},{4,6},{5,7},{6,8},{7,9},{8,10},{9,11},{10,... | collective-permute-start | bytes 6291464 | tf_op jit(solution)/shard_map/ppermute | solution.py:14
  18.2 76.6 %collective-permute-start.1 = (bf16[512,2048]{1,0:T(8,128)(2,1)}, bf16[512,2048]{1,0:T(8,128)(2,1)}, u32[]{:S(2)}, u32[]{:S(2)}) collective-permute-start(bf16[512,2048]{1,0:T(8,128)(2,1)} %slice.28), channel_id=1, source_target_pairs={{0,1},{1,2},{2,3},{3,4},{4,5},{5,6},{6,7},{7,8},{8,9},{9,10},{10,1... | collective-permute-start | bytes 6291464 | tf_op jit(solution)/shard_map/ppermute | solution.py:14
  32.0 110.5 %all-to-all-start = ((bf16[4,128,3072]{2,0,1:T(4,128)(2,1)}), bf16[4,128,3072]{2,0,1:T(4,128)(2,1)S(1)}, u32[]{:S(2)}, u32[]{:S(2)}) async-start(bf16[4,128,3072]{2,0,1:T(4,128)(2,1)} %copy.48), calls=%async_computation | async-start | bytes 6291456 | tf_op jit(solution)/shard_map/all_to_all | solution.py:79
  145.4 3.0 %copy-start.3 = (bf16[4,64,2,1024]{3,0,2,1:T(4,128)(2,1)S(1)}, bf16[4,64,2,1024]{3,0,2,1:T(4,128)(2,1)}, u32[]{:S(2)}) copy-start(bf16[4,64,2,1024]{3,0,2,1:T(4,128)(2,1)} %get-tuple-element.7) | copy-start | bytes 3145732
  149.7 3.3 %copy-start.5 = (bf16[4,64,2,8,128]{4,3,0,2,1:T(8,128)(2,1)S(1)}, bf16[4,64,2,8,128]{4,3,0,2,1:T(8,128)(2,1)}, u32[]{:S(2)}) copy-start(bf16[4,64,2,8,128]{4,3,0,2,1:T(8,128)(2,1)} %reshape.109) | copy-start | bytes 3145732
  157.6 44.7 %all-to-all-start.1 = ((bf16[4,128,1024]{2,0,1:T(4,128)(2,1)}), bf16[4,128,1024]{2,0,1:T(4,128)(2,1)}, u32[]{:S(2)}, u32[]{:S(2)}) async-start(bf16[4,128,1024]{2,0,1:T(4,128)(2,1)} %reshape.112), calls=%async_computation.1 | async-start | bytes 2097152 | tf_op jit(solution)/shard_map/all_to_all | solution.py:65
  173.4 10.6 %copy-start.2 = (bf16[1536,1024]{1,0:T(8,128)(2,1)S(1)}, bf16[1536,1024]{1,0:T(8,128)(2,1)}, u32[]{:S(2)}) copy-start(bf16[1536,1024]{1,0:T(8,128)(2,1)} %get-tuple-element.6) | copy-start | bytes 9437188
  200.7 4.7 %copy-start.1 = (bf16[512,2048]{1,0:T(8,128)(2,1)S(1)}, bf16[512,2048]{1,0:T(8,128)(2,1)}, u32[]{:S(2)}) copy-start(bf16[512,2048]{1,0:T(8,128)(2,1)} %param.3) | copy-start | bytes 6291460
where the time goes:
time: 206 us; the launch traced here: 205 us
  waiting for transfers between devices  92 us (45%)
  matrix products  47.1 us (23%)
  starting transfers between devices  32.5 us (16%)
  local copies, waits for them, and re-layouts  26.5 us (13%)
  other arithmetic  7.16 us (3%)
    ppermute x2, waiting for transfers between devices, passed_along(): lax.ppermute(value, axis, [(source, source + steps) for source in range(l...  52.3 us
    all_to_all x1, waiting for transfers between devices, on_device(): lax.all_to_all(col_proj, 'seq', split_axis=1, concat_axis=1, tiled=True)  39.7 us
    all_to_all x1, starting transfers between devices, column_attend(): return lax.all_to_all(out, 'seq', split_axis=1, concat_axis=1, tiled=True)  15.7 us
    sub x2, matrix products, softmax_rounded(): expd = jnp.exp(scores - top)  13.9 us
    dot_general x1, matrix products, band_attention(): jnp.einsum('htu,uhd->thd', weights, values, preferred_element_type=jnp.fl...  13.7 us
    dot_general x1, matrix products, on_device(): jnp.dot(tokens, w_row, preferred_element_type=jnp.float32)  9.78 us
    all_to_all x1, starting transfers between devices, on_device(): lax.all_to_all(col_proj, 'seq', split_axis=1, concat_axis=1, tiled=True)  8.65 us
    ppermute x2, starting transfers between devices, passed_along(): lax.ppermute(value, axis, [(source, source + steps) for source in range(l...  8.09 us
  transfers between devices with their start and end apart: 4, of which 2 were waited for; matrix products, arithmetic and copies ran while one was open for 24% of the time, Pallas kernels for 0%

commit v1 on v0

v1 whole, which is shorter than its diff:
```python
import functools

import jax
import jax.numpy as jnp
from jax import lax
from jax.experimental import pallas as pl
from jax.experimental.pallas import tpu as pltpu
from jax.sharding import PartitionSpec as P

HEAD = 128
HEADS = 8
STRIDE = 1024
HALF = 512
SCALE = 1.0 / HEAD**0.5
NEG = -1e30
VMEM_LIMIT = 48 << 20
STAT_ROWS = 32
PAYLOAD = HALF + STAT_ROWS


def params():
    return pltpu.CompilerParams(vmem_limit_bytes=VMEM_LIMIT)


def cost(flops, data):
    return pl.CostEstimate(flops=flops, bytes_accessed=data, transcendentals=0)


def project_kernel(core_ref, x_ref, w_ref, *refs):
    q_ref, kv_ref = refs[-2:]
    part = pl.program_id(0)
    value = jnp.dot(x_ref[...], w_ref[...], preferred_element_type=jnp.float32)
    value = value.astype(jnp.bfloat16)

    @pl.when(part == 0)
    def _():
        q_ref[...] = value

    @pl.when(part > 0)
    def _():
        kv_ref[...] = value


def project_band(core, tokens, w_row, own, before=None):
    depth = tokens.shape[1]
    half = (lambda c: c[0]) if own else (lambda c: 1 - c[0])
    aliased = [] if before is None else list(before)
    return pl.pallas_call(
        project_kernel,
        grid_spec=pltpu.PrefetchScalarGridSpec(
            num_scalar_prefetch=1,
            grid=(3,),
            in_specs=[
                pl.BlockSpec((HALF, depth), lambda j, c: (0, 0)),
                pl.BlockSpec((depth, HALF), lambda j, c: (0, 2 * j + c[0])),
            ]
            + [pl.BlockSpec(memory_space=pl.ANY)] * len(aliased),
            out_specs=[
                pl.BlockSpec((HALF, HALF), lambda j, c: (half(c), 0)),
                pl.BlockSpec((HALF, HALF), lambda j, c: (half(c), jnp.maximum(j - 1, 0))),
            ],
        ),
        out_shape=[
            jax.ShapeDtypeStruct((STRIDE, HALF), jnp.bfloat16),
            jax.ShapeDtypeStruct((STRIDE, STRIDE), jnp.bfloat16),
        ],
        input_output_aliases={3 + i: i for i in range(len(aliased))},
        compiler_params=params(),
        cost_estimate=cost(2 * HALF * depth * 3 * HALF, (HALF * depth + depth * 3 * HALF + HALF * 3 * HALF) * 2),
        name="project_band",
    )(core, tokens, w_row, *aliased)


def attend(queries, keys, values_t, allowed):
    scores = lax.dot_general(
        keys, queries, (((1,), (1,)), ((), ())), preferred_element_type=jnp.float32
    )
    if allowed is not None:
        scores = jnp.where(allowed, scores, NEG)
    top = jnp.max(scores, axis=0, keepdims=True)
    expd = jnp.exp((scores - top) * SCALE)
    total = jnp.sum(expd, axis=0, keepdims=True)
    out = jnp.dot(values_t, expd.astype(jnp.bfloat16), preferred_element_type=jnp.float32)
    return out * (1.0 / total), top, total


def split3(value):
    high = value.astype(jnp.bfloat16).astype(jnp.float32)
    rest = value - high
    mid = rest.astype(jnp.bfloat16).astype(jnp.float32)
    return high, mid, rest - mid


def band_kernel(earlier, core_ref, q_ref, k_ref, v_ref, same_ref, cross_ref, stat_ref):
    head = pl.program_id(0)
    core = core_ref[0]
    block = 256
    values_t = v_ref[...].astype(jnp.float32).T.astype(jnp.bfloat16)
    for part in range(STRIDE // block):
        low, high = (part * block, STRIDE) if earlier else (0, (part + 1) * block)
        shape = (high - low, block)
        kpos = low + lax.broadcasted_iota(jnp.int32, shape, 0)
        qpos = part * block + lax.broadcasted_iota(jnp.int32, shape, 1)
        allowed = kpos > qpos if earlier else kpos <= qpos
        out, top, total = attend(
            q_ref[part * block : (part + 1) * block, :],
            k_ref[low:high, :],
            values_t[:, low:high],
            allowed,
        )
        out = out.astype(jnp.bfloat16)
        half, column = divmod(part * block, HALF)
        rows = pl.ds(pl.multiple_of(head * HEAD, HEAD), HEAD)

        @pl.when(core == half)
        def _():
            same_ref[rows, column : column + block] = out

        @pl.when(core != half)
        def _():
            cross_ref[rows, column : column + block] = out

        stats = jnp.concatenate(
            list(split3(top)) + list(split3(total)) + [jnp.zeros((2, block), jnp.float32)], axis=0
        )
        stat_ref[head, :, part * block : (part + 1) * block] = stats

    @pl.when(head == 3)
    def _():
        stats = jnp.concatenate([stat_ref[h] for h in range(4)], axis=0).astype(jnp.bfloat16)
        for half in range(2):
            piece = stats[:, half * HALF : (half + 1) * HALF]

            @pl.when(core == half)
            def _():
                same_ref[HALF:PAYLOAD, :] = piece

            @pl.when(core != half)
            def _():
                cross_ref[HALF:PAYLOAD, :] = piece


def band_part(earlier, core, query, keyval):
    whole = pl.BlockSpec((PAYLOAD, HALF), lambda h, c: (0, 0))
    return pl.pallas_call(
        functools.partial(band_kernel, earlier),
        grid_spec=pltpu.PrefetchScalarGridSpec(
            num_scalar_prefetch=1,
            grid=(4,),
            in_specs=[
                pl.BlockSpec((STRIDE, HEAD), lambda h, c: (0, h)),
                pl.BlockSpec((STRIDE, HEAD), lambda h, c: (0, h)),
                pl.BlockSpec((STRIDE, HEAD), lambda h, c: (0, 4 + h)),
            ],
            out_specs=[whole, whole],
            scratch_shapes=[pltpu.VMEM((4, 8, STRIDE), jnp.float32)],
        ),
        out_shape=[jax.ShapeDtypeStruct((PAYLOAD, HALF), jnp.bfloat16)] * 2,
        compiler_params=params(),
        cost_estimate=cost(5 * 10**9, 8 << 20),
        name="band_earlier" if earlier else "band_local",
    )(core, query, keyval, keyval)


def column_kernel(q_ref, k_ref, v_ref, o_ref, *, group):
    rows = q_ref.shape[0]
    block = 256
    values_t = v_ref[...].astype(jnp.float32).T.astype(jnp.bfloat16)
    for part in range(rows // block):
        high = (part + 1) * block
        shape = (high, block)
        kpos = lax.broadcasted_iota(jnp.int32, shape, 0)
        qpos = part * block + lax.broadcasted_iota(jnp.int32, shape, 1)
        allowed = (kpos <= qpos) & (((qpos - kpos) & (group - 1)) == 0)
        out, _, _ = attend(
            q_ref[part * block : high, :], k_ref[:high, :], values_t[:, :high], allowed
        )
        o_ref[part * block : high, :] = out.T.astype(jnp.bfloat16)


def column_attention(projected, group):
    rows = projected.shape[0]
    spec = lambda third: pl.BlockSpec((rows, HEAD), lambda h: (0, third * HEADS + h))
    return pl.pallas_call(
        functools.partial(column_kernel, group=group),
        grid=(HEADS,),
        in_specs=[spec(0), spec(1), spec(2)],
        out_specs=pl.BlockSpec((rows, HEAD), lambda h: (0, h)),
        out_shape=jax.ShapeDtypeStruct((rows, HEADS * HEAD), jnp.bfloat16),
        compiler_params=params(),
        cost_estimate=cost(3 * 10**9, 4 << 20),
        name="column_attention",
    )(projected, projected, projected)


def merge_kernel(flags_ref, local_ref, earlier_ref, o_ref):
    has_earlier = flags_ref[1] > 0
    for head in range(4):
        def stats(ref):
            s = ref[0, HALF : HALF + STAT_ROWS, :].astype(jnp.float32)[8 * head : 8 * head + 8]
            return s[0:1] + s[1:2] + s[2:3], s[3:4] + s[4:5] + s[5:6]

        top_l, sum_l = stats(local_ref)
        top_e, sum_e = stats(earlier_ref)
        top_e = jnp.where(has_earlier, top_e, NEG)
        top = jnp.maximum(top_l, top_e)
        weight_l = jnp.exp((top_l - top) * SCALE) * sum_l
        weight_e = jnp.exp((top_e - top) * SCALE) * sum_e
        weight_e = jnp.where(has_earlier, weight_e, 0.0)
        inverse = 1.0 / (weight_l + weight_e)
        rows = slice(head * HEAD, (head + 1) * HEAD)
        out_l = local_ref[0, rows, :].astype(jnp.float32)
        out_e = earlier_ref[0, rows, :].astype(jnp.float32)
        out = out_l * (weight_l * inverse) + out_e * (weight_e * inverse)
        o_ref[:, rows] = out.T.astype(jnp.bfloat16)


def merge_band(flags, local, earlier):
    return pl.pallas_call(
        merge_kernel,
        grid_spec=pltpu.PrefetchScalarGridSpec(
            num_scalar_prefetch=1,
            grid=(2,),
            in_specs=[
                pl.BlockSpec((1, PAYLOAD, HALF), lambda j, c: (j, 0, 0)),
                pl.BlockSpec((1, PAYLOAD, HALF), lambda j, c: (j, 0, 0)),
            ],
            out_specs=pl.BlockSpec((HALF, HALF), lambda j, c: (0, j + c[0] - 2 * j * c[0])),
        ),
        out_shape=jax.ShapeDtypeStruct((HALF, 2 * HALF), jnp.bfloat16),
        compiler_params=params(),
        cost_estimate=cost(10**7, 4 << 20),
        name="merge_band",
    )(flags, local, earlier)


def on_device(tokens, w_row, w_column):
    count = lax.axis_size("seq")
    chips = count // 2
    rank = lax.axis_index("seq")
    core = (rank % 2).astype(jnp.int32)
    core_arr = core.reshape(1)
    flags = jnp.stack([core, (rank >= 2).astype(jnp.int32)])
    group = HALF // chips
    same_core = [list(range(0, count, 2)), list(range(1, count, 2))]
    swap = [(d, d ^ 1) for d in range(count)]

    def exchange(value):
        width = value.shape[1]
        value = lax.all_to_all(
            value.reshape(chips, group, width), "seq", split_axis=0, concat_axis=0,
            axis_index_groups=same_core, tiled=True,
        )
        return value.reshape(HALF, width)

    columns = exchange(tokens)
    sibling = lax.ppermute(tokens, "seq", swap)

    projected = project_band(core_arr, tokens, w_row, True)
    query, keyval = project_band(core_arr, sibling, w_row, False, projected)
    next_query = lax.ppermute(query, "seq", [(d, d - 2) for d in range(2, count)])
    local_same, local_cross = band_part(False, core_arr, query, keyval)
    local_cross = lax.ppermute(local_cross, "seq", swap)
    early_same, early_cross = band_part(True, core_arr, next_query, keyval)
    early_same = lax.ppermute(early_same, "seq", [(d, d + 2) for d in range(count - 2)])
    early_cross = lax.ppermute(
        early_cross, "seq", [(d, (d + 2) ^ 1) for d in range(count - 2)]
    )

    col_proj = jnp.dot(columns, w_column, preferred_element_type=jnp.float32).astype(jnp.bfloat16)
    col_out = exchange(column_attention(col_proj, group))
    band_out = merge_band(
        flags, jnp.stack([local_same, local_cross]), jnp.stack([early_same, early_cross])
    )
    return jnp.concatenate([band_out, col_out], axis=1)


def solution(mesh):
    in_specs = (P("seq", None), P(), P())
    out_specs = P("seq", None)
    return jax.shard_map(
        on_device, mesh=mesh, in_specs=in_specs, out_specs=out_specs, check_vma=False
    )
```

time: 206 us -> 133 us (0.65)
  the two profiles are of different devices: /device:TPU:0 before, /device:TPU:7 now
where the time goes in v1:
time: 133 us; the launch traced here: 132 us
  Pallas kernels  46.5 us (35%)
  starting transfers between devices  35.5 us (27%)
  waiting for transfers between devices  32.4 us (24%)
  matrix products  10.3 us (8%)
  other arithmetic  4.1 us (3%)
  local copies, waits for them, and re-layouts  3.12 us (2%)
    pallas_call x2, Pallas kernels, band_part(): pl.pallas_call(functools.partial(band_kernel, earlier), grid_spec=pltpu.P...  24 us
    all_to_all x2, starting transfers between devices, exchange(): lax.all_to_all(value.reshape(chips, group, width), 'seq', split_axis=0, c...  19.5 us
    ppermute x1, waiting for transfers between devices, on_device(): lax.ppermute(early_same, 'seq', [(d, d + 2) for d in range(count - 2)])  12.9 us
    pallas_call x2, Pallas kernels, project_band(): pl.pallas_call(project_kernel, grid_spec=pltpu.PrefetchScalarGridSpec(num...  12.4 us
    ppermute x1, waiting for transfers between devices, on_device(): lax.ppermute(early_cross, 'seq', [(d, d + 2 ^ 1) for d in range(count - 2)])  12 us
    dot_general x1, matrix products, on_device(): jnp.dot(columns, w_column, preferred_element_type=jnp.float32)  10.3 us
    pallas_call x1, Pallas kernels, column_attention(): pl.pallas_call(functools.partial(column_kernel, group=group), grid=(HEADS...  8.59 us
    all_to_all x2, waiting for transfers between devices, exchange(): lax.all_to_all(value.reshape(chips, group, width), 'seq', split_axis=0, c...  7.42 us
  transfers between devices with their start and end apart: 7, of which 3 were waited for; matrix products, arithmetic and copies ran while one was open for 9% of the time, Pallas kernels for 35%

profile of v1, /device:TPU:7, one launch (start us, length us, event | category | flops | bytes accessed | tf_op | source)
XLA Modules:
  0.0 132.0 jit_solution(15538455461572569224)
XLA Ops:
  0.0 0.7 collective-permute-start
  0.7 0.0 copy-start
  0.7 11.4 %all-to-all-start = ((bf16[64,8,2048]{2,1,0:T(8,128)(2,1)}), bf16[64,8,2048]{2,1,0:T(8,128)(2,1)}, u32[]{:S(2)}, u32[]{:S(2)}) async-start(bf16[64,8,2048]{2,1,0:T(8,128)(2,1)} %bitcast.13), calls=%async_computation | async-start | bytes 4194304 | tf_op jit(solution)/shard_map/all_to_all | solution.py:250
  12.1 0.0 copy-done
  12.1 5.9 %project_band.2 = (bf16[1024,512]{1,0:T(8,128)(2,1)S(1)}, bf16[1024,1024]{1,0:T(8,128)(2,1)S(1)}) custom-call(s32[1]{0:T(128)} %bitcast.core_ref, bf16[512,2048]{1,0:T(8,128)(2,1)S(1)} %copy-done, bf16[2048,3072]{1,0:T(8,128)(2,1)} %w_ref.3), custom_call_target="tpu_custom_call" | custom-call | flops 3221225472 | bytes 9961472 | tf_op jit(solution)/shard_map/project_band/pallas_call | solution.py:48
  18.0 0.0 collective-permute-done.x_ref
  18.0 6.5 %project_band.3 = (bf16[1024,512]{1,0:T(8,128)(2,1)S(1)}, bf16[1024,1024]{1,0:T(8,128)(2,1)S(1)}) custom-call(s32[1]{0:T(128)} %bitcast.core_ref, bf16[512,2048]{1,0:T(8,128)(2,1)} %collective-permute-done.x_ref, bf16[2048,3072]{1,0:T(8,128)(2,1)} %w_ref.3, ...), custom_call_target="tpu_custom_call", output_to_operand_aliasing={{0}: (3, {}), {1}: (4, {})} | custom-call | flops 3221225472 | bytes 9961472 | tf_op jit(solution)/shard_map/project_band/pallas_call | solution.py:48
  24.6 0.0 copy-start.1
  24.6 1.3 copy-done.1
  25.9 6.7 %collective-permute-start.2 = (bf16[1024,512]{1,0:T(8,128)(2,1)S(1)}, bf16[1024,512]{1,0:T(8,128)(2,1)}, u32[]{:S(2)}, u32[]{:S(2)}) collective-permute-start(bf16[1024,512]{1,0:T(8,128)(2,1)S(1)} %get-tuple-element.15.q_ref), channel_id=1, source_target_pairs={{2,0},{3,1},{4,2},{5,3},{6,4},{7,5},{8,6},{9,7},{10,8},{11,9},{12,... | collective-permute-start | bytes 3145736 | tf_op jit(solution)/shard_map/ppermute | solution.py:261
  32.6 7.4 %all-to-all-done = bf16[64,8,2048]{2,1,0:T(8,128)(2,1)} async-done(((bf16[64,8,2048]{2,1,0:T(8,128)(2,1)}), bf16[64,8,2048]{2,1,0:T(8,128)(2,1)}, u32[]{:S(2)}, u32[]{:S(2)}) %all-to-all-start) | async-done | bytes 2097184 | tf_op jit(solution)/shard_map/all_to_all | solution.py:250
  40.0 10.3 %convolution_convert_fusion.q_ref.k_ref.v_ref = bf16[512,3072]{1,0:T(8,128)(2,1)S(1)} fusion(bf16[2048,3072]{1,0:T(8,128)(2,1)} %param.5, bf16[64,8,2048]{2,1,0:T(8,128)(2,1)} %all-to-all-done), kind=kOutput, calls=%fused_computation | convolution fusion | flops 6444023808 | bytes 17825792 | tf_op jit(solution)/shard_map/dot_general | solution.py:270
  50.3 8.6 %column_attention.1 = bf16[512,1024]{1,0:T(8,128)(2,1)S(1)} custom-call(bf16[512,3072]{1,0:T(8,128)(2,1)S(1)} %convolution_convert_fusion.q_ref.k_ref.v_ref, bf16[512,3072]{1,0:T(8,128)(2,1)S(1)} %convolution_convert_fusion.q_ref.k_ref.v_ref, bf16[512,3072]{1,0:T(8,128)(2,1)S(1)} %convolution_convert_fusion.q_ref.k_ref.v_ref), custom_call_target="tpu_custom_call" | custom-call | flops 3000000000 | bytes 4194304 | tf_op jit(solution)/shard_map/column_attention/pallas_call | solution.py:184
  58.9 0.0 copy-start.3
  58.9 1.0 copy-done.3
  59.9 0.0 copy-start.2
  59.9 8.1 %all-to-all-start.1 = ((bf16[64,8,1024]{2,1,0:T(8,128)(2,1)}), bf16[64,8,1024]{2,1,0:T(8,128)(2,1)}, u32[]{:S(2)}, u32[]{:S(2)}) async-start(bf16[64,8,1024]{2,1,0:T(8,128)(2,1)} %bitcast.14), calls=%async_computation.1 | async-start | bytes 2097152 | tf_op jit(solution)/shard_map/all_to_all | solution.py:250
  68.0 0.0 copy-done.2
  68.0 11.6 %band_local.1 = (bf16[544,512]{1,0:T(8,128)(2,1)S(1)}, bf16[544,512]{1,0:T(8,128)(2,1)}) custom-call(s32[1]{0:T(128)} %bitcast.core_ref, bf16[1024,512]{1,0:T(8,128)(2,1)S(1)} %get-tuple-element.15.q_ref, bf16[1024,1024]{1,0:T(8,128)(2,1)S(1)} %copy-done.2, bf16[1024,1024]{1,0:T(8,128)(2,1)S(1)} %copy-done.2), custom_call_target="tpu_custom_call" | custom-call | flops 5000000000 | bytes 8388608 | tf_op jit(solution)/shard_map/band_local/pallas_call | solution.py:145
  79.6 0.0 copy-start.4
  79.6 0.8 copy-done.4
  80.4 2.3 %collective-permute-start.1 = (bf16[544,512]{1,0:T(8,128)(2,1)}, bf16[544,512]{1,0:T(8,128)(2,1)}, u32[]{:S(2)}, u32[]{:S(2)}) collective-permute-start(bf16[544,512]{1,0:T(8,128)(2,1)} %get-tuple-element.18), channel_id=1, source_target_pairs={{0,1},{1,0},{2,3},{3,2},{4,5},{5,4},{6,7},{7,6},{8,9},{9,8},{10,11... | collective-permute-start | bytes 1671176 | tf_op jit(solution)/shard_map/ppermute | solution.py:263
  82.7 0.0 collective-permute-done.2.q_ref
  82.7 0.0 copy-start.5
  82.7 12.4 %band_earlier.1 = (bf16[544,512]{1,0:T(8,128)(2,1)}, bf16[544,512]{1,0:T(8,128)(2,1)S(1)}) custom-call(s32[1]{0:T(128)} %bitcast.core_ref, bf16[1024,512]{1,0:T(8,128)(2,1)} %collective-permute-done.2.q_ref, bf16[1024,1024]{1,0:T(8,128)(2,1)S(1)} %copy-done.2, bf16[1024,1024]{1,0:T(8,128)(2,1)S(1)} %copy-done.2), custom_call_target="tpu_custom_call" | custom-call | flops 5000000000 | bytes 8388608 | tf_op jit(solution)/shard_map/band_earlier/pallas_call | solution.py:145
  95.1 3.1 %collective-permute-start.3 = (bf16[544,512]{1,0:T(8,128)(2,1)}, bf16[544,512]{1,0:T(8,128)(2,1)S(1)}, u32[]{:S(2)}, u32[]{:S(2)}) collective-permute-start(bf16[544,512]{1,0:T(8,128)(2,1)} %get-tuple-element.19), channel_id=1, source_target_pairs={{0,2},{1,3},{2,4},{3,5},{4,6},{5,7},{6,8},{7,9},{8,10},{9,11},{10,... | collective-permute-start | bytes 1671176 | tf_op jit(solution)/shard_map/ppermute | solution.py:265
  98.2 3.3 %collective-permute-start.4 = (bf16[544,512]{1,0:T(8,128)(2,1)S(1)}, bf16[544,512]{1,0:T(8,128)(2,1)S(1)}, u32[]{:S(2)}, u32[]{:S(2)}) collective-permute-start(bf16[544,512]{1,0:T(8,128)(2,1)S(1)} %get-tuple-element.20), channel_id=1, source_target_pairs={{0,3},{1,2},{2,5},{3,4},{4,7},{5,6},{6,9},{7,8},{8,11},{9,10},{10,... | collective-permute-start | bytes 1671176 | tf_op jit(solution)/shard_map/ppermute | solution.py:266
  101.5 0.1 pad_add_fusion.flags_ref
  101.6 0.0 collective-permute-done.1
  101.6 0.0 copy-done.5
  101.6 1.2 pad_maximum_fusion.1.local_ref
  102.7 12.9 %collective-permute-done.3 = bf16[544,512]{1,0:T(8,128)(2,1)S(1)} collective-permute-done((bf16[544,512]{1,0:T(8,128)(2,1)}, bf16[544,512]{1,0:T(8,128)(2,1)S(1)}, u32[]{:S(2)}, u32[]{:S(2)}) %collective-permute-start.3) | collective-permute-done | bytes 557088 | tf_op jit(solution)/shard_map/ppermute | solution.py:265
  115.7 12.0 %collective-permute-done.4 = bf16[544,512]{1,0:T(8,128)(2,1)S(1)} collective-permute-done((bf16[544,512]{1,0:T(8,128)(2,1)S(1)}, bf16[544,512]{1,0:T(8,128)(2,1)S(1)}, u32[]{:S(2)}, u32[]{:S(2)}) %collective-permute-start.4) | collective-permute-done | bytes 557088 | tf_op jit(solution)/shard_map/ppermute | solution.py:266
  127.7 0.1 pad_maximum_fusion.2.earlier_ref
  127.8 1.4 %merge_band.1 = bf16[512,1024]{1,0:T(8,128)(2,1)S(1)} custom-call(s32[2]{0:T(128)S(1)} %pad_add_fusion.flags_ref, bf16[2,544,512]{2,1,0:T(8,128)(2,1)S(1)} %pad_maximum_fusion.1.local_ref, bf16[2,544,512]{2,1,0:T(8,128)(2,1)S(1)} %pad_maximum_fusion.2.earlier_ref), custom_call_target="tpu_custom_call" | custom-call | flops 10000000 | bytes 4194304 | tf_op jit(solution)/shard_map/merge_band/pallas_call | solution.py:219
  129.3 0.0 all-to-all-done.1
  129.3 2.8 %pad_maximum_fusion = bf16[512,2048]{1,0:T(8,128)(2,1)} fusion(bf16[512,1024]{1,0:T(8,128)(2,1)} %bitcast.9, bf16[512,1024]{1,0:T(8,128)(2,1)S(1)} %merge_band.1), kind=kLoop, calls=%fused_computation.1 | loop fusion | flops 4194304 | bytes 4194304 | tf_op jit(solution)/shard_map/concatenate | solution.py:275
Async XLA Ops:
  0.0 18.0 %collective-permute-start = (bf16[512,2048]{1,0:T(8,128)(2,1)}, bf16[512,2048]{1,0:T(8,128)(2,1)}, u32[]{:S(2)}, u32[]{:S(2)}) collective-permute-start(bf16[512,2048]{1,0:T(8,128)(2,1)} %x_ref.1), channel_id=1, source_target_pairs={{0,1},{1,0},{2,3},{3,2},{4,5},{5,4},{6,7},{7,6},{8,9},{9,8},{10,11... | collective-permute-start | bytes 6291464 | tf_op jit(solution)/shard_map/ppermute | solution.py:257
  0.7 11.4 %copy-start = (bf16[512,2048]{1,0:T(8,128)(2,1)S(1)}, bf16[512,2048]{1,0:T(8,128)(2,1)}, u32[]{:S(2)}) copy-start(bf16[512,2048]{1,0:T(8,128)(2,1)} %x_ref.1) | copy-start | bytes 6291460
  0.7 39.3 %all-to-all-start = ((bf16[64,8,2048]{2,1,0:T(8,128)(2,1)}), bf16[64,8,2048]{2,1,0:T(8,128)(2,1)}, u32[]{:S(2)}, u32[]{:S(2)}) async-start(bf16[64,8,2048]{2,1,0:T(8,128)(2,1)} %bitcast.13), calls=%async_computation | async-start | bytes 4194304 | tf_op jit(solution)/shard_map/all_to_all | solution.py:250
  24.6 1.3 %copy-start.1 = (bf16[1024,1024]{1,0:T(8,128)(2,1)}, bf16[1024,1024]{1,0:T(8,128)(2,1)S(1)}, u32[]{:S(2)}) copy-start(bf16[1024,1024]{1,0:T(8,128)(2,1)S(1)} %get-tuple-element.16.k_ref.v_ref) | copy-start | bytes 6291460
  25.9 56.8 %collective-permute-start.2 = (bf16[1024,512]{1,0:T(8,128)(2,1)S(1)}, bf16[1024,512]{1,0:T(8,128)(2,1)}, u32[]{:S(2)}, u32[]{:S(2)}) collective-permute-start(bf16[1024,512]{1,0:T(8,128)(2,1)S(1)} %get-tuple-element.15.q_ref), channel_id=1, source_target_pairs={{2,0},{3,1},{4,2},{5,3},{6,4},{7,5},{8,6},{9,7},{10,8},{11,9},{12,... | collective-permute-start | bytes 3145736 | tf_op jit(solution)/shard_map/ppermute | solution.py:261
  58.9 1.0 copy-start.3
  59.9 8.1 %copy-start.2 = (bf16[1024,1024]{1,0:T(8,128)(2,1)S(1)}, bf16[1024,1024]{1,0:T(8,128)(2,1)}, u32[]{:S(2)}) copy-start(bf16[1024,1024]{1,0:T(8,128)(2,1)} %copy-done.1) | copy-start | bytes 6291460
  59.9 69.4 %all-to-all-start.1 = ((bf16[64,8,1024]{2,1,0:T(8,128)(2,1)}), bf16[64,8,1024]{2,1,0:T(8,128)(2,1)}, u32[]{:S(2)}, u32[]{:S(2)}) async-start(bf16[64,8,1024]{2,1,0:T(8,128)(2,1)} %bitcast.14), calls=%async_computation.1 | async-start | bytes 2097152 | tf_op jit(solution)/shard_map/all_to_all | solution.py:250
  79.6 0.8 copy-start.4
  80.4 21.1 %collective-permute-start.1 = (bf16[544,512]{1,0:T(8,128)(2,1)}, bf16[544,512]{1,0:T(8,128)(2,1)}, u32[]{:S(2)}, u32[]{:S(2)}) collective-permute-start(bf16[544,512]{1,0:T(8,128)(2,1)} %get-tuple-element.18), channel_id=1, source_target_pairs={{0,1},{1,0},{2,3},{3,2},{4,5},{5,4},{6,7},{7,6},{8,9},{9,8},{10,11... | collective-permute-start | bytes 1671176 | tf_op jit(solution)/shard_map/ppermute | solution.py:263
  82.7 18.9 %copy-start.5 = (bf16[544,512]{1,0:T(8,128)(2,1)S(1)}, bf16[544,512]{1,0:T(8,128)(2,1)}, u32[]{:S(2)}) copy-start(bf16[544,512]{1,0:T(8,128)(2,1)} %copy-done.4) | copy-start | bytes 1671172
  95.1 20.6 %collective-permute-start.3 = (bf16[544,512]{1,0:T(8,128)(2,1)}, bf16[544,512]{1,0:T(8,128)(2,1)S(1)}, u32[]{:S(2)}, u32[]{:S(2)}) collective-permute-start(bf16[544,512]{1,0:T(8,128)(2,1)} %get-tuple-element.19), channel_id=1, source_target_pairs={{0,2},{1,3},{2,4},{3,5},{4,6},{5,7},{6,8},{7,9},{8,10},{9,11},{10,... | collective-permute-start | bytes 1671176 | tf_op jit(solution)/shard_map/ppermute | solution.py:265
  98.2 29.5 %collective-permute-start.4 = (bf16[544,512]{1,0:T(8,128)(2,1)S(1)}, bf16[544,512]{1,0:T(8,128)(2,1)S(1)}, u32[]{:S(2)}, u32[]{:S(2)}) collective-permute-start(bf16[544,512]{1,0:T(8,128)(2,1)S(1)} %get-tuple-element.20), channel_id=1, source_target_pairs={{0,3},{1,2},{2,5},{3,4},{4,7},{5,6},{6,9},{7,8},{8,11},{9,10},{10,... | collective-permute-start | bytes 1671176 | tf_op jit(solution)/shard_map/ppermute | solution.py:266

commit v2 on v0

v2 whole, which is shorter than its diff:
```python
import functools
import math

import jax
import jax.numpy as jnp
from jax import lax
from jax.experimental import pallas as pl
from jax.experimental.pallas import tpu as pltpu
from jax.sharding import PartitionSpec as P

HEAD = 128
HEADS = 8
STRIDE = 1024
HALF = 512
BLOCK = 256
SCALE2 = math.log2(math.e) / math.sqrt(HEAD)
NEG = -1e30
VMEM_LIMIT = 28 << 20


def params():
    return pltpu.CompilerParams(vmem_limit_bytes=VMEM_LIMIT)


def cost(us):
    return pl.CostEstimate(flops=int(us * 10**9), bytes_accessed=1 << 14, transcendentals=0)


def halves(core, own_ref, sibling_ref, w, store):
    for place, ref in ((core, own_ref), (1 - core, sibling_ref)):
        value = jnp.dot(ref[...], w, preferred_element_type=jnp.float32)
        store(pl.ds(pl.multiple_of(place * HALF, HALF), HALF), value)


def query_kernel(core_ref, own_ref, sibling_ref, w_ref, a_ref, b_ref):
    for step, ref in enumerate((a_ref, b_ref)):
        @pl.when(pl.program_id(0) == step)
        def _():
            def store(rows, value):
                ref[rows, :] = value.astype(jnp.bfloat16)

            halves(core_ref[0], own_ref, sibling_ref, w_ref[...], store)


def keyval_kernel(core_ref, own_ref, sibling_ref, w_ref, k_ref, vt_ref):
    @pl.when(pl.program_id(0) < 2)
    def _():
        def store(rows, value):
            k_ref[rows, :] = value.astype(jnp.bfloat16)

        halves(core_ref[0], own_ref, sibling_ref, w_ref[...], store)

    @pl.when(pl.program_id(0) >= 2)
    def _():
        def store(rows, value):
            vt_ref[:, rows] = value.T.astype(jnp.bfloat16)

        halves(core_ref[0], own_ref, sibling_ref, w_ref[...], store)


def project(kernel, steps, first, core, tokens, sibling, w_row, out_specs, out_shape, name):
    depth = tokens.shape[1]
    whole = pl.BlockSpec((HALF, depth), lambda j, c: (0, 0))
    weights = pl.BlockSpec(
        (depth, BLOCK), lambda j, c: (0, 4 * (first + j // 2) + 2 * c[0] + j % 2)
    )
    return pl.pallas_call(
        kernel,
        grid_spec=pltpu.PrefetchScalarGridSpec(
            num_scalar_prefetch=1,
            grid=(steps,),
            in_specs=[whole, whole, weights],
            out_specs=out_specs,
        ),
        out_shape=out_shape,
        compiler_params=params(),
        cost_estimate=cost(1.3 * steps),
        name=name,
    )(core, tokens, sibling, w_row)


def project_query(core, tokens, sibling, w_row):
    spec = pl.BlockSpec((STRIDE, BLOCK), lambda j, c: (0, 0))
    shape = jax.ShapeDtypeStruct((STRIDE, BLOCK), jnp.bfloat16)
    return project(
        query_kernel, 2, 0, core, tokens, sibling, w_row, [spec, spec], [shape, shape], "query"
    )


def project_keyval(core, tokens, sibling, w_row):
    return project(
        keyval_kernel, 4, 1, core, tokens, sibling, w_row,
        [
            pl.BlockSpec((STRIDE, BLOCK), lambda j, c: (0, jnp.minimum(j, 1))),
            pl.BlockSpec((BLOCK, STRIDE), lambda j, c: (jnp.maximum(j - 2, 0), 0)),
        ],
        [
            jax.ShapeDtypeStruct((STRIDE, HALF), jnp.bfloat16),
            jax.ShapeDtypeStruct((HALF, STRIDE), jnp.bfloat16),
        ],
        "keyval",
    )


def score_blocks(query, key_ref, columns, spans):
    return [
        lax.dot_general(
            key_ref[low:high, columns], query, (((1,), (1,)), ((), ())),
            preferred_element_type=jnp.float32,
        )
        for low, high in spans
    ]


def softmax_out(scores, biases, value_t_blocks):
    scores = [s if b is None else s + b for s, b in zip(scores, biases)]
    top = functools.reduce(jnp.maximum, [jnp.max(s, axis=0, keepdims=True) for s in scores])
    expd = [jnp.exp2((s - top) * SCALE2) for s in scores]
    total = sum(jnp.sum(e, axis=0, keepdims=True) for e in expd)
    out = sum(
        jnp.dot(v, e.astype(jnp.bfloat16), preferred_element_type=jnp.float32)
        for v, e in zip(value_t_blocks, expd)
    )
    return out * (1.0 / total), top, total


def pipelined(jobs, ahead, start, finish):
    pending, results = [], {}
    for job in jobs:
        pending.append((job, start(*job)))
        if len(pending) > ahead:
            first, value = pending.pop(0)
            results[first] = finish(*first, value)
    for first, value in pending:
        results[first] = finish(*first, value)
    return results


def split3(value):
    high = value.astype(jnp.bfloat16).astype(jnp.float32)
    rest = value - high
    mid = rest.astype(jnp.bfloat16).astype(jnp.float32)
    return [high, mid, rest - mid]


def band_kernel(
    earlier, heads, ahead, core_ref, q_ref, k_ref, vt_ref, same_ref, cross_ref, stat_ref, bias_ref
):
    step = pl.program_id(0)
    core = core_ref[0]
    parts = STRIDE // BLOCK

    @pl.when(step == 0)
    def _():
        kpos = lax.broadcasted_iota(jnp.int32, (BLOCK, BLOCK), 0)
        qpos = lax.broadcasted_iota(jnp.int32, (BLOCK, BLOCK), 1)
        allowed = kpos > qpos if earlier else kpos <= qpos
        bias_ref[...] = jnp.where(allowed, 0.0, NEG)

    def spans(part):
        low, high = part * BLOCK, (part + 1) * BLOCK
        rest = (high, STRIDE) if earlier else (0, low)
        return [(low, high)] + ([rest] if rest[0] < rest[1] else [])

    def columns(head):
        return slice(head * HEAD, (head + 1) * HEAD)

    def start(part, head):
        query = q_ref[part * BLOCK : (part + 1) * BLOCK, columns(head)]
        return score_blocks(query, k_ref, columns(head), spans(part))

    def finish(part, head, scores):
        values = [vt_ref[columns(head), low:high] for low, high in spans(part)]
        out, top, total = softmax_out(scores, [bias_ref[...], None], values)
        return out.astype(jnp.bfloat16), top, total

    jobs = [(part, head) for part in range(parts) for head in range(2)]
    results = pipelined(jobs, ahead, start, finish)
    for head in range(2):
        stats = [
            jnp.concatenate(
                split3(results[part, head][1])
                + split3(results[part, head][2])
                + [jnp.zeros((2, BLOCK), jnp.float32)],
                axis=0,
            )
            for part in range(parts)
        ]
        stat_ref[step * 2 + head] = jnp.concatenate(stats, axis=1)
    rows = pl.ds(pl.multiple_of(step * 2 * HEAD, 2 * HEAD), 2 * HEAD)
    for half in range(2):
        piece = jnp.concatenate(
            [
                jnp.concatenate([results[2 * half + part, head][0] for part in range(2)], axis=1)
                for head in range(2)
            ],
            axis=0,
        )

        @pl.when(core == half)
        def _():
            same_ref[rows, :] = piece

        @pl.when(core != half)
        def _():
            cross_ref[rows, :] = piece

    @pl.when(step == heads // 2 - 1)
    def _():
        stats = jnp.concatenate([stat_ref[h] for h in range(heads)], axis=0).astype(jnp.bfloat16)
        for half in range(2):
            piece = stats[:, half * HALF : (half + 1) * HALF]

            @pl.when(core == half)
            def _():
                same_ref[heads * HEAD :, :] = piece

            @pl.when(core != half)
            def _():
                cross_ref[heads * HEAD :, :] = piece


def band_part(earlier, core, query, keys, values_t, first=0):
    heads = query.shape[1] // HEAD
    payload = heads * (HEAD + 8)
    whole = pl.BlockSpec((payload, HALF), lambda h, c: (0, 0))
    return pl.pallas_call(
        functools.partial(band_kernel, earlier, heads, 2 if earlier else 4),
        grid_spec=pltpu.PrefetchScalarGridSpec(
            num_scalar_prefetch=1,
            grid=(heads // 2,),
            in_specs=[
                pl.BlockSpec((STRIDE, 2 * HEAD), lambda h, c: (0, h)),
                pl.BlockSpec((STRIDE, 2 * HEAD), lambda h, c: (0, first + h)),
                pl.BlockSpec((2 * HEAD, STRIDE), lambda h, c: (first + h, 0)),
            ],
            out_specs=[whole, whole],
            scratch_shapes=[
                pltpu.VMEM((heads, 8, STRIDE), jnp.float32),
                pltpu.VMEM((BLOCK, BLOCK), jnp.float32),
            ],
        ),
        out_shape=[jax.ShapeDtypeStruct((payload, HALF), jnp.bfloat16)] * 2,
        compiler_params=params(),
        cost_estimate=cost(1.7 * heads),
        name="band_earlier" if earlier else "band_local",
    )(core, query, keys, values_t)


def column_kernel(group, x_ref, wq_ref, wk_ref, wv_ref, o_ref, k_ref, bias_ref):
    parts = HALF // BLOCK

    @pl.when(pl.program_id(0) == 0)
    def _():
        kpos = lax.broadcasted_iota(jnp.int32, (BLOCK, BLOCK), 0)
        qpos = lax.broadcasted_iota(jnp.int32, (BLOCK, BLOCK), 1)
        column = ((qpos - kpos) & (group - 1)) == 0
        bias_ref[0] = jnp.where(column, 0.0, NEG)
        bias_ref[1] = jnp.where(column & (kpos <= qpos), 0.0, NEG)

    x = x_ref[...]
    query = jnp.dot(x, wq_ref[...], preferred_element_type=jnp.float32).astype(jnp.bfloat16)
    keys = jnp.dot(x, wk_ref[...], preferred_element_type=jnp.float32).astype(jnp.bfloat16)
    k_ref[...] = keys
    values_t = jnp.dot(x, wv_ref[...], preferred_element_type=jnp.float32).T.astype(jnp.bfloat16)

    def spans(part):
        return [(block * BLOCK, (block + 1) * BLOCK) for block in range(part + 1)]

    def columns(head):
        return slice(head * HEAD, (head + 1) * HEAD)

    def start(part, head):
        part_query = query[part * BLOCK : (part + 1) * BLOCK, columns(head)]
        return score_blocks(part_query, k_ref, columns(head), spans(part))

    def finish(part, head, scores):
        values = [values_t[columns(head), low:high] for low, high in spans(part)]
        biases = [bias_ref[1 if block == part else 0] for block in range(part + 1)]
        out = softmax_out(scores, biases, values)[0]
        o_ref[part * BLOCK : (part + 1) * BLOCK, columns(head)] = out.T.astype(jnp.bfloat16)

    pipelined([(part, head) for part in range(parts) for head in range(2)], 2, start, finish)


def column_attention(x, w_column, group):
    rows, depth = x.shape
    pairs = HEADS // 2
    weights = lambda third: pl.BlockSpec((depth, 2 * HEAD), lambda j: (0, third * pairs + j))
    return pl.pallas_call(
        functools.partial(column_kernel, group),
        grid=(pairs,),
        in_specs=[pl.BlockSpec((rows, depth), lambda j: (0, 0)), weights(0), weights(1), weights(2)],
        out_specs=pl.BlockSpec((rows, 2 * HEAD), lambda j: (0, j)),
        out_shape=jax.ShapeDtypeStruct((rows, HEADS * HEAD), jnp.bfloat16),
        scratch_shapes=[
            pltpu.VMEM((rows, 2 * HEAD), jnp.bfloat16),
            pltpu.VMEM((2, BLOCK, BLOCK), jnp.float32),
        ],
        compiler_params=params(),
        cost_estimate=cost(10),
        name="column_attention",
    )(x, w_column, w_column, w_column)


def merge_heads(has_earlier, local_ref, earlier_refs, o_ref):
    local_heads, part_heads = 4, 2
    for head in range(local_heads):
        def stats(ref, heads, index):
            start = heads * HEAD
            rows = ref[start : start + 8 * heads, :].astype(jnp.float32)
            rows = rows[8 * index : 8 * index + 8]
            return rows[0:1] + rows[1:2] + rows[2:3], rows[3:4] + rows[4:5] + rows[5:6]

        earlier_ref, index = earlier_refs[head // part_heads], head % part_heads
        top_l, sum_l = stats(local_ref, local_heads, head)
        top_e, sum_e = stats(earlier_ref, part_heads, index)
        top_e = jnp.where(has_earlier, top_e, NEG)
        top = jnp.maximum(top_l, top_e)
        weight_l = jnp.exp2((top_l - top) * SCALE2) * sum_l
        weight_e = jnp.exp2((top_e - top) * SCALE2) * sum_e
        weight_e = jnp.where(has_earlier, weight_e, 0.0)
        inverse = 1.0 / (weight_l + weight_e)
        out_l = local_ref[head * HEAD : (head + 1) * HEAD, :].astype(jnp.float32)
        out_e = earlier_ref[index * HEAD : (index + 1) * HEAD, :].astype(jnp.float32)
        out = out_l * (weight_l * inverse) + out_e * (weight_e * inverse)
        o_ref[:, head * HEAD : (head + 1) * HEAD] = out.T.astype(jnp.bfloat16)


def finish_kernel(
    flags_ref, local_same, local_cross, same_a, same_b, cross_a, cross_b, col_ref, o_ref
):
    step = pl.program_id(0)
    has_earlier = flags_ref[1] > 0

    @pl.when(step < 2)
    def _():
        o_ref[...] = col_ref[...]

    @pl.when(step == 2)
    def _():
        merge_heads(has_earlier, local_same, (same_a, same_b), o_ref)

    @pl.when(step == 3)
    def _():
        merge_heads(has_earlier, local_cross, (cross_a, cross_b), o_ref)


def finish(flags, local_same, local_cross, same_a, same_b, cross_a, cross_b, col_out):
    bands = [local_same, local_cross, same_a, same_b, cross_a, cross_b]

    def out_block(j, c):
        core = c[0]
        return (0, jnp.where(j < 2, 2 + j, jnp.where(j == 2, core, 1 - core)))

    return pl.pallas_call(
        finish_kernel,
        grid_spec=pltpu.PrefetchScalarGridSpec(
            num_scalar_prefetch=1,
            grid=(4,),
            in_specs=[pl.BlockSpec(b.shape, lambda j, c: (0, 0)) for b in bands]
            + [pl.BlockSpec((HALF, HALF), lambda j, c: (0, jnp.minimum(j, 1)))],
            out_specs=pl.BlockSpec((HALF, HALF), out_block),
        ),
        out_shape=jax.ShapeDtypeStruct((HALF, 2 * HEADS * HEAD), jnp.bfloat16),
        compiler_params=params(),
        cost_estimate=cost(3),
        name="merge",
    )(flags, *bands, col_out)


def after(value, *others):
    return lax.optimization_barrier((value,) + others)[0]


def on_device(tokens, w_row, w_column):
    count = lax.axis_size("seq")
    chips = count // 2
    rank = lax.axis_index("seq")
    core = (rank % 2).astype(jnp.int32)
    core_arr = core.reshape(1)
    flags = jnp.stack([core, (rank >= 2).astype(jnp.int32)])
    group = HALF // chips
    same_core = [list(range(0, count, 2)), list(range(1, count, 2))]

    def exchange(value):
        width = value.shape[1]
        value = lax.all_to_all(
            value.reshape(chips, group, width), "seq", split_axis=0, concat_axis=0,
            axis_index_groups=same_core, tiled=True,
        )
        return value.reshape(HALF, width)

    def swapped(value):
        return lax.ppermute(value, "seq", [(d, d ^ 1) for d in range(count)])

    def to_previous(value):
        return lax.ppermute(value, "seq", [(d, d - 2) for d in range(2, count)])

    def to_next(same, cross):
        same = lax.ppermute(same, "seq", [(d, d + 2) for d in range(count - 2)])
        cross = lax.ppermute(cross, "seq", [(d, (d + 2) ^ 1) for d in range(count - 2)])
        return same, cross

    w_row = pltpu.with_memory_space_constraint(w_row, pltpu.HBM)
    w_column = pltpu.with_memory_space_constraint(w_column, pltpu.HBM)
    columns = exchange(tokens)
    sibling = swapped(tokens)
    query_a, query_b = project_query(core_arr, tokens, sibling, w_row)
    next_a, next_b = to_previous(query_a), to_previous(query_b)
    keys, values_t = project_keyval(core_arr, tokens, sibling, w_row)
    local_same, local_cross = band_part(
        False, core_arr, jnp.concatenate([query_a, query_b], axis=1), keys, values_t
    )
    parts_a = band_part(True, core_arr, after(next_a, local_same), keys, values_t, 0)
    same_a, cross_a = to_next(*parts_a)
    col_out = column_attention(after(columns, parts_a[0]), w_column, group)
    parts_b = band_part(True, core_arr, after(next_b, col_out), keys, values_t, 1)
    same_b, cross_b = to_next(*parts_b)
    return finish(
        flags, local_same, swapped(local_cross), same_a, same_b, cross_a, cross_b,
        exchange(after(col_out, same_a, cross_a)),
    )


def solution(mesh):
    in_specs = (P("seq", None), P(), P())
    out_specs = P("seq", None)
    return jax.shard_map(
        on_device, mesh=mesh, in_specs=in_specs, out_specs=out_specs, check_vma=False
    )
```

time: 206 us -> 119 us (0.58)
  the two profiles are of different devices: /device:TPU:0 before, /device:TPU:3 now
where the time goes in v2:
time: 119 us; the launch traced here: 118 us
  Pallas kernels  45 us (38%)
  starting transfers between devices  44.8 us (38%)
  waiting for transfers between devices  24.6 us (21%)
  local copies, waits for them, and re-layouts  3.52 us (3%)
    all_to_all x2, starting transfers between devices, exchange(): lax.all_to_all(value.reshape(chips, group, width), 'seq', split_axis=0, c...  20.7 us
    pallas_call x1, Pallas kernels, column_attention(): pl.pallas_call(functools.partial(column_kernel, group), grid=(pairs,), in...  17.6 us
    pallas_call x3, Pallas kernels, band_part(): pl.pallas_call(functools.partial(band_kernel, earlier, heads, 2 if earlie...  12.2 us
    pallas_call x2, Pallas kernels, project(): pl.pallas_call(kernel, grid_spec=pltpu.PrefetchScalarGridSpec(num_scalar_...  12.1 us
    ppermute x2, waiting for transfers between devices, to_previous(): return lax.ppermute(value, 'seq', [(d, d - 2) for d in range(2, count)])  9.48 us
    ppermute x2, waiting for transfers between devices, to_next(): same = lax.ppermute(same, 'seq', [(d, d + 2) for d in range(count - 2)])  9.12 us
    ppermute x2, starting transfers between devices, to_previous(): return lax.ppermute(value, 'seq', [(d, d - 2) for d in range(2, count)])  8.9 us
    ppermute x2, starting transfers between devices, to_next(): lax.ppermute(cross, 'seq', [(d, d + 2 ^ 1) for d in range(count - 2)])  7.16 us
  transfers between devices with their start and end apart: 10, of which 3 were waited for; matrix products, arithmetic and copies ran while one was open for 0% of the time, Pallas kernels for 35%

profile of v2, /device:TPU:3, one launch (start us, length us, event | category | flops | bytes accessed | tf_op | source)
XLA Modules:
  0.0 118.3 jit_solution(10976732322094894683)
XLA Ops:
  0.0 0.7 collective-permute-start
  0.7 0.0 copy-start
  0.7 11.3 %all-to-all-start = ((bf16[64,8,2048]{2,1,0:T(8,128)(2,1)}), bf16[64,8,2048]{2,1,0:T(8,128)(2,1)}, u32[]{:S(2)}, u32[]{:S(2)}) async-start(bf16[64,8,2048]{2,1,0:T(8,128)(2,1)} %bitcast.6), calls=%async_computation | async-start | bytes 4194304 | tf_op jit(solution)/shard_map/all_to_all | solution.py:388
  12.0 0.0 collective-permute-done.sibling_ref
  12.0 0.0 copy-done
  12.0 4.6 %query.1 = (bf16[1024,256]{1,0:T(8,128)(2,1)S(1)}, bf16[1024,256]{1,0:T(8,128)(2,1)S(1)}) custom-call(s32[1]{0:T(128)} %bitcast.core_ref, bf16[512,2048]{1,0:T(8,128)(2,1)S(1)} %copy-done, bf16[512,2048]{1,0:T(8,128)(2,1)} %collective-permute-done.sibling_ref, bf16[2048,3072]{1,0:T(8,128)(2,1)} %w_ref.3), custom_call_target="tpu_custom_call" | custom-call | flops 2600000000 | bytes 16384 | tf_op jit(solution)/shard_map/query/pallas_call | solution.py:67
  16.6 6.4 %collective-permute-start.2 = (bf16[1024,256]{1,0:T(8,128)(2,1)S(1)}, bf16[1024,256]{1,0:T(8,128)(2,1)S(1)}, u32[]{:S(2)}, u32[]{:S(2)}) collective-permute-start(bf16[1024,256]{1,0:T(8,128)(2,1)S(1)} %get-tuple-element.19), channel_id=1, source_target_pairs={{2,0},{3,1},{4,2},{5,3},{6,4},{7,5},{8,6},{9,7},{10,8},{11,9},{12,... | collective-permute-start | bytes 1572872 | tf_op jit(solution)/shard_map/ppermute | solution.py:398
  23.0 2.5 %collective-permute-start.4 = (bf16[1024,256]{1,0:T(8,128)(2,1)S(1)}, bf16[1024,256]{1,0:T(8,128)(2,1)}, u32[]{:S(2)}, u32[]{:S(2)}) collective-permute-start(bf16[1024,256]{1,0:T(8,128)(2,1)S(1)} %get-tuple-element.20), channel_id=1, source_target_pairs={{2,0},{3,1},{4,2},{5,3},{6,4},{7,5},{8,6},{9,7},{10,8},{11,9},{12,... | collective-permute-start | bytes 1572872 | tf_op jit(solution)/shard_map/ppermute | solution.py:398
  25.5 0.1 pad_maximum_fusion.q_ref
  25.6 7.5 %keyval.1 = (bf16[1024,512]{1,0:T(8,128)(2,1)S(1)}, bf16[512,1024]{1,0:T(8,128)(2,1)S(1)}) custom-call(s32[1]{0:T(128)} %bitcast.core_ref, bf16[512,2048]{1,0:T(8,128)(2,1)S(1)} %copy-done, bf16[512,2048]{1,0:T(8,128)(2,1)} %collective-permute-done.sibling_ref, bf16[2048,3072]{1,0:T(8,128)(2,1)} %w_ref.3), custom_call_target="tpu_custom_call" | custom-call | flops 5200000000 | bytes 16384 | tf_op jit(solution)/shard_map/keyval/pallas_call | solution.py:67
  33.1 0.0 copy-start.1
  33.1 0.0 copy-start.3
  33.1 5.6 %band_local.1 = (bf16[544,512]{1,0:T(8,128)(2,1)S(1)}, bf16[544,512]{1,0:T(8,128)(2,1)S(1)}) custom-call(s32[1]{0:T(128)} %bitcast.core_ref, bf16[1024,512]{1,0:T(8,128)(2,1)S(1)} %pad_maximum_fusion.q_ref, bf16[1024,512]{1,0:T(8,128)(2,1)S(1)} %get-tuple-element.21.k_ref, bf16[512,1024]{1,0:T(8,128)(2,1)S(1)} %get-tuple-element.22.vt_ref), custom_call_target="tpu_custom_call" | custom-call | flops 6800000000 | bytes 16384 | tf_op jit(solution)/shard_map/band_local/pallas_call | solution.py:227
  38.7 0.0 copy-start.5
  38.7 9.5 %collective-permute-done.2.q_ref = bf16[1024,256]{1,0:T(8,128)(2,1)S(1)} collective-permute-done((bf16[1024,256]{1,0:T(8,128)(2,1)S(1)}, bf16[1024,256]{1,0:T(8,128)(2,1)S(1)}, u32[]{:S(2)}, u32[]{:S(2)}) %collective-permute-start.2) | collective-permute-done | bytes 524320 | tf_op jit(solution)/shard_map/ppermute | solution.py:398
  48.2 0.0 copy-done.1
  48.2 0.0 copy-done.3
  48.2 2.4 %band_earlier.2 = (bf16[272,512]{1,0:T(8,128)(2,1)S(1)}, bf16[272,512]{1,0:T(8,128)(2,1)S(1)}) custom-call(s32[1]{0:T(128)} %bitcast.core_ref, bf16[1024,256]{1,0:T(8,128)(2,1)S(1)} %collective-permute-done.2.q_ref, bf16[1024,512]{1,0:T(8,128)(2,1)S(1)} %get-tuple-element.21.k_ref, bf16[512,1024]{1,0:T(8,128)(2,1)S(1)} %get-tuple-element.22.vt_ref), custom_call_target="tpu_custom_call" | custom-call | flops 3400000000 | bytes 16384 | tf_op jit(solution)/shard_map/band_earlier/pallas_call | solution.py:227
  50.6 0.0 copy-done.5
  50.6 3.3 %collective-permute-start.3 = (bf16[272,512]{1,0:T(8,128)(2,1)S(1)}, bf16[272,512]{1,0:T(8,128)(2,1)S(1)}, u32[]{:S(2)}, u32[]{:S(2)}) collective-permute-start(bf16[272,512]{1,0:T(8,128)(2,1)S(1)} %get-tuple-element.26), channel_id=1, source_target_pairs={{0,2},{1,3},{2,4},{3,5},{4,6},{5,7},{6,8},{7,9},{8,10},{9,11},{10,... | collective-permute-start | bytes 835592 | tf_op jit(solution)/shard_map/ppermute | solution.py:401
  53.9 0.0 all-to-all-done
  53.9 3.9 %collective-permute-start.6 = (bf16[272,512]{1,0:T(8,128)(2,1)S(1)}, bf16[272,512]{1,0:T(8,128)(2,1)S(1)}, u32[]{:S(2)}, u32[]{:S(2)}) collective-permute-start(bf16[272,512]{1,0:T(8,128)(2,1)S(1)} %get-tuple-element.30), channel_id=1, source_target_pairs={{0,3},{1,2},{2,5},{3,4},{4,7},{5,6},{6,9},{7,8},{8,11},{9,10},{10,... | collective-permute-start | bytes 835592 | tf_op jit(solution)/shard_map/ppermute | solution.py:402
  57.8 17.6 %column_attention.1 = bf16[512,1024]{1,0:T(8,128)(2,1)} custom-call(bf16[512,2048]{1,0:T(8,128)(2,1)} %bitcast.3.x_ref, bf16[2048,3072]{1,0:T(8,128)(2,1)} %wv_ref.1, bf16[2048,3072]{1,0:T(8,128)(2,1)} %wv_ref.1, bf16[2048,3072]{1,0:T(8,128)(2,1)} %wv_ref.1), custom_call_target="tpu_custom_call" | custom-call | flops 10000000000 | bytes 16384 | tf_op jit(solution)/shard_map/column_attention/pallas_call | solution.py:290
  75.4 0.0 collective-permute-done.6.cross_a
  75.4 0.0 collective-permute-done.3.same_a
  75.4 9.4 %all-to-all-start.1 = ((bf16[64,8,1024]{2,1,0:T(8,128)(2,1)}), bf16[64,8,1024]{2,1,0:T(8,128)(2,1)S(1)}, u32[]{:S(2)}, u32[]{:S(2)}) async-start(bf16[64,8,1024]{2,1,0:T(8,128)(2,1)} %bitcast.4), calls=%async_computation.1 | async-start | bytes 2097152 | tf_op jit(solution)/shard_map/all_to_all | solution.py:388
  84.9 1.0 collective-permute-start.1
  85.9 0.0 collective-permute-done.4.q_ref
  85.9 0.0 copy-start.2
  85.9 1.2 %copy-done.2 = bf16[1024,512]{1,0:T(8,128)(2,1)S(1)} copy-done((bf16[1024,512]{1,0:T(8,128)(2,1)S(1)}, bf16[1024,512]{1,0:T(8,128)(2,1)}, u32[]{:S(2)}) %copy-start.2) | copy-done | bytes 1048600
  87.1 0.0 copy-start.4
  87.1 1.2 %copy-done.4 = bf16[512,1024]{1,0:T(8,128)(2,1)S(1)} copy-done((bf16[512,1024]{1,0:T(8,128)(2,1)S(1)}, bf16[512,1024]{1,0:T(8,128)(2,1)}, u32[]{:S(2)}) %copy-start.4) | copy-done | bytes 1048600
  88.4 4.2 %band_earlier.3 = (bf16[272,512]{1,0:T(8,128)(2,1)}, bf16[272,512]{1,0:T(8,128)(2,1)}) custom-call(s32[1]{0:T(128)} %bitcast.core_ref, bf16[1024,256]{1,0:T(8,128)(2,1)} %collective-permute-done.4.q_ref, bf16[1024,512]{1,0:T(8,128)(2,1)S(1)} %copy-done.2, bf16[512,1024]{1,0:T(8,128)(2,1)S(1)} %copy-done.4), custom_call_target="tpu_custom_call" | custom-call | flops 3400000000 | bytes 16384 | tf_op jit(solution)/shard_map/band_earlier/pallas_call | solution.py:227
  92.6 3.1 %collective-permute-start.5 = (bf16[272,512]{1,0:T(8,128)(2,1)}, bf16[272,512]{1,0:T(8,128)(2,1)S(1)}, u32[]{:S(2)}, u32[]{:S(2)}) collective-permute-start(bf16[272,512]{1,0:T(8,128)(2,1)} %get-tuple-element.29), channel_id=1, source_target_pairs={{0,2},{1,3},{2,4},{3,5},{4,6},{5,7},{6,8},{7,9},{8,10},{9,11},{10,... | collective-permute-start | bytes 835592 | tf_op jit(solution)/shard_map/ppermute | solution.py:401
  95.7 3.3 %collective-permute-start.7 = (bf16[272,512]{1,0:T(8,128)(2,1)}, bf16[272,512]{1,0:T(8,128)(2,1)S(1)}, u32[]{:S(2)}, u32[]{:S(2)}) collective-permute-start(bf16[272,512]{1,0:T(8,128)(2,1)} %get-tuple-element.31), channel_id=1, source_target_pairs={{0,3},{1,2},{2,5},{3,4},{4,7},{5,6},{6,9},{7,8},{8,11},{9,10},{10,... | collective-permute-start | bytes 835592 | tf_op jit(solution)/shard_map/ppermute | solution.py:402
  98.9 0.1 pad_add_fusion.flags_ref
  99.0 0.0 collective-permute-done.1.local_cross
  99.0 9.1 %collective-permute-done.5.same_b = bf16[272,512]{1,0:T(8,128)(2,1)S(1)} collective-permute-done((bf16[272,512]{1,0:T(8,128)(2,1)}, bf16[272,512]{1,0:T(8,128)(2,1)S(1)}, u32[]{:S(2)}, u32[]{:S(2)}) %collective-permute-start.5) | collective-permute-done | bytes 278560 | tf_op jit(solution)/shard_map/ppermute | solution.py:401
  108.1 6.0 %collective-permute-done.7.cross_b = bf16[272,512]{1,0:T(8,128)(2,1)S(1)} collective-permute-done((bf16[272,512]{1,0:T(8,128)(2,1)}, bf16[272,512]{1,0:T(8,128)(2,1)S(1)}, u32[]{:S(2)}, u32[]{:S(2)}) %collective-permute-start.7) | collective-permute-done | bytes 278560 | tf_op jit(solution)/shard_map/ppermute | solution.py:402
  114.2 0.0 all-to-all-done.1
  114.2 0.0 copy-start.6
  114.2 1.1 copy-done.6
  115.2 3.1 %merge.1 = bf16[512,2048]{1,0:T(8,128)(2,1)} custom-call(s32[2]{0:T(128)S(1)} %pad_add_fusion.flags_ref, bf16[544,512]{1,0:T(8,128)(2,1)S(1)} %copy-done.6, bf16[544,512]{1,0:T(8,128)(2,1)S(1)} %collective-permute-done.1.local_cross, bf16[272,512]{1,0:T(8,128)(2,1)S(1)} %collective-permute-done.3.same_a, bf16[272,512]{1,0:T(8,128)(2,1)S(1)} %collective-permute-done.5.same_b, ...), custom_call_target="tpu_custom_call" | custom-call | flops 3000000000 | bytes 16384 | tf_op jit(solution)/shard_map/merge/pallas_call | solution.py:356
Async XLA Ops:
  0.0 12.0 %collective-permute-start = (bf16[512,2048]{1,0:T(8,128)(2,1)}, bf16[512,2048]{1,0:T(8,128)(2,1)}, u32[]{:S(2)}, u32[]{:S(2)}) collective-permute-start(bf16[512,2048]{1,0:T(8,128)(2,1)} %own_ref.3), channel_id=1, source_target_pairs={{0,1},{1,0},{2,3},{3,2},{4,5},{5,4},{6,7},{7,6},{8,9},{9,8},{10,11... | collective-permute-start | bytes 6291464 | tf_op jit(solution)/shard_map/ppermute | solution.py:395
  0.7 11.3 %copy-start = (bf16[512,2048]{1,0:T(8,128)(2,1)S(1)}, bf16[512,2048]{1,0:T(8,128)(2,1)}, u32[]{:S(2)}) copy-start(bf16[512,2048]{1,0:T(8,128)(2,1)} %own_ref.3) | copy-start | bytes 6291460
  0.7 53.2 %all-to-all-start = ((bf16[64,8,2048]{2,1,0:T(8,128)(2,1)}), bf16[64,8,2048]{2,1,0:T(8,128)(2,1)}, u32[]{:S(2)}, u32[]{:S(2)}) async-start(bf16[64,8,2048]{2,1,0:T(8,128)(2,1)} %bitcast.6), calls=%async_computation | async-start | bytes 4194304 | tf_op jit(solution)/shard_map/all_to_all | solution.py:388
  16.6 31.6 %collective-permute-start.2 = (bf16[1024,256]{1,0:T(8,128)(2,1)S(1)}, bf16[1024,256]{1,0:T(8,128)(2,1)S(1)}, u32[]{:S(2)}, u32[]{:S(2)}) collective-permute-start(bf16[1024,256]{1,0:T(8,128)(2,1)S(1)} %get-tuple-element.19), channel_id=1, source_target_pairs={{2,0},{3,1},{4,2},{5,3},{6,4},{7,5},{8,6},{9,7},{10,8},{11,9},{12,... | collective-permute-start | bytes 1572872 | tf_op jit(solution)/shard_map/ppermute | solution.py:398
  23.0 62.9 %collective-permute-start.4 = (bf16[1024,256]{1,0:T(8,128)(2,1)S(1)}, bf16[1024,256]{1,0:T(8,128)(2,1)}, u32[]{:S(2)}, u32[]{:S(2)}) collective-permute-start(bf16[1024,256]{1,0:T(8,128)(2,1)S(1)} %get-tuple-element.20), channel_id=1, source_target_pairs={{2,0},{3,1},{4,2},{5,3},{6,4},{7,5},{8,6},{9,7},{10,8},{11,9},{12,... | collective-permute-start | bytes 1572872 | tf_op jit(solution)/shard_map/ppermute | solution.py:398
  33.1 15.1 %copy-start.1 = (bf16[1024,512]{1,0:T(8,128)(2,1)}, bf16[1024,512]{1,0:T(8,128)(2,1)S(1)}, u32[]{:S(2)}) copy-start(bf16[1024,512]{1,0:T(8,128)(2,1)S(1)} %get-tuple-element.21.k_ref) | copy-start | bytes 3145732
  33.1 15.1 %copy-start.3 = (bf16[512,1024]{1,0:T(8,128)(2,1)}, bf16[512,1024]{1,0:T(8,128)(2,1)S(1)}, u32[]{:S(2)}) copy-start(bf16[512,1024]{1,0:T(8,128)(2,1)S(1)} %get-tuple-element.22.vt_ref) | copy-start | bytes 3145732
  38.7 11.9 %copy-start.5 = (bf16[544,512]{1,0:T(8,128)(2,1)}, bf16[544,512]{1,0:T(8,128)(2,1)S(1)}, u32[]{:S(2)}) copy-start(bf16[544,512]{1,0:T(8,128)(2,1)S(1)} %get-tuple-element.23.local_same) | copy-start | bytes 1671172
  50.6 24.8 %collective-permute-start.3 = (bf16[272,512]{1,0:T(8,128)(2,1)S(1)}, bf16[272,512]{1,0:T(8,128)(2,1)S(1)}, u32[]{:S(2)}, u32[]{:S(2)}) collective-permute-start(bf16[272,512]{1,0:T(8,128)(2,1)S(1)} %get-tuple-element.26), channel_id=1, source_target_pairs={{0,2},{1,3},{2,4},{3,5},{4,6},{5,7},{6,8},{7,9},{8,10},{9,11},{10,... | collective-permute-start | bytes 835592 | tf_op jit(solution)/shard_map/ppermute | solution.py:401
  53.9 21.5 %collective-permute-start.6 = (bf16[272,512]{1,0:T(8,128)(2,1)S(1)}, bf16[272,512]{1,0:T(8,128)(2,1)S(1)}, u32[]{:S(2)}, u32[]{:S(2)}) collective-permute-start(bf16[272,512]{1,0:T(8,128)(2,1)S(1)} %get-tuple-element.30), channel_id=1, source_target_pairs={{0,3},{1,2},{2,5},{3,4},{4,7},{5,6},{6,9},{7,8},{8,11},{9,10},{10,... | collective-permute-start | bytes 835592 | tf_op jit(solution)/shard_map/ppermute | solution.py:402
  75.4 38.8 %all-to-all-start.1 = ((bf16[64,8,1024]{2,1,0:T(8,128)(2,1)}), bf16[64,8,1024]{2,1,0:T(8,128)(2,1)S(1)}, u32[]{:S(2)}, u32[]{:S(2)}) async-start(bf16[64,8,1024]{2,1,0:T(8,128)(2,1)} %bitcast.4), calls=%async_computation.1 | async-start | bytes 2097152 | tf_op jit(solution)/shard_map/all_to_all | solution.py:388
  84.9 14.2 %collective-permute-start.1 = (bf16[544,512]{1,0:T(8,128)(2,1)S(1)}, bf16[544,512]{1,0:T(8,128)(2,1)S(1)}, u32[]{:S(2)}, u32[]{:S(2)}) collective-permute-start(bf16[544,512]{1,0:T(8,128)(2,1)S(1)} %get-tuple-element.24), channel_id=1, source_target_pairs={{0,1},{1,0},{2,3},{3,2},{4,5},{5,4},{6,7},{7,6},{8,9},{9,8},{10,11... | collective-permute-start | bytes 1671176 | tf_op jit(solution)/shard_map/ppermute | solution.py:395
  85.9 1.2 %copy-start.2 = (bf16[1024,512]{1,0:T(8,128)(2,1)S(1)}, bf16[1024,512]{1,0:T(8,128)(2,1)}, u32[]{:S(2)}) copy-start(bf16[1024,512]{1,0:T(8,128)(2,1)} %copy-done.1) | copy-start | bytes 3145732
  87.1 1.2 %copy-start.4 = (bf16[512,1024]{1,0:T(8,128)(2,1)S(1)}, bf16[512,1024]{1,0:T(8,128)(2,1)}, u32[]{:S(2)}) copy-start(bf16[512,1024]{1,0:T(8,128)(2,1)} %copy-done.3) | copy-start | bytes 3145732
  92.6 15.6 %collective-permute-start.5 = (bf16[272,512]{1,0:T(8,128)(2,1)}, bf16[272,512]{1,0:T(8,128)(2,1)S(1)}, u32[]{:S(2)}, u32[]{:S(2)}) collective-permute-start(bf16[272,512]{1,0:T(8,128)(2,1)} %get-tuple-element.29), channel_id=1, source_target_pairs={{0,2},{1,3},{2,4},{3,5},{4,6},{5,7},{6,8},{7,9},{8,10},{9,11},{10,... | collective-permute-start | bytes 835592 | tf_op jit(solution)/shard_map/ppermute | solution.py:401
  95.7 18.5 %collective-permute-start.7 = (bf16[272,512]{1,0:T(8,128)(2,1)}, bf16[272,512]{1,0:T(8,128)(2,1)S(1)}, u32[]{:S(2)}, u32[]{:S(2)}) collective-permute-start(bf16[272,512]{1,0:T(8,128)(2,1)} %get-tuple-element.31), channel_id=1, source_target_pairs={{0,3},{1,2},{2,5},{3,4},{4,7},{5,6},{6,9},{7,8},{8,11},{9,10},{10,... | collective-permute-start | bytes 835592 | tf_op jit(solution)/shard_map/ppermute | solution.py:402
  114.2 1.1 copy-start.6

commit v3 on v2

v3 whole, which is shorter than its diff:
```python
import functools
import math

import jax
import jax.numpy as jnp
from jax import lax
from jax.experimental import pallas as pl
from jax.experimental.pallas import tpu as pltpu
from jax.sharding import PartitionSpec as P

HEAD = 128
HEADS = 8
STRIDE = 1024
HALF = 512
BLOCK = 256
SCALE2 = math.log2(math.e) / math.sqrt(HEAD)
NEG = -1e30
VMEM_LIMIT = 28 << 20


def params():
    return pltpu.CompilerParams(vmem_limit_bytes=VMEM_LIMIT)


def cost(us):
    return pl.CostEstimate(flops=int(us * 10**9), bytes_accessed=1 << 14, transcendentals=0)


def project_kernel(parts, core_ref, x_ref, w_ref, *refs):
    outs = refs[-len(parts) :]
    value = jnp.dot(x_ref[...], w_ref[...], preferred_element_type=jnp.float32)
    for index, (part, out_ref) in enumerate(zip(parts, outs)):

        @pl.when(pl.program_id(0) // 2 == index)
        def _():
            out_ref[...] = (value.T if part == 2 else value).astype(jnp.bfloat16)


def project(parts, own, core, x, w_row, before=()):
    depth = x.shape[1]
    half = (lambda c: c[0]) if own else (lambda c: 1 - c[0])

    def weight_block(j, c):
        return (0, 4 * (parts[0] + j // 2) + 2 * c[0] + j % 2)

    def spec(index, part):
        block = lambda j: jnp.clip(j - 2 * index, 0, 1)
        if part == 2:
            return pl.BlockSpec((BLOCK, HALF), lambda j, c: (block(j), half(c)))
        return pl.BlockSpec((HALF, BLOCK), lambda j, c: (half(c), block(j)))

    shapes = [(HALF, STRIDE) if part == 2 else (STRIDE, HALF) for part in parts]
    return pl.pallas_call(
        functools.partial(project_kernel, parts),
        grid_spec=pltpu.PrefetchScalarGridSpec(
            num_scalar_prefetch=1,
            grid=(2 * len(parts),),
            in_specs=[
                pl.BlockSpec((HALF, depth), lambda j, c: (0, 0)),
                pl.BlockSpec((depth, BLOCK), weight_block),
            ]
            + [pl.BlockSpec(memory_space=pl.ANY)] * len(before),
            out_specs=[spec(index, part) for index, part in enumerate(parts)],
        ),
        out_shape=[jax.ShapeDtypeStruct(shape, jnp.bfloat16) for shape in shapes],
        input_output_aliases={3 + index: index for index in range(len(before))},
        compiler_params=params(),
        cost_estimate=cost(0.2 * len(parts)),
        name="project",
    )(core, x, w_row, *before)


def score_blocks(query, key_ref, columns, spans):
    return [
        lax.dot_general(
            key_ref[low:high, columns], query, (((1,), (1,)), ((), ())),
            preferred_element_type=jnp.float32,
        )
        for low, high in spans
    ]


def softmax_out(scores, biases, value_t_blocks):
    scores = [s if b is None else s + b for s, b in zip(scores, biases)]
    top = functools.reduce(jnp.maximum, [jnp.max(s, axis=0, keepdims=True) for s in scores])
    expd = [jnp.exp2((s - top) * SCALE2) for s in scores]
    total = sum(jnp.sum(e, axis=0, keepdims=True) for e in expd)
    out = sum(
        jnp.dot(v, e.astype(jnp.bfloat16), preferred_element_type=jnp.float32)
        for v, e in zip(value_t_blocks, expd)
    )
    return out * (1.0 / total), top, total


def pipelined(jobs, ahead, start, finish):
    pending, results = [], {}
    for job in jobs:
        pending.append((job, start(*job)))
        if len(pending) > ahead:
            first, value = pending.pop(0)
            results[first] = finish(*first, value)
    for first, value in pending:
        results[first] = finish(*first, value)
    return results


def split3(value):
    high = value.astype(jnp.bfloat16).astype(jnp.float32)
    rest = value - high
    mid = rest.astype(jnp.bfloat16).astype(jnp.float32)
    return [high, mid, rest - mid]


def band_kernel(
    earlier, heads, ahead, core_ref, q_ref, k_ref, vt_ref, same_ref, cross_ref, stat_ref, bias_ref
):
    step = pl.program_id(0)
    core = core_ref[0]
    parts = STRIDE // BLOCK

    @pl.when(step == 0)
    def _():
        kpos = lax.broadcasted_iota(jnp.int32, (BLOCK, BLOCK), 0)
        qpos = lax.broadcasted_iota(jnp.int32, (BLOCK, BLOCK), 1)
        allowed = kpos > qpos if earlier else kpos <= qpos
        bias_ref[...] = jnp.where(allowed, 0.0, NEG)

    def spans(part):
        low, high = part * BLOCK, (part + 1) * BLOCK
        rest = (high, STRIDE) if earlier else (0, low)
        return [(low, high)] + ([rest] if rest[0] < rest[1] else [])

    def columns(head):
        return slice(head * HEAD, (head + 1) * HEAD)

    def start(part, head):
        query = q_ref[part * BLOCK : (part + 1) * BLOCK, columns(head)]
        return score_blocks(query, k_ref, columns(head), spans(part))

    def finish(part, head, scores):
        values = [vt_ref[columns(head), low:high] for low, high in spans(part)]
        out, top, total = softmax_out(scores, [bias_ref[...], None], values)
        return out.astype(jnp.bfloat16), top, total

    jobs = [(part, head) for part in range(parts) for head in range(2)]
    results = pipelined(jobs, ahead, start, finish)
    for head in range(2):
        stats = [
            jnp.concatenate(
                split3(results[part, head][1])
                + split3(results[part, head][2])
                + [jnp.zeros((2, BLOCK), jnp.float32)],
                axis=0,
            )
            for part in range(parts)
        ]
        stat_ref[step * 2 + head] = jnp.concatenate(stats, axis=1)
    rows = pl.ds(pl.multiple_of(step * 2 * HEAD, 2 * HEAD), 2 * HEAD)
    for half in range(2):
        piece = jnp.concatenate(
            [
                jnp.concatenate([results[2 * half + part, head][0] for part in range(2)], axis=1)
                for head in range(2)
            ],
            axis=0,
        )

        @pl.when(core == half)
        def _():
            same_ref[rows, :] = piece

        @pl.when(core != half)
        def _():
            cross_ref[rows, :] = piece

    @pl.when(step == heads // 2 - 1)
    def _():
        stats = jnp.concatenate([stat_ref[h] for h in range(heads)], axis=0).astype(jnp.bfloat16)
        for half in range(2):
            piece = stats[:, half * HALF : (half + 1) * HALF]

            @pl.when(core == half)
            def _():
                same_ref[heads * HEAD :, :] = piece

            @pl.when(core != half)
            def _():
                cross_ref[heads * HEAD :, :] = piece


def band_part(earlier, core, query, keys, values_t, first=0):
    heads = query.shape[1] // HEAD
    payload = heads * (HEAD + 8)
    whole = pl.BlockSpec((payload, HALF), lambda h, c: (0, 0))
    return pl.pallas_call(
        functools.partial(band_kernel, earlier, heads, 2 if earlier else 4),
        grid_spec=pltpu.PrefetchScalarGridSpec(
            num_scalar_prefetch=1,
            grid=(heads // 2,),
            in_specs=[
                pl.BlockSpec((STRIDE, 2 * HEAD), lambda h, c: (0, h)),
                pl.BlockSpec((STRIDE, 2 * HEAD), lambda h, c: (0, first + h)),
                pl.BlockSpec((2 * HEAD, STRIDE), lambda h, c: (first + h, 0)),
            ],
            out_specs=[whole, whole],
            scratch_shapes=[
                pltpu.VMEM((heads, 8, STRIDE), jnp.float32),
                pltpu.VMEM((BLOCK, BLOCK), jnp.float32),
            ],
        ),
        out_shape=[jax.ShapeDtypeStruct((payload, HALF), jnp.bfloat16)] * 2,
        compiler_params=params(),
        cost_estimate=cost(20 if earlier else 0.2),
        name="band_earlier" if earlier else "band_local",
    )(core, query, keys, values_t)


def column_kernel(group, q_ref, k_ref, v_ref, o_ref, bias_ref):
    parts = HALF // BLOCK
    heads = q_ref.shape[1] // HEAD

    @pl.when(pl.program_id(0) == 0)
    def _():
        kpos = lax.broadcasted_iota(jnp.int32, (BLOCK, BLOCK), 0)
        qpos = lax.broadcasted_iota(jnp.int32, (BLOCK, BLOCK), 1)
        column = ((qpos - kpos) & (group - 1)) == 0
        bias_ref[0] = jnp.where(column, 0.0, NEG)
        bias_ref[1] = jnp.where(column & (kpos <= qpos), 0.0, NEG)

    values_t = v_ref[...].astype(jnp.float32).T.astype(jnp.bfloat16)

    def spans(part):
        return [(block * BLOCK, (block + 1) * BLOCK) for block in range(part + 1)]

    def columns(head):
        return slice(head * HEAD, (head + 1) * HEAD)

    def start(part, head):
        query = q_ref[part * BLOCK : (part + 1) * BLOCK, columns(head)]
        return score_blocks(query, k_ref, columns(head), spans(part))

    def finish(part, head, scores):
        values = [values_t[columns(head), low:high] for low, high in spans(part)]
        biases = [bias_ref[1 if block == part else 0] for block in range(part + 1)]
        out = softmax_out(scores, biases, values)[0]
        o_ref[part * BLOCK : (part + 1) * BLOCK, columns(head)] = out.T.astype(jnp.bfloat16)

    pipelined([(part, head) for part in range(parts) for head in range(heads)], 2, start, finish)


def column_attention(projected, group):
    rows = projected.shape[0]
    heads = 4
    steps = HEADS // heads
    spec = lambda third: pl.BlockSpec((rows, heads * HEAD), lambda j: (0, third * steps + j))
    return pl.pallas_call(
        functools.partial(column_kernel, group),
        grid=(steps,),
        in_specs=[spec(0), spec(1), spec(2)],
        out_specs=pl.BlockSpec((rows, heads * HEAD), lambda j: (0, j)),
        out_shape=jax.ShapeDtypeStruct((rows, HEADS * HEAD), jnp.bfloat16),
        scratch_shapes=[pltpu.VMEM((2, BLOCK, BLOCK), jnp.float32)],
        compiler_params=params(),
        cost_estimate=cost(6),
        name="column_attention",
    )(projected, projected, projected)


def merge_kernel(flags_ref, local_same, local_cross, earlier_same, earlier_cross, o_ref):
    has_earlier = flags_ref[1] > 0

    def stats(ref, head):
        rows = ref[HALF:, :].astype(jnp.float32)[8 * head : 8 * head + 8]
        return rows[0:1] + rows[1:2] + rows[2:3], rows[3:4] + rows[4:5] + rows[5:6]

    def merge(local_ref, earlier_ref):
        for head in range(4):
            top_l, sum_l = stats(local_ref, head)
            top_e, sum_e = stats(earlier_ref, head)
            top_e = jnp.where(has_earlier, top_e, NEG)
            top = jnp.maximum(top_l, top_e)
            weight_l = jnp.exp2((top_l - top) * SCALE2) * sum_l
            weight_e = jnp.exp2((top_e - top) * SCALE2) * sum_e
            weight_e = jnp.where(has_earlier, weight_e, 0.0)
            inverse = 1.0 / (weight_l + weight_e)
            columns = slice(head * HEAD, (head + 1) * HEAD)
            out_l = local_ref[columns, :].astype(jnp.float32)
            out_e = earlier_ref[columns, :].astype(jnp.float32)
            out = out_l * (weight_l * inverse) + out_e * (weight_e * inverse)
            o_ref[:, columns] = out.T.astype(jnp.bfloat16)

    @pl.when(pl.program_id(0) == 0)
    def _():
        merge(local_same, earlier_same)

    @pl.when(pl.program_id(0) == 1)
    def _():
        merge(local_cross, earlier_cross)


def merge_band(flags, *payloads):
    def out_block(j, c):
        return (0, jnp.where(j == 0, c[0], 1 - c[0]))

    return pl.pallas_call(
        merge_kernel,
        grid_spec=pltpu.PrefetchScalarGridSpec(
            num_scalar_prefetch=1,
            grid=(2,),
            in_specs=[pl.BlockSpec(p.shape, lambda j, c: (0, 0)) for p in payloads],
            out_specs=pl.BlockSpec((HALF, HALF), out_block),
        ),
        out_shape=jax.ShapeDtypeStruct((HALF, 2 * HEADS * HEAD), jnp.bfloat16),
        compiler_params=params(),
        cost_estimate=cost(60),
        name="merge_band",
    )(flags, *payloads)


def place_kernel(columns_ref, _, o_ref):
    o_ref[...] = columns_ref[...]


def place_columns(band_out, col_out):
    width = col_out.shape[1]
    return pl.pallas_call(
        place_kernel,
        grid=(4,),
        in_specs=[
            pl.BlockSpec((HALF // 4, width), lambda j: (j, 0)),
            pl.BlockSpec(memory_space=pl.ANY),
        ],
        out_specs=pl.BlockSpec((HALF // 4, width), lambda j: (j, 1)),
        out_shape=jax.ShapeDtypeStruct(band_out.shape, jnp.bfloat16),
        input_output_aliases={1: 0},
        compiler_params=params(),
        cost_estimate=cost(1),
        name="place_columns",
    )(col_out, band_out)


def in_hbm(value):
    return pltpu.with_memory_space_constraint(value, pltpu.HBM)


def after(value, *others):
    return lax.optimization_barrier((value,) + others)[0]


def on_device(tokens, w_row, w_column):
    count = lax.axis_size("seq")
    chips = count // 2
    rank = lax.axis_index("seq")
    core = (rank % 2).astype(jnp.int32)
    core_arr = core.reshape(1)
    flags = jnp.stack([core, (rank >= 2).astype(jnp.int32)])
    group = HALF // chips
    same_core = [list(range(0, count, 2)), list(range(1, count, 2))]

    def exchange(value):
        width = value.shape[1]
        value = lax.all_to_all(
            value.reshape(chips, group, width), "seq", split_axis=0, concat_axis=0,
            axis_index_groups=same_core, tiled=True,
        )
        return value.reshape(HALF, width)

    def swapped(value):
        return lax.ppermute(value, "seq", [(d, d ^ 1) for d in range(count)])

    def to_previous(value):
        return lax.ppermute(value, "seq", [(d, d - 2) for d in range(2, count)])

    def to_next(same, cross):
        same = lax.ppermute(same, "seq", [(d, d + 2) for d in range(count - 2)])
        cross = lax.ppermute(cross, "seq", [(d, (d + 2) ^ 1) for d in range(count - 2)])
        return same, cross

    w_row = in_hbm(w_row)
    sibling = swapped(tokens)
    query, keys, values_t = project((0, 1, 2), True, core_arr, tokens, w_row)
    query, keys, values_t = in_hbm(query), in_hbm(keys), in_hbm(values_t)
    (query,) = project((0,), False, core_arr, sibling, w_row, (query,))
    next_query = to_previous(query)
    columns = exchange(after(tokens, query))
    keys, values_t = project((1, 2), False, core_arr, sibling, w_row, (keys, values_t))
    query, keys, values_t = in_hbm(query), in_hbm(keys), in_hbm(values_t)
    local_same, local_cross = band_part(False, core_arr, query, keys, values_t)
    earlier = band_part(True, core_arr, after(next_query, local_same), keys, values_t)
    same, cross = to_next(*earlier)
    columns = after(columns, earlier[0])
    col_proj = jnp.dot(columns, w_column, preferred_element_type=jnp.float32).astype(jnp.bfloat16)
    col_out = exchange(column_attention(col_proj, group))
    band_out = merge_band(flags, local_same, swapped(local_cross), same, cross)
    return place_columns(band_out, col_out)


def solution(mesh):
    in_specs = (P("seq", None), P(), P())
    out_specs = P("seq", None)
    return jax.shard_map(
        on_device, mesh=mesh, in_specs=in_specs, out_specs=out_specs, check_vma=False
    )
```

time: 119 us -> 135 us (1.13)
  the two profiles are of different devices: /device:TPU:3 before, /device:TPU:0 now
where the time goes in v3:
time: 135 us; the launch traced here: 134 us
  Pallas kernels  43.5 us (32%)
  starting transfers between devices  41.9 us (31%)
  waiting for transfers between devices  35.9 us (27%)
  matrix products  10.3 us (8%)
  local copies, waits for them, and re-layouts  2.56 us (2%)
    all_to_all x2, starting transfers between devices, exchange(): lax.all_to_all(value.reshape(chips, group, width), 'seq', split_axis=0, c...  34.1 us
    ppermute x1, waiting for transfers between devices, to_previous(): return lax.ppermute(value, 'seq', [(d, d - 2) for d in range(2, count)])  21.4 us
    pallas_call x3, Pallas kernels, project(): pl.pallas_call(functools.partial(project_kernel, parts), grid_spec=pltpu....  17.2 us
    pallas_call x2, Pallas kernels, band_part(): pl.pallas_call(functools.partial(band_kernel, earlier, heads, 2 if earlie...  14.6 us
    all_to_all x2, waiting for transfers between devices, exchange(): lax.all_to_all(value.reshape(chips, group, width), 'seq', split_axis=0, c...  14.4 us
    dot_general x1, matrix products, on_device(): jnp.dot(columns, w_column, preferred_element_type=jnp.float32)  10.3 us
    pallas_call x1, Pallas kernels, column_attention(): pl.pallas_call(functools.partial(column_kernel, group), grid=(steps,), in...  6.89 us
    ppermute x1, starting transfers between devices, to_next(): same = lax.ppermute(same, 'seq', [(d, d + 2) for d in range(count - 2)])  3.92 us
  transfers between devices with their start and end apart: 7, of which 2 were waited for; matrix products, arithmetic and copies ran while one was open for 8% of the time, Pallas kernels for 28%

profile of v3, /device:TPU:0, one launch (start us, length us, event | category | flops | bytes accessed | tf_op | source)
XLA Modules:
  0.0 134.3 jit_solution(5624243370620399182)
XLA Ops:
  0.0 0.0 collective-permute-start
  0.0 0.0 copy-start
  0.0 1.6 %copy-done = bf16[512,2048]{1,0:T(8,128)(2,1)S(1)} copy-done((bf16[512,2048]{1,0:T(8,128)(2,1)S(1)}, bf16[512,2048]{1,0:T(8,128)(2,1)}, u32[]{:S(2)}) %copy-start) | copy-done | bytes 2097176
  1.6 7.2 %project.3 = (bf16[1024,512]{1,0:T(8,128)(2,1)S(1)}, bf16[1024,512]{1,0:T(8,128)(2,1)S(1)}, bf16[512,1024]{1,0:T(8,128)(2,1)S(1)}) custom-call(s32[1]{0:T(128)} %bitcast.core_ref, bf16[512,2048]{1,0:T(8,128)(2,1)S(1)} %copy-done, bf16[2048,3072]{1,0:T(8,128)(2,1)} %w_ref.5), custom_call_target="tpu_custom_call" | custom-call | flops 600000000 | bytes 16384 | tf_op jit(solution)/shard_map/project/pallas_call | solution.py:53
  8.8 0.0 copy-start.3
  8.8 1.0 copy-done.3
  9.8 0.0 copy-start.1
  9.8 0.0 copy-start.2
  9.8 0.0 collective-permute-done.x_ref
  9.8 4.2 %project.4.q_ref = bf16[1024,512]{1,0:T(8,128)(2,1)} custom-call(s32[1]{0:T(128)} %bitcast.core_ref, bf16[512,2048]{1,0:T(8,128)(2,1)S(1)} %collective-permute-done.x_ref, bf16[2048,3072]{1,0:T(8,128)(2,1)} %w_ref.5, bf16[1024,512]{1,0:T(8,128)(2,1)} %copy-done.3), custom_call_target="tpu_custom_call", output_to_operand_aliasing={{}: (3, {})} | custom-call | flops 200000000 | bytes 16384 | tf_op jit(solution)/shard_map/project/pallas_call | solution.py:53
  14.0 0.0 copy-done.1
  14.0 0.0 copy-done.2
  14.0 1.3 collective-permute-start.1
  15.3 13.0 %all-to-all-start = ((bf16[64,8,2048]{2,1,0:T(8,128)(2,1)}), bf16[64,8,2048]{2,1,0:T(8,128)(2,1)}, u32[]{:S(2)}, u32[]{:S(2)}) async-start(bf16[64,8,2048]{2,1,0:T(8,128)(2,1)} %bitcast.8), calls=%async_computation | async-start | bytes 4194304 | tf_op jit(solution)/shard_map/all_to_all | solution.py:362
  28.2 0.1 pad_add_fusion.flags_ref
  28.3 5.9 %project.5 = (bf16[1024,512]{1,0:T(8,128)(2,1)}, bf16[512,1024]{1,0:T(8,128)(2,1)}) custom-call(s32[1]{0:T(128)} %bitcast.core_ref, bf16[512,2048]{1,0:T(8,128)(2,1)S(1)} %collective-permute-done.x_ref, bf16[2048,3072]{1,0:T(8,128)(2,1)} %w_ref.5, bf16[1024,512]{1,0:T(8,128)(2,1)} %copy-done.1, ...), custom_call_target="tpu_custom_call", output_to_operand_aliasing={{0}: (3, {}), {1}: (4, {})} | custom-call | flops 400000000 | bytes 16384 | tf_op jit(solution)/shard_map/project/pallas_call | solution.py:53
  34.2 7.5 %band_local.1 = (bf16[544,512]{1,0:T(8,128)(2,1)S(1)}, bf16[544,512]{1,0:T(8,128)(2,1)}) custom-call(s32[1]{0:T(128)} %bitcast.core_ref, bf16[1024,512]{1,0:T(8,128)(2,1)} %project.4.q_ref, bf16[1024,512]{1,0:T(8,128)(2,1)} %get-tuple-element.21.k_ref, bf16[512,1024]{1,0:T(8,128)(2,1)} %get-tuple-element.22.vt_ref), custom_call_target="tpu_custom_call" | custom-call | flops 200000000 | bytes 16384 | tf_op jit(solution)/shard_map/band_local/pallas_call | solution.py:195
  41.7 0.0 collective-permute-start.2
  41.7 21.4 %collective-permute-done.1.q_ref = bf16[1024,512]{1,0:T(8,128)(2,1)S(1)} collective-permute-done((bf16[1024,512]{1,0:T(8,128)(2,1)}, bf16[1024,512]{1,0:T(8,128)(2,1)S(1)}, u32[]{:S(2)}, u32[]{:S(2)}) %collective-permute-start.1) | collective-permute-done | bytes 1048608 | tf_op jit(solution)/shard_map/ppermute | solution.py:372
  63.2 7.1 %band_earlier.1 = (bf16[544,512]{1,0:T(8,128)(2,1)}, bf16[544,512]{1,0:T(8,128)(2,1)}) custom-call(s32[1]{0:T(128)} %bitcast.core_ref, bf16[1024,512]{1,0:T(8,128)(2,1)S(1)} %collective-permute-done.1.q_ref, bf16[1024,512]{1,0:T(8,128)(2,1)} %get-tuple-element.21.k_ref, bf16[512,1024]{1,0:T(8,128)(2,1)} %get-tuple-element.22.vt_ref), custom_call_target="tpu_custom_call" | custom-call | flops 20000000000 | bytes 16384 | tf_op jit(solution)/shard_map/band_earlier/pallas_call | solution.py:195
  70.2 3.9 %collective-permute-start.3 = (bf16[544,512]{1,0:T(8,128)(2,1)}, bf16[544,512]{1,0:T(8,128)(2,1)S(1)}, u32[]{:S(2)}, u32[]{:S(2)}) collective-permute-start(bf16[544,512]{1,0:T(8,128)(2,1)} %get-tuple-element.25), channel_id=1, source_target_pairs={{0,2},{1,3},{2,4},{3,5},{4,6},{5,7},{6,8},{7,9},{8,10},{9,11},{10,... | collective-permute-start | bytes 1671176 | tf_op jit(solution)/shard_map/ppermute | solution.py:375
  74.1 2.6 %collective-permute-start.4 = (bf16[544,512]{1,0:T(8,128)(2,1)}, bf16[544,512]{1,0:T(8,128)(2,1)S(1)}, u32[]{:S(2)}, u32[]{:S(2)}) collective-permute-start(bf16[544,512]{1,0:T(8,128)(2,1)} %get-tuple-element.28), channel_id=1, source_target_pairs={{0,3},{1,2},{2,5},{3,4},{4,7},{5,6},{6,9},{7,8},{8,11},{9,10},{10,... | collective-permute-start | bytes 1671176 | tf_op jit(solution)/shard_map/ppermute | solution.py:376
  76.7 0.0 all-to-all-done
  76.8 10.3 %convolution_convert_fusion.q_ref.k_ref.v_ref = bf16[512,3072]{1,0:T(8,128)(2,1)S(1)} fusion(bf16[512,2048]{1,0:T(8,128)(2,1)} %bitcast.2, bf16[2048,3072]{1,0:T(8,128)(2,1)} %param.5), kind=kOutput, calls=%fused_computation | convolution fusion | flops 6444023808 | bytes 17825792 | tf_op jit(solution)/shard_map/dot_general | solution.py:392
  87.0 6.9 %column_attention.1 = bf16[512,1024]{1,0:T(8,128)(2,1)} custom-call(bf16[512,3072]{1,0:T(8,128)(2,1)S(1)} %convolution_convert_fusion.q_ref.k_ref.v_ref, bf16[512,3072]{1,0:T(8,128)(2,1)S(1)} %convolution_convert_fusion.q_ref.k_ref.v_ref, bf16[512,3072]{1,0:T(8,128)(2,1)S(1)} %convolution_convert_fusion.q_ref.k_ref.v_ref), custom_call_target="tpu_custom_call" | custom-call | flops 6000000000 | bytes 16384 | tf_op jit(solution)/shard_map/column_attention/pallas_call | solution.py:256
  93.9 21.1 %all-to-all-start.1 = ((bf16[64,8,1024]{2,1,0:T(8,128)(2,1)}), bf16[64,8,1024]{2,1,0:T(8,128)(2,1)S(1)}, u32[]{:S(2)}, u32[]{:S(2)}) async-start(bf16[64,8,1024]{2,1,0:T(8,128)(2,1)} %bitcast.3), calls=%async_computation.1 | async-start | bytes 2097152 | tf_op jit(solution)/shard_map/all_to_all | solution.py:362
  115.1 0.0 collective-permute-done.2.local_cross
  115.1 0.0 collective-permute-done.3.earlier_same
  115.1 0.0 collective-permute-done.4.earlier_cross
  115.1 3.2 %merge_band.1._ = bf16[512,2048]{1,0:T(8,128)(2,1)} custom-call(s32[2]{0:T(128)S(1)} %pad_add_fusion.flags_ref, bf16[544,512]{1,0:T(8,128)(2,1)S(1)} %get-tuple-element.23.local_same, bf16[544,512]{1,0:T(8,128)(2,1)} %collective-permute-done.2.local_cross, bf16[544,512]{1,0:T(8,128)(2,1)S(1)} %collective-permute-done.3.earlier_same, ...), custom_call_target="tpu_custom_call" | custom-call | flops 60000002048 | bytes 16384 | tf_op jit(solution)/shard_map/merge_band/pallas_call | solution.py:305
  118.3 14.4 %all-to-all-done.1 = bf16[64,8,1024]{2,1,0:T(8,128)(2,1)S(1)} async-done(((bf16[64,8,1024]{2,1,0:T(8,128)(2,1)}), bf16[64,8,1024]{2,1,0:T(8,128)(2,1)S(1)}, u32[]{:S(2)}, u32[]{:S(2)}) %all-to-all-start.1) | async-done | bytes 1048608 | tf_op jit(solution)/shard_map/all_to_all | solution.py:362
  132.7 1.5 %place_columns.1 = bf16[512,2048]{1,0:T(8,128)(2,1)} custom-call(bf16[512,1024]{1,0:T(8,128)(2,1)S(1)} %bitcast.9, bf16[512,2048]{1,0:T(8,128)(2,1)} %merge_band.1._), custom_call_target="tpu_custom_call", output_to_operand_aliasing={{}: (1, {})} | custom-call | flops 1000000000 | bytes 16384 | tf_op jit(solution)/shard_map/place_columns/pallas_call | solution.py:326
Async XLA Ops:
  0.0 9.8 %collective-permute-start = (bf16[512,2048]{1,0:T(8,128)(2,1)}, bf16[512,2048]{1,0:T(8,128)(2,1)S(1)}, u32[]{:S(2)}, u32[]{:S(2)}) collective-permute-start(bf16[512,2048]{1,0:T(8,128)(2,1)} %x_ref.1), channel_id=1, source_target_pairs={{0,1},{1,0},{2,3},{3,2},{4,5},{5,4},{6,7},{7,6},{8,9},{9,8},{10,11... | collective-permute-start | bytes 6291464 | tf_op jit(solution)/shard_map/ppermute | solution.py:369
  0.0 1.6 %copy-start = (bf16[512,2048]{1,0:T(8,128)(2,1)S(1)}, bf16[512,2048]{1,0:T(8,128)(2,1)}, u32[]{:S(2)}) copy-start(bf16[512,2048]{1,0:T(8,128)(2,1)} %x_ref.1) | copy-start | bytes 6291460
  8.8 1.0 copy-start.3
  9.8 4.2 %copy-start.1 = (bf16[1024,512]{1,0:T(8,128)(2,1)}, bf16[1024,512]{1,0:T(8,128)(2,1)S(1)}, u32[]{:S(2)}) copy-start(bf16[1024,512]{1,0:T(8,128)(2,1)S(1)} %get-tuple-element.19.refs_0_) | copy-start | bytes 3145732
  9.8 4.2 %copy-start.2 = (bf16[512,1024]{1,0:T(8,128)(2,1)}, bf16[512,1024]{1,0:T(8,128)(2,1)S(1)}, u32[]{:S(2)}) copy-start(bf16[512,1024]{1,0:T(8,128)(2,1)S(1)} %get-tuple-element.20.refs_1_) | copy-start | bytes 3145732
  14.0 49.2 %collective-permute-start.1 = (bf16[1024,512]{1,0:T(8,128)(2,1)}, bf16[1024,512]{1,0:T(8,128)(2,1)S(1)}, u32[]{:S(2)}, u32[]{:S(2)}) collective-permute-start(bf16[1024,512]{1,0:T(8,128)(2,1)} %project.4.q_ref), channel_id=1, source_target_pairs={{2,0},{3,1},{4,2},{5,3},{6,4},{7,5},{8,6},{9,7},{10,8},{11,9},{12,... | collective-permute-start | bytes 3145736 | tf_op jit(solution)/shard_map/ppermute | solution.py:372
  15.3 61.5 %all-to-all-start = ((bf16[64,8,2048]{2,1,0:T(8,128)(2,1)}), bf16[64,8,2048]{2,1,0:T(8,128)(2,1)}, u32[]{:S(2)}, u32[]{:S(2)}) async-start(bf16[64,8,2048]{2,1,0:T(8,128)(2,1)} %bitcast.8), calls=%async_computation | async-start | bytes 4194304 | tf_op jit(solution)/shard_map/all_to_all | solution.py:362
  41.7 73.4 %collective-permute-start.2 = (bf16[544,512]{1,0:T(8,128)(2,1)}, bf16[544,512]{1,0:T(8,128)(2,1)}, u32[]{:S(2)}, u32[]{:S(2)}) collective-permute-start(bf16[544,512]{1,0:T(8,128)(2,1)} %get-tuple-element.27), channel_id=1, source_target_pairs={{0,1},{1,0},{2,3},{3,2},{4,5},{5,4},{6,7},{7,6},{8,9},{9,8},{10,11... | collective-permute-start | bytes 1671176 | tf_op jit(solution)/shard_map/ppermute | solution.py:369
  70.2 44.9 %collective-permute-start.3 = (bf16[544,512]{1,0:T(8,128)(2,1)}, bf16[544,512]{1,0:T(8,128)(2,1)S(1)}, u32[]{:S(2)}, u32[]{:S(2)}) collective-permute-start(bf16[544,512]{1,0:T(8,128)(2,1)} %get-tuple-element.25), channel_id=1, source_target_pairs={{0,2},{1,3},{2,4},{3,5},{4,6},{5,7},{6,8},{7,9},{8,10},{9,11},{10,... | collective-permute-start | bytes 1671176 | tf_op jit(solution)/shard_map/ppermute | solution.py:375
  74.1 40.9 %collective-permute-start.4 = (bf16[544,512]{1,0:T(8,128)(2,1)}, bf16[544,512]{1,0:T(8,128)(2,1)S(1)}, u32[]{:S(2)}, u32[]{:S(2)}) collective-permute-start(bf16[544,512]{1,0:T(8,128)(2,1)} %get-tuple-element.28), channel_id=1, source_target_pairs={{0,3},{1,2},{2,5},{3,4},{4,7},{5,6},{6,9},{7,8},{8,11},{9,10},{10,... | collective-permute-start | bytes 1671176 | tf_op jit(solution)/shard_map/ppermute | solution.py:376
  93.9 38.8 %all-to-all-start.1 = ((bf16[64,8,1024]{2,1,0:T(8,128)(2,1)}), bf16[64,8,1024]{2,1,0:T(8,128)(2,1)S(1)}, u32[]{:S(2)}, u32[]{:S(2)}) async-start(bf16[64,8,1024]{2,1,0:T(8,128)(2,1)} %bitcast.3), calls=%async_computation.1 | async-start | bytes 2097152 | tf_op jit(solution)/shard_map/all_to_all | solution.py:362

commit v4 on v3

--- a/solution.py
+++ b/solution.py
@@ -16,6 +16,7 @@
 SCALE2 = math.log2(math.e) / math.sqrt(HEAD)
 NEG = -1e30
 VMEM_LIMIT = 28 << 20
+PROJECT_COST, LOCAL_COST, A_COST, B_COST, MERGE_COST = 0.5, 0.5, 20, 0.5, 2
 
 
 def params():
@@ -26,48 +27,55 @@
     return pl.CostEstimate(flops=int(us * 10**9), bytes_accessed=1 << 14, transcendentals=0)
 
 
-def project_kernel(parts, core_ref, x_ref, w_ref, *refs):
-    outs = refs[-len(parts) :]
-    value = jnp.dot(x_ref[...], w_ref[...], preferred_element_type=jnp.float32)
-    for index, (part, out_ref) in enumerate(zip(parts, outs)):
-
-        @pl.when(pl.program_id(0) // 2 == index)
+def project_kernel(core_ref, own_ref, sibling_ref, w_ref, kv_a, kv_b, q_a, q_b):
+    core = core_ref[0]
+    for step, (kind, ref) in enumerate(PROJECT_ORDER):
+        ref = {"kv_a": kv_a, "kv_b": kv_b, "q_a": q_a, "q_b": q_b}[ref]
+
+        @pl.when(pl.program_id(0) == step)
         def _():
-            out_ref[...] = (value.T if part == 2 else value).astype(jnp.bfloat16)
-
-
-def project(parts, own, core, x, w_row, before=()):
-    depth = x.shape[1]
-    half = (lambda c: c[0]) if own else (lambda c: 1 - c[0])
+            for place, x_ref in ((core, own_ref), (1 - core, sibling_ref)):
+                value = jnp.dot(x_ref[...], w_ref[...], preferred_element_type=jnp.float32)
+                row = pl.multiple_of(place * HALF, HALF)
+                if kind == 2:
+                    value = value.T.astype(jnp.bfloat16)
+                    for block in range(HALF // BLOCK):
+                        rows = pl.ds(STRIDE + row + block * BLOCK, BLOCK)
+                        ref[rows, :] = value[:, block * BLOCK : (block + 1) * BLOCK]
+                else:
+                    ref[pl.ds(row, HALF), :] = value.astype(jnp.bfloat16)
+
+
+PROJECT_ORDER = [(1, "kv_a"), (2, "kv_a"), (0, "q_b"), (1, "kv_b"), (2, "kv_b"), (0, "q_a")]
+
+
+def project(core, tokens, sibling, w_row):
+    depth = tokens.shape[1]
 
     def weight_block(j, c):
-        return (0, 4 * (parts[0] + j // 2) + 2 * c[0] + j % 2)
-
-    def spec(index, part):
-        block = lambda j: jnp.clip(j - 2 * index, 0, 1)
-        if part == 2:
-            return pl.BlockSpec((BLOCK, HALF), lambda j, c: (block(j), half(c)))
-        return pl.BlockSpec((HALF, BLOCK), lambda j, c: (half(c), block(j)))
-
-    shapes = [(HALF, STRIDE) if part == 2 else (STRIDE, HALF) for part in parts]
+        kind = lax.rem(j + 1, 3)
+        pair = jnp.where((j >= 2) & (j <= 4), 1, 0)
+        return (0, 4 * kind + 2 * c[0] + pair)
+
+    whole = lambda rows, width: pl.BlockSpec((rows, width), lambda j, c: (0, 0))
+    outs = [(2 * STRIDE, BLOCK), (2 * STRIDE, BLOCK), (STRIDE, BLOCK), (STRIDE, BLOCK)]
     return pl.pallas_call(
-        functools.partial(project_kernel, parts),
+        project_kernel,
         grid_spec=pltpu.PrefetchScalarGridSpec(
             num_scalar_prefetch=1,
-            grid=(2 * len(parts),),
+            grid=(len(PROJECT_ORDER),),
             in_specs=[
-                pl.BlockSpec((HALF, depth), lambda j, c: (0, 0)),
+                whole(HALF, depth),
+                whole(HALF, depth),
                 pl.BlockSpec((depth, BLOCK), weight_block),
-            ]
-            + [pl.BlockSpec(memory_space=pl.ANY)] * len(before),
-            out_specs=[spec(index, part) for index, part in enumerate(parts)],
+            ],
+            out_specs=[whole(*shape) for shape in outs],
         ),
-        out_shape=[jax.ShapeDtypeStruct(shape, jnp.bfloat16) for shape in shapes],
-        input_output_aliases={3 + index: index for index in range(len(before))},
+        out_shape=[jax.ShapeDtypeStruct(shape, jnp.bfloat16) for shape in outs],
         compiler_params=params(),
-        cost_estimate=cost(0.2 * len(parts)),
+        cost_estimate=cost(PROJECT_COST),
         name="project",
-    )(core, x, w_row, *before)
+    )(core, tokens, sibling, w_row)
 
 
 def score_blocks(query, key_ref, columns, spans):
@@ -111,12 +119,12 @@
     return [high, mid, rest - mid]
 
 
-def band_kernel(
-    earlier, heads, ahead, core_ref, q_ref, k_ref, vt_ref, same_ref, cross_ref, stat_ref, bias_ref
-):
+def band_kernel(earlier, pairs, core_ref, *refs):
+    inputs, (same_ref, cross_ref, stat_ref, bias_ref) = refs[: 2 * pairs], refs[2 * pairs :]
     step = pl.program_id(0)
     core = core_ref[0]
     parts = STRIDE // BLOCK
+    heads = 2 * pairs
 
     @pl.when(step == 0)
     def _():
@@ -133,47 +141,63 @@
     def columns(head):
         return slice(head * HEAD, (head + 1) * HEAD)
 
-    def start(part, head):
-        query = q_ref[part * BLOCK : (part + 1) * BLOCK, columns(head)]
-        return score_blocks(query, k_ref, columns(head), spans(part))
-
-    def finish(part, head, scores):
-        values = [vt_ref[columns(head), low:high] for low, high in spans(part)]
-        out, top, total = softmax_out(scores, [bias_ref[...], None], values)
-        return out.astype(jnp.bfloat16), top, total
-
-    jobs = [(part, head) for part in range(parts) for head in range(2)]
-    results = pipelined(jobs, ahead, start, finish)
-    for head in range(2):
-        stats = [
-            jnp.concatenate(
-                split3(results[part, head][1])
-                + split3(results[part, head][2])
-                + [jnp.zeros((2, BLOCK), jnp.float32)],
+    def attend(pair):
+        q_ref, kv_ref = inputs[2 * pair : 2 * pair + 2]
+
+        def values_t(head, low, high):
+            blocks = [
+                kv_ref[STRIDE + at + head * HEAD : STRIDE + at + (head + 1) * HEAD, :]
+                for at in range(low, high, BLOCK)
+            ]
+            return jnp.concatenate(blocks, axis=1)
+
+        def start(part, head):
+            query = q_ref[part * BLOCK : (part + 1) * BLOCK, columns(head)]
+            return score_blocks(query, kv_ref, columns(head), spans(part))
+
+        def finish(part, head, scores):
+            values = [values_t(head, low, high) for low, high in spans(part)]
+            out, top, total = softmax_out(scores, [bias_ref[...], None], values)
+            return out.astype(jnp.bfloat16), top, total
+
+        jobs = [(part, head) for part in range(parts) for head in range(2)]
+        results = pipelined(jobs, 2 if earlier else 4, start, finish)
+        for head in range(2):
+            stats = [
+                jnp.concatenate(
+                    split3(results[part, head][1])
+                    + split3(results[part, head][2])
+                    + [jnp.zeros((2, BLOCK), jnp.float32)],
+                    axis=0,
+                )
+                for part in range(parts)
+            ]
+            stat_ref[2 * pair + head] = jnp.concatenate(stats, axis=1)
+        rows = slice(pair * 2 * HEAD, (pair + 1) * 2 * HEAD)
+        for half in range(2):
+            piece = jnp.concatenate(
+                [
+                    jnp.concatenate([results[2 * half + i, head][0] for i in range(2)], axis=1)
+                    for head in range(2)
+                ],
                 axis=0,
             )
-            for part in range(parts)
-        ]
-        stat_ref[step * 2 + head] = jnp.concatenate(stats, axis=1)
-    rows = pl.ds(pl.multiple_of(step * 2 * HEAD, 2 * HEAD), 2 * HEAD)
-    for half in range(2):
-        piece = jnp.concatenate(
-            [
-                jnp.concatenate([results[2 * half + part, head][0] for part in range(2)], axis=1)
-                for head in range(2)
-            ],
-            axis=0,
-        )
-
-        @pl.when(core == half)
+
+            @pl.when(core == half)
+            def _():
+                same_ref[rows, :] = piece
+
+            @pl.when(core != half)
+            def _():
+                cross_ref[rows, :] = piece
+
+    for pair in range(pairs):
+
+        @pl.when(step == pair)
         def _():
-            same_ref[rows, :] = piece
-
-        @pl.when(core != half)
-        def _():
-            cross_ref[rows, :] = piece
-
-    @pl.when(step == heads // 2 - 1)
+            attend(pair)
+
+    @pl.when(step == pairs - 1)
     def _():
         stats = jnp.concatenate([stat_ref[h] for h in range(heads)], axis=0).astype(jnp.bfloat16)
         for half in range(2):
@@ -188,31 +212,27 @@
                 cross_ref[heads * HEAD :, :] = piece
 
 
-def band_part(earlier, core, query, keys, values_t, first=0):
-    heads = query.shape[1] // HEAD
-    payload = heads * (HEAD + 8)
-    whole = pl.BlockSpec((payload, HALF), lambda h, c: (0, 0))
+def band_part(earlier, core, *inputs, estimate):
+    pairs = len(inputs) // 2
+    payload = 2 * pairs * (HEAD + 8)
+    whole = lambda shape: pl.BlockSpec(shape, lambda j, c: (0, 0))
     return pl.pallas_call(
-        functools.partial(band_kernel, earlier, heads, 2 if earlier else 4),
+        functools.partial(band_kernel, earlier, pairs),
         grid_spec=pltpu.PrefetchScalarGridSpec(
             num_scalar_prefetch=1,
-            grid=(heads // 2,),
-            in_specs=[
-                pl.BlockSpec((STRIDE, 2 * HEAD), lambda h, c: (0, h)),
-                pl.BlockSpec((STRIDE, 2 * HEAD), lambda h, c: (0, first + h)),
-                pl.BlockSpec((2 * HEAD, STRIDE), lambda h, c: (first + h, 0)),
-            ],
-            out_specs=[whole, whole],
+            grid=(pairs,),
+            in_specs=[whole(value.shape) for value in inputs],
+            out_specs=[whole((payload, HALF))] * 2,
             scratch_shapes=[
-                pltpu.VMEM((heads, 8, STRIDE), jnp.float32),
+                pltpu.VMEM((2 * pairs, 8, STRIDE), jnp.float32),
                 pltpu.VMEM((BLOCK, BLOCK), jnp.float32),
             ],
         ),
         out_shape=[jax.ShapeDtypeStruct((payload, HALF), jnp.bfloat16)] * 2,
         compiler_params=params(),
-        cost_estimate=cost(20 if earlier else 0.2),
+        cost_estimate=cost(estimate),
         name="band_earlier" if earlier else "band_local",
-    )(core, query, keys, values_t)
+    )(core, *inputs)
 
 
 def column_kernel(group, q_ref, k_ref, v_ref, o_ref, bias_ref):
@@ -266,17 +286,20 @@
     )(projected, projected, projected)
 
 
-def merge_kernel(flags_ref, local_same, local_cross, earlier_same, earlier_cross, o_ref):
+def merge_kernel(
+    flags_ref, local_same, local_cross, same_a, same_b, cross_a, cross_b, o_ref
+):
     has_earlier = flags_ref[1] > 0
 
-    def stats(ref, head):
-        rows = ref[HALF:, :].astype(jnp.float32)[8 * head : 8 * head + 8]
+    def stats(ref, heads, head):
+        rows = ref[heads * HEAD :, :].astype(jnp.float32)[8 * head : 8 * head + 8]
         return rows[0:1] + rows[1:2] + rows[2:3], rows[3:4] + rows[4:5] + rows[5:6]
 
-    def merge(local_ref, earlier_ref):
+    def merge(local_ref, earlier_refs):
         for head in range(4):
-            top_l, sum_l = stats(local_ref, head)
-            top_e, sum_e = stats(earlier_ref, head)
+            earlier_ref, index = earlier_refs[head // 2], head % 2
+            top_l, sum_l = stats(local_ref, 4, head)
+            top_e, sum_e = stats(earlier_ref, 2, index)
             top_e = jnp.where(has_earlier, top_e, NEG)
             top = jnp.maximum(top_l, top_e)
             weight_l = jnp.exp2((top_l - top) * SCALE2) * sum_l
@@ -285,17 +308,17 @@
             inverse = 1.0 / (weight_l + weight_e)
             columns = slice(head * HEAD, (head + 1) * HEAD)
             out_l = local_ref[columns, :].astype(jnp.float32)
-            out_e = earlier_ref[columns, :].astype(jnp.float32)
+            out_e = earlier_ref[index * HEAD : (index + 1) * HEAD, :].astype(jnp.float32)
             out = out_l * (weight_l * inverse) + out_e * (weight_e * inverse)
             o_ref[:, columns] = out.T.astype(jnp.bfloat16)
 
     @pl.when(pl.program_id(0) == 0)
     def _():
-        merge(local_same, earlier_same)
+        merge(local_same, (same_a, same_b))
 
     @pl.when(pl.program_id(0) == 1)
     def _():
-        merge(local_cross, earlier_cross)
+        merge(local_cross, (cross_a, cross_b))
 
 
 def merge_band(flags, *payloads):
@@ -312,7 +335,7 @@
         ),
         out_shape=jax.ShapeDtypeStruct((HALF, 2 * HEADS * HEAD), jnp.bfloat16),
         compiler_params=params(),
-        cost_estimate=cost(60),
+        cost_estimate=cost(MERGE_COST),
         name="merge_band",
     )(flags, *payloads)
 
@@ -368,30 +391,33 @@
     def swapped(value):
         return lax.ppermute(value, "seq", [(d, d ^ 1) for d in range(count)])
 
-    def to_previous(value):
-        return lax.ppermute(value, "seq", [(d, d - 2) for d in range(2, count)])
-
-    def to_next(same, cross):
-        same = lax.ppermute(same, "seq", [(d, d + 2) for d in range(count - 2)])
-        cross = lax.ppermute(cross, "seq", [(d, (d + 2) ^ 1) for d in range(count - 2)])
-        return same, cross
+    def to_next(value):
+        return lax.ppermute(value, "seq", [(d, d + 2) for d in range(count - 2)])
 
     w_row = in_hbm(w_row)
+    columns = exchange(tokens)
     sibling = swapped(tokens)
-    query, keys, values_t = project((0, 1, 2), True, core_arr, tokens, w_row)
-    query, keys, values_t = in_hbm(query), in_hbm(keys), in_hbm(values_t)
-    (query,) = project((0,), False, core_arr, sibling, w_row, (query,))
-    next_query = to_previous(query)
-    columns = exchange(after(tokens, query))
-    keys, values_t = project((1, 2), False, core_arr, sibling, w_row, (keys, values_t))
-    query, keys, values_t = in_hbm(query), in_hbm(keys), in_hbm(values_t)
-    local_same, local_cross = band_part(False, core_arr, query, keys, values_t)
-    earlier = band_part(True, core_arr, after(next_query, local_same), keys, values_t)
-    same, cross = to_next(*earlier)
-    columns = after(columns, earlier[0])
+    kv_a, kv_b, q_a, q_b = project(core_arr, tokens, sibling, w_row)
+    previous_kv_a = to_next(kv_a)
+    next_q_b = lax.ppermute(q_b, "seq", [(d, d - 2) for d in range(2, count)])
+    local_same, local_cross = band_part(
+        False, core_arr, q_a, kv_a, q_b, kv_b, estimate=LOCAL_COST
+    )
+    sent_same, sent_cross = band_part(
+        True, core_arr, after(next_q_b, local_same), kv_b, estimate=B_COST
+    )
+    same_b = to_next(sent_same)
+    cross_b = lax.ppermute(sent_cross, "seq", [(d, (d + 2) ^ 1) for d in range(count - 2)])
+    columns = after(columns, sent_same)
     col_proj = jnp.dot(columns, w_column, preferred_element_type=jnp.float32).astype(jnp.bfloat16)
-    col_out = exchange(column_attention(col_proj, group))
-    band_out = merge_band(flags, local_same, swapped(local_cross), same, cross)
+    col_out = column_attention(col_proj, group)
+    same_a, cross_a = band_part(
+        True, core_arr, q_a, after(previous_kv_a, col_out, same_b, cross_b), estimate=A_COST
+    )
+    col_out = exchange(col_out)
+    band_out = merge_band(
+        flags, local_same, swapped(local_cross), same_a, same_b, swapped(cross_a), cross_b
+    )
     return place_columns(band_out, col_out)
 
 

time: 135 us -> 106 us (0.79)
  waiting for transfers between devices: 35.9 us -> 24.7 us
  Pallas kernels: 43.5 us -> 34.6 us
  starting transfers between devices: 41.9 us -> 34.6 us
  local copies, waits for them, and re-layouts: 2.56 us -> 1.07 us
    all_to_all x2, starting transfers between devices: 34.1 us -> 21.4 us  [exchange(): lax.all_to_all(value.reshape(chips, group, width), 'seq', split_axis=0, c...]
    pallas_call x5 -> x4, Pallas kernels: 31.8 us -> 23 us  [the longest x3 12.9 us: band_part(): pl.pallas_call(functools.partial(band_kernel, earlier, pairs), grid_spec=...]
    ppermute x3 -> x4, waiting for transfers between devices: 21.5 us -> 13.9 us  [the longest x1 13.9 us: on_device(): next_q_b = lax.ppermute(q_b, 'seq', [(d, d - 2) for d in range(2, count)])]
    ppermute x3 -> x4, starting transfers between devices: 7.79 us -> 12.8 us  [the longest x2 9.12 us: to_next(): return lax.ppermute(value, 'seq', [(d, d + 2) for d in range(count - 2)])]
    all_to_all x2, waiting for transfers between devices: 14.4 us -> 9.65 us  [exchange(): lax.all_to_all(value.reshape(chips, group, width), 'seq', split_axis=0, c...]
    unnamed x8 -> x10, local copies, waits for them, and re-layouts: 2.56 us -> 1.07 us
  transfers between devices with their start and end apart: 7 -> 9, of which waited for: 2 -> 3; matrix products, arithmetic and copies ran while one was open for 8% -> 10% of each run, Pallas kernels for 28% -> 31%
where the time goes in v4:
time: 106 us; the launch traced here: 105 us
  starting transfers between devices  34.6 us (33%)
  Pallas kernels  34.6 us (33%)
  waiting for transfers between devices  24.7 us (23%)
  matrix products  10.3 us (10%)
  local copies, waits for them, and re-layouts  1.07 us (1%)
    all_to_all x2, starting transfers between devices, exchange(): lax.all_to_all(value.reshape(chips, group, width), 'seq', split_axis=0, c...  21.4 us
    ppermute x1, waiting for transfers between devices, on_device(): next_q_b = lax.ppermute(q_b, 'seq', [(d, d - 2) for d in range(2, count)])  13.9 us
    pallas_call x3, Pallas kernels, band_part(): pl.pallas_call(functools.partial(band_kernel, earlier, pairs), grid_spec=...  12.9 us
    dot_general x1, matrix products, on_device(): jnp.dot(columns, w_column, preferred_element_type=jnp.float32)  10.3 us
    pallas_call x1, Pallas kernels, project(): pl.pallas_call(project_kernel, grid_spec=pltpu.PrefetchScalarGridSpec(num...  10.1 us
    all_to_all x2, waiting for transfers between devices, exchange(): lax.all_to_all(value.reshape(chips, group, width), 'seq', split_axis=0, c...  9.65 us
    ppermute x2, starting transfers between devices, to_next(): return lax.ppermute(value, 'seq', [(d, d + 2) for d in range(count - 2)])  9.12 us
    pallas_call x1, Pallas kernels, column_attention(): pl.pallas_call(functools.partial(column_kernel, group), grid=(steps,), in...  6.88 us
  transfers between devices with their start and end apart: 9, of which 3 were waited for; matrix products, arithmetic and copies ran while one was open for 10% of the time, Pallas kernels for 31%

profile of v4, /device:TPU:0, one launch (start us, length us, event | category | flops | bytes accessed | tf_op | source)
XLA Modules:
  0.0 105.5 jit_solution(15491839710229337007)
XLA Ops:
  0.0 0.0 copy-start
  0.0 0.0 collective-permute-start
  0.0 11.9 %all-to-all-start = ((bf16[64,8,2048]{2,1,0:T(8,128)(2,1)}), bf16[64,8,2048]{2,1,0:T(8,128)(2,1)}, u32[]{:S(2)}, u32[]{:S(2)}) async-start(bf16[64,8,2048]{2,1,0:T(8,128)(2,1)} %bitcast.8), calls=%async_computation | async-start | bytes 4194304 | tf_op jit(solution)/shard_map/all_to_all | solution.py:385
  11.9 0.0 collective-permute-done.sibling_ref
  11.9 0.0 copy-done
  12.0 10.1 %project.1 = (bf16[2048,256]{1,0:T(8,128)(2,1)S(1)}, bf16[2048,256]{1,0:T(8,128)(2,1)S(1)}, bf16[1024,256]{1,0:T(8,128)(2,1)S(1)}, bf16[1024,256]{1,0:T(8,128)(2,1)S(1)}) custom-call(s32[1]{0:T(128)} %bitcast.2.core_ref, bf16[512,2048]{1,0:T(8,128)(2,1)S(1)} %copy-done, bf16[512,2048]{1,0:T(8,128)(2,1)} %collective-permute-done.sibling_ref, ...), custom_call_target="tpu_custom_call" | custom-call | flops 500000000 | bytes 16384 | tf_op jit(solution)/shard_map/project/pallas_call | solution.py:62
  22.0 0.0 copy-start.1
  22.0 1.3 %collective-permute-start.1 = (bf16[1024,256]{1,0:T(8,128)(2,1)S(1)}, bf16[1024,256]{1,0:T(8,128)(2,1)S(1)}, u32[]{:S(2)}, u32[]{:S(2)}) collective-permute-start(bf16[1024,256]{1,0:T(8,128)(2,1)S(1)} %get-tuple-element.18.refs_2_), channel_id=1, source_target_pairs={{2,0},{3,1},{4,2},{5,3},{6,4},{7,5},{8,6},{9,7},{10,8},{11,9},{12,... | collective-permute-start | bytes 1572872 | tf_op jit(solution)/shard_map/ppermute | solution.py:402
  23.3 5.5 %collective-permute-start.3 = (bf16[2048,256]{1,0:T(8,128)(2,1)S(1)}, bf16[2048,256]{1,0:T(8,128)(2,1)}, u32[]{:S(2)}, u32[]{:S(2)}) collective-permute-start(bf16[2048,256]{1,0:T(8,128)(2,1)S(1)} %get-tuple-element.20.refs_1_), channel_id=1, source_target_pairs={{0,2},{1,3},{2,4},{3,5},{4,6},{5,7},{6,8},{7,9},{8,10},{9,11},{10,... | collective-permute-start | bytes 3145736 | tf_op jit(solution)/shard_map/ppermute | solution.py:395
  28.9 6.1 %band_local.1 = (bf16[544,512]{1,0:T(8,128)(2,1)S(1)}, bf16[544,512]{1,0:T(8,128)(2,1)}) custom-call(s32[1]{0:T(128)} %bitcast.2.core_ref, bf16[1024,256]{1,0:T(8,128)(2,1)S(1)} %get-tuple-element.19.refs_0_, bf16[2048,256]{1,0:T(8,128)(2,1)S(1)} %get-tuple-element.20.refs_1_, bf16[1024,256]{1,0:T(8,128)(2,1)S(1)} %get-tuple-element.18.refs_2_, ...), custom_call_target="tpu_custom_call" | custom-call | flops 500000000 | bytes 16384 | tf_op jit(solution)/shard_map/band_local/pallas_call | solution.py:219
  35.0 0.0 copy-start.3
  35.0 0.0 collective-permute-start.2
  35.0 13.9 %collective-permute-done.1.refs_0_ = bf16[1024,256]{1,0:T(8,128)(2,1)S(1)} collective-permute-done((bf16[1024,256]{1,0:T(8,128)(2,1)S(1)}, bf16[1024,256]{1,0:T(8,128)(2,1)S(1)}, u32[]{:S(2)}, u32[]{:S(2)}) %collective-permute-start.1) | collective-permute-done | bytes 524320 | tf_op jit(solution)/shard_map/ppermute | solution.py:402
  48.9 3.2 %band_earlier.2 = (bf16[272,512]{1,0:T(8,128)(2,1)}, bf16[272,512]{1,0:T(8,128)(2,1)}) custom-call(s32[1]{0:T(128)} %bitcast.2.core_ref, bf16[1024,256]{1,0:T(8,128)(2,1)S(1)} %collective-permute-done.1.refs_0_, bf16[2048,256]{1,0:T(8,128)(2,1)S(1)} %get-tuple-element.21.refs_3_.refs_1_), custom_call_target="tpu_custom_call" | custom-call | flops 500000000 | bytes 16384 | tf_op jit(solution)/shard_map/band_earlier/pallas_call | solution.py:219
  52.1 0.0 copy-done.1
  52.1 0.0 copy-done.3
  52.1 3.6 %collective-permute-start.4 = (bf16[272,512]{1,0:T(8,128)(2,1)}, bf16[272,512]{1,0:T(8,128)(2,1)S(1)}, u32[]{:S(2)}, u32[]{:S(2)}) collective-permute-start(bf16[272,512]{1,0:T(8,128)(2,1)} %get-tuple-element.24), channel_id=1, source_target_pairs={{0,2},{1,3},{2,4},{3,5},{4,6},{5,7},{6,8},{7,9},{8,10},{9,11},{10,... | collective-permute-start | bytes 835592 | tf_op jit(solution)/shard_map/ppermute | solution.py:395
  55.7 0.0 all-to-all-done
  55.7 2.3 %collective-permute-start.5 = (bf16[272,512]{1,0:T(8,128)(2,1)}, bf16[272,512]{1,0:T(8,128)(2,1)S(1)}, u32[]{:S(2)}, u32[]{:S(2)}) collective-permute-start(bf16[272,512]{1,0:T(8,128)(2,1)} %get-tuple-element.27), channel_id=1, source_target_pairs={{0,3},{1,2},{2,5},{3,4},{4,7},{5,6},{6,9},{7,8},{8,11},{9,10},{10,... | collective-permute-start | bytes 835592 | tf_op jit(solution)/shard_map/ppermute | solution.py:410
  58.1 10.3 %convolution_convert_fusion.q_ref.k_ref.v_ref = bf16[512,3072]{1,0:T(8,128)(2,1)S(1)} fusion(bf16[512,2048]{1,0:T(8,128)(2,1)} %bitcast.1, bf16[2048,3072]{1,0:T(8,128)(2,1)} %param.5), kind=kOutput, calls=%fused_computation | convolution fusion | flops 6444023808 | bytes 17825792 | tf_op jit(solution)/shard_map/dot_general | solution.py:412
  68.4 0.0 copy-start.2
  68.4 6.9 %column_attention.1 = bf16[512,1024]{1,0:T(8,128)(2,1)} custom-call(bf16[512,3072]{1,0:T(8,128)(2,1)S(1)} %convolution_convert_fusion.q_ref.k_ref.v_ref, bf16[512,3072]{1,0:T(8,128)(2,1)S(1)} %convolution_convert_fusion.q_ref.k_ref.v_ref, bf16[512,3072]{1,0:T(8,128)(2,1)S(1)} %convolution_convert_fusion.q_ref.k_ref.v_ref), custom_call_target="tpu_custom_call" | custom-call | flops 6000000000 | bytes 16384 | tf_op jit(solution)/shard_map/column_attention/pallas_call | solution.py:276
  75.3 9.5 %all-to-all-start.1 = ((bf16[64,8,1024]{2,1,0:T(8,128)(2,1)}), bf16[64,8,1024]{2,1,0:T(8,128)(2,1)S(1)}, u32[]{:S(2)}, u32[]{:S(2)}) async-start(bf16[64,8,1024]{2,1,0:T(8,128)(2,1)} %bitcast.3), calls=%async_computation.1 | async-start | bytes 2097152 | tf_op jit(solution)/shard_map/all_to_all | solution.py:385
  84.8 0.0 collective-permute-done.5.cross_b
  84.8 0.0 collective-permute-done.4.same_b
  84.8 0.0 collective-permute-done.3.refs_1_
  84.8 0.0 copy-done.2
  84.8 3.6 %band_earlier.3 = (bf16[272,512]{1,0:T(8,128)(2,1)S(1)}, bf16[272,512]{1,0:T(8,128)(2,1)S(1)}) custom-call(s32[1]{0:T(128)} %bitcast.2.core_ref, bf16[1024,256]{1,0:T(8,128)(2,1)S(1)} %copy-done.2, bf16[2048,256]{1,0:T(8,128)(2,1)} %collective-permute-done.3.refs_1_), custom_call_target="tpu_custom_call" | custom-call | flops 20000000000 | bytes 16384 | tf_op jit(solution)/shard_map/band_earlier/pallas_call | solution.py:219
  88.4 0.4 collective-permute-start.6
  88.8 0.1 pad_add_fusion.flags_ref
  88.9 0.0 collective-permute-done.2.local_cross
  88.9 1.1 %collective-permute-done.6.cross_a = bf16[272,512]{1,0:T(8,128)(2,1)S(1)} collective-permute-done((bf16[272,512]{1,0:T(8,128)(2,1)S(1)}, bf16[272,512]{1,0:T(8,128)(2,1)S(1)}, u32[]{:S(2)}, u32[]{:S(2)}) %collective-permute-start.6) | collective-permute-done | bytes 278560 | tf_op jit(solution)/shard_map/ppermute | solution.py:392
  90.0 0.0 copy-start.4
  90.0 1.1 copy-done.4
  91.1 3.2 %merge_band.1._ = bf16[512,2048]{1,0:T(8,128)(2,1)} custom-call(s32[2]{0:T(128)S(1)} %pad_add_fusion.flags_ref, bf16[544,512]{1,0:T(8,128)(2,1)S(1)} %copy-done.4, bf16[544,512]{1,0:T(8,128)(2,1)} %collective-permute-done.2.local_cross, bf16[272,512]{1,0:T(8,128)(2,1)S(1)} %get-tuple-element.29.same_a, bf16[272,512]{1,0:T(8,128)(2,1)S(1)} %collective-permute-done.4.same_b, ...), custom_call_target="tpu_custom_call" | custom-call | flops 2000000000 | bytes 16384 | tf_op jit(solution)/shard_map/merge_band/pallas_call | solution.py:328
  94.3 9.7 %all-to-all-done.1 = bf16[64,8,1024]{2,1,0:T(8,128)(2,1)S(1)} async-done(((bf16[64,8,1024]{2,1,0:T(8,128)(2,1)}), bf16[64,8,1024]{2,1,0:T(8,128)(2,1)S(1)}, u32[]{:S(2)}, u32[]{:S(2)}) %all-to-all-start.1) | async-done | bytes 1048608 | tf_op jit(solution)/shard_map/all_to_all | solution.py:385
  103.9 1.5 %place_columns.1 = bf16[512,2048]{1,0:T(8,128)(2,1)} custom-call(bf16[512,1024]{1,0:T(8,128)(2,1)S(1)} %bitcast.9, bf16[512,2048]{1,0:T(8,128)(2,1)} %merge_band.1._), custom_call_target="tpu_custom_call", output_to_operand_aliasing={{}: (1, {})} | custom-call | flops 1000000000 | bytes 16384 | tf_op jit(solution)/shard_map/place_columns/pallas_call | solution.py:349
Async XLA Ops:
  0.0 12.0 %copy-start = (bf16[512,2048]{1,0:T(8,128)(2,1)S(1)}, bf16[512,2048]{1,0:T(8,128)(2,1)}, u32[]{:S(2)}) copy-start(bf16[512,2048]{1,0:T(8,128)(2,1)} %own_ref.1) | copy-start | bytes 6291460
  0.0 11.9 %collective-permute-start = (bf16[512,2048]{1,0:T(8,128)(2,1)}, bf16[512,2048]{1,0:T(8,128)(2,1)}, u32[]{:S(2)}, u32[]{:S(2)}) collective-permute-start(bf16[512,2048]{1,0:T(8,128)(2,1)} %own_ref.1), channel_id=1, source_target_pairs={{0,1},{1,0},{2,3},{3,2},{4,5},{5,4},{6,7},{7,6},{8,9},{9,8},{10,11... | collective-permute-start | bytes 6291464 | tf_op jit(solution)/shard_map/ppermute | solution.py:392
  0.0 55.7 %all-to-all-start = ((bf16[64,8,2048]{2,1,0:T(8,128)(2,1)}), bf16[64,8,2048]{2,1,0:T(8,128)(2,1)}, u32[]{:S(2)}, u32[]{:S(2)}) async-start(bf16[64,8,2048]{2,1,0:T(8,128)(2,1)} %bitcast.8), calls=%async_computation | async-start | bytes 4194304 | tf_op jit(solution)/shard_map/all_to_all | solution.py:385
  22.0 30.1 %copy-start.1 = (bf16[1024,256]{1,0:T(8,128)(2,1)}, bf16[1024,256]{1,0:T(8,128)(2,1)S(1)}, u32[]{:S(2)}) copy-start(bf16[1024,256]{1,0:T(8,128)(2,1)S(1)} %get-tuple-element.19.refs_0_) | copy-start | bytes 1572868
  22.0 26.9 %collective-permute-start.1 = (bf16[1024,256]{1,0:T(8,128)(2,1)S(1)}, bf16[1024,256]{1,0:T(8,128)(2,1)S(1)}, u32[]{:S(2)}, u32[]{:S(2)}) collective-permute-start(bf16[1024,256]{1,0:T(8,128)(2,1)S(1)} %get-tuple-element.18.refs_2_), channel_id=1, source_target_pairs={{2,0},{3,1},{4,2},{5,3},{6,4},{7,5},{8,6},{9,7},{10,8},{11,9},{12,... | collective-permute-start | bytes 1572872 | tf_op jit(solution)/shard_map/ppermute | solution.py:402
  23.3 61.4 %collective-permute-start.3 = (bf16[2048,256]{1,0:T(8,128)(2,1)S(1)}, bf16[2048,256]{1,0:T(8,128)(2,1)}, u32[]{:S(2)}, u32[]{:S(2)}) collective-permute-start(bf16[2048,256]{1,0:T(8,128)(2,1)S(1)} %get-tuple-element.20.refs_1_), channel_id=1, source_target_pairs={{0,2},{1,3},{2,4},{3,5},{4,6},{5,7},{6,8},{7,9},{8,10},{9,11},{10,... | collective-permute-start | bytes 3145736 | tf_op jit(solution)/shard_map/ppermute | solution.py:395
  35.0 17.1 %copy-start.3 = (bf16[544,512]{1,0:T(8,128)(2,1)}, bf16[544,512]{1,0:T(8,128)(2,1)S(1)}, u32[]{:S(2)}) copy-start(bf16[544,512]{1,0:T(8,128)(2,1)S(1)} %get-tuple-element.22.local_same) | copy-start | bytes 1671172
  35.0 53.9 %collective-permute-start.2 = (bf16[544,512]{1,0:T(8,128)(2,1)}, bf16[544,512]{1,0:T(8,128)(2,1)}, u32[]{:S(2)}, u32[]{:S(2)}) collective-permute-start(bf16[544,512]{1,0:T(8,128)(2,1)} %get-tuple-element.26), channel_id=1, source_target_pairs={{0,1},{1,0},{2,3},{3,2},{4,5},{5,4},{6,7},{7,6},{8,9},{9,8},{10,11... | collective-permute-start | bytes 1671176 | tf_op jit(solution)/shard_map/ppermute | solution.py:392
  52.1 32.7 %collective-permute-start.4 = (bf16[272,512]{1,0:T(8,128)(2,1)}, bf16[272,512]{1,0:T(8,128)(2,1)S(1)}, u32[]{:S(2)}, u32[]{:S(2)}) collective-permute-start(bf16[272,512]{1,0:T(8,128)(2,1)} %get-tuple-element.24), channel_id=1, source_target_pairs={{0,2},{1,3},{2,4},{3,5},{4,6},{5,7},{6,8},{7,9},{8,10},{9,11},{10,... | collective-permute-start | bytes 835592 | tf_op jit(solution)/shard_map/ppermute | solution.py:395
  55.7 29.0 %collective-permute-start.5 = (bf16[272,512]{1,0:T(8,128)(2,1)}, bf16[272,512]{1,0:T(8,128)(2,1)S(1)}, u32[]{:S(2)}, u32[]{:S(2)}) collective-permute-start(bf16[272,512]{1,0:T(8,128)(2,1)} %get-tuple-element.27), channel_id=1, source_target_pairs={{0,3},{1,2},{2,5},{3,4},{4,7},{5,6},{6,9},{7,8},{8,11},{9,10},{10,... | collective-permute-start | bytes 835592 | tf_op jit(solution)/shard_map/ppermute | solution.py:410
  68.4 16.4 %copy-start.2 = (bf16[1024,256]{1,0:T(8,128)(2,1)S(1)}, bf16[1024,256]{1,0:T(8,128)(2,1)}, u32[]{:S(2)}) copy-start(bf16[1024,256]{1,0:T(8,128)(2,1)} %copy-done.1) | copy-start | bytes 1572868
  75.3 28.7 %all-to-all-start.1 = ((bf16[64,8,1024]{2,1,0:T(8,128)(2,1)}), bf16[64,8,1024]{2,1,0:T(8,128)(2,1)S(1)}, u32[]{:S(2)}, u32[]{:S(2)}) async-start(bf16[64,8,1024]{2,1,0:T(8,128)(2,1)} %bitcast.3), calls=%async_computation.1 | async-start | bytes 2097152 | tf_op jit(solution)/shard_map/all_to_all | solution.py:385
  88.4 1.6 %collective-permute-start.6 = (bf16[272,512]{1,0:T(8,128)(2,1)S(1)}, bf16[272,512]{1,0:T(8,128)(2,1)S(1)}, u32[]{:S(2)}, u32[]{:S(2)}) collective-permute-start(bf16[272,512]{1,0:T(8,128)(2,1)S(1)} %get-tuple-element.30), channel_id=1, source_target_pairs={{0,1},{1,0},{2,3},{3,2},{4,5},{5,4},{6,7},{7,6},{8,9},{9,8},{10,11... | collective-permute-start | bytes 835592 | tf_op jit(solution)/shard_map/ppermute | solution.py:392
  90.0 1.1 copy-start.4

commit v5 on v4

v5 whole, which is shorter than its diff:
```python
import functools
import math

import jax
import jax.numpy as jnp
from jax import lax
from jax.experimental import pallas as pl
from jax.experimental.pallas import tpu as pltpu
from jax.sharding import PartitionSpec as P

HEAD = 128
HEADS = 8
STRIDE = 1024
HALF = 512
BLOCK = 256
SCALE2 = math.log2(math.e) / math.sqrt(HEAD)
NEG = -1e30
VMEM_LIMIT = 28 << 20
PROJECT_COST, LOCAL_COST, B_COST, COMPLETE_COST = 0.5, 0.5, 0.5, 20


def params():
    return pltpu.CompilerParams(vmem_limit_bytes=VMEM_LIMIT)


def cost(us):
    return pl.CostEstimate(flops=int(us * 10**9), bytes_accessed=1 << 14, transcendentals=0)


def project_kernel(core_ref, own_ref, sibling_ref, w_ref, kv_a, kv_b, q_a, q_b):
    core = core_ref[0]
    for step, (kind, ref) in enumerate(PROJECT_ORDER):
        ref = {"kv_a": kv_a, "kv_b": kv_b, "q_a": q_a, "q_b": q_b}[ref]

        @pl.when(pl.program_id(0) == step)
        def _():
            for place, x_ref in ((core, own_ref), (1 - core, sibling_ref)):
                value = jnp.dot(x_ref[...], w_ref[...], preferred_element_type=jnp.float32)
                row = pl.multiple_of(place * HALF, HALF)
                if kind == 2:
                    value = value.T.astype(jnp.bfloat16)
                    for block in range(HALF // BLOCK):
                        rows = pl.ds(STRIDE + row + block * BLOCK, BLOCK)
                        ref[rows, :] = value[:, block * BLOCK : (block + 1) * BLOCK]
                else:
                    ref[pl.ds(row, HALF), :] = value.astype(jnp.bfloat16)


PROJECT_ORDER = [(1, "kv_a"), (2, "kv_a"), (0, "q_b"), (1, "kv_b"), (2, "kv_b"), (0, "q_a")]


def project(core, tokens, sibling, w_row):
    depth = tokens.shape[1]

    def weight_block(j, c):
        kind = lax.rem(j + 1, 3)
        pair = jnp.where((j >= 2) & (j <= 4), 1, 0)
        return (0, 4 * kind + 2 * c[0] + pair)

    whole = lambda rows, width: pl.BlockSpec((rows, width), lambda j, c: (0, 0))
    outs = [(2 * STRIDE, BLOCK), (2 * STRIDE, BLOCK), (STRIDE, BLOCK), (STRIDE, BLOCK)]
    return pl.pallas_call(
        project_kernel,
        grid_spec=pltpu.PrefetchScalarGridSpec(
            num_scalar_prefetch=1,
            grid=(len(PROJECT_ORDER),),
            in_specs=[
                whole(HALF, depth),
                whole(HALF, depth),
                pl.BlockSpec((depth, BLOCK), weight_block),
            ],
            out_specs=[whole(*shape) for shape in outs],
        ),
        out_shape=[jax.ShapeDtypeStruct(shape, jnp.bfloat16) for shape in outs],
        compiler_params=params(),
        cost_estimate=cost(PROJECT_COST),
        name="project",
    )(core, tokens, sibling, w_row)


def score_blocks(query, key_ref, columns, spans):
    return [
        lax.dot_general(
            key_ref[low:high, columns], query, (((1,), (1,)), ((), ())),
            preferred_element_type=jnp.float32,
        )
        for low, high in spans
    ]


def softmax_out(scores, biases, value_t_blocks):
    scores = [s if b is None else s + b for s, b in zip(scores, biases)]
    top = functools.reduce(jnp.maximum, [jnp.max(s, axis=0, keepdims=True) for s in scores])
    expd = [jnp.exp2((s - top) * SCALE2) for s in scores]
    total = sum(jnp.sum(e, axis=0, keepdims=True) for e in expd)
    out = sum(
        jnp.dot(v, e.astype(jnp.bfloat16), preferred_element_type=jnp.float32)
        for v, e in zip(value_t_blocks, expd)
    )
    return out, top, total


def pipelined(jobs, ahead, start, finish):
    pending, results = [], {}
    for job in jobs:
        pending.append((job, start(*job)))
        if len(pending) > ahead:
            first, value = pending.pop(0)
            results[first] = finish(*first, value)
    for first, value in pending:
        results[first] = finish(*first, value)
    return results


def split3(value):
    high = value.astype(jnp.bfloat16).astype(jnp.float32)
    rest = value - high
    mid = rest.astype(jnp.bfloat16).astype(jnp.float32)
    return [high, mid, rest - mid]


def columns_of(head):
    return slice(head * HEAD, (head + 1) * HEAD)


def band_jobs(earlier, ahead, q_ref, kv_ref, bias, finish):
    def spans(part):
        low, high = part * BLOCK, (part + 1) * BLOCK
        rest = (high, STRIDE) if earlier else (0, low)
        return [(low, high)] + ([rest] if rest[0] < rest[1] else [])

    def values_t(head, low, high):
        rows = lambda at: slice(STRIDE + at + head * HEAD, STRIDE + at + (head + 1) * HEAD)
        return jnp.concatenate([kv_ref[rows(at), :] for at in range(low, high, BLOCK)], axis=1)

    def start(part, head):
        query = q_ref[part * BLOCK : (part + 1) * BLOCK, columns_of(head)]
        return score_blocks(query, kv_ref, columns_of(head), spans(part))

    def end(part, head, scores):
        values = [values_t(head, low, high) for low, high in spans(part)]
        return finish(part, head, scores, [bias, None], values)

    jobs = [(part, head) for part in range(STRIDE // BLOCK) for head in range(2)]
    return pipelined(jobs, ahead, start, end)


def band_bias(earlier):
    kpos = lax.broadcasted_iota(jnp.int32, (BLOCK, BLOCK), 0)
    qpos = lax.broadcasted_iota(jnp.int32, (BLOCK, BLOCK), 1)
    return jnp.where(kpos > qpos if earlier else kpos <= qpos, 0.0, NEG)


def band_kernel(earlier, pairs, *refs):
    inputs, (out_ref, stat_ref, bias_ref) = refs[: 2 * pairs], refs[2 * pairs :]
    step = pl.program_id(0)
    heads = 2 * pairs

    @pl.when(step == 0)
    def _():
        bias_ref[...] = band_bias(earlier)

    def attend(pair):
        def finish(part, head, scores, biases, values):
            out, top, total = softmax_out(scores, biases, values)
            queries = slice(part * BLOCK, (part + 1) * BLOCK)
            row = (2 * pair + head) * HEAD
            out = out * (1.0 / total)
            out_ref[row : row + HEAD, queries] = out.astype(jnp.bfloat16)
            stat_ref[2 * pair + head, :, queries] = jnp.concatenate(
                split3(top) + split3(total) + [jnp.zeros((2, BLOCK), jnp.float32)], axis=0
            )

        ahead = 2 if earlier else 4
        band_jobs(earlier, ahead, *inputs[2 * pair : 2 * pair + 2], bias_ref[...], finish)

    for pair in range(pairs):

        @pl.when(step == pair)
        def _():
            attend(pair)

    @pl.when(step == pairs - 1)
    def _():
        stats = jnp.concatenate([stat_ref[h] for h in range(heads)], axis=0)
        out_ref[heads * HEAD :, :] = stats.astype(jnp.bfloat16)


def band_part(earlier, *inputs, estimate):
    pairs = len(inputs) // 2
    payload = (2 * pairs * (HEAD + 8), STRIDE)
    whole = lambda shape: pl.BlockSpec(shape, lambda j: (0, 0))
    return pl.pallas_call(
        functools.partial(band_kernel, earlier, pairs),
        grid=(pairs,),
        in_specs=[whole(value.shape) for value in inputs],
        out_specs=whole(payload),
        scratch_shapes=[
            pltpu.VMEM((2 * pairs, 8, STRIDE), jnp.float32),
            pltpu.VMEM((BLOCK, BLOCK), jnp.float32),
        ],
        out_shape=jax.ShapeDtypeStruct(payload, jnp.bfloat16),
        compiler_params=params(),
        cost_estimate=cost(estimate),
        name="band_earlier" if earlier else "band_local",
    )(*inputs)


def complete_kernel(flags_ref, q_ref, kv_ref, local_ref, earlier_ref, same_ref, cross_ref, bias_ref):
    core = flags_ref[0]
    has_earlier = flags_ref[1] > 0
    bias_ref[...] = band_bias(True)

    def stats(ref, heads, head, queries):
        rows = ref[heads * HEAD :, queries].astype(jnp.float32)[8 * head : 8 * head + 8]
        return rows[0:1] + rows[1:2] + rows[2:3], rows[3:4] + rows[4:5] + rows[5:6]

    def merge(part, head, out_e, top_e, scale_e, sum_e):
        queries = slice(part * BLOCK, (part + 1) * BLOCK)
        top_l, sum_l = stats(local_ref, 4, head, queries)
        top_e = jnp.where(has_earlier, top_e, NEG)
        top = jnp.maximum(top_l, top_e)
        weight_l = jnp.exp2((top_l - top) * SCALE2) * sum_l
        weight_e = jnp.where(has_earlier, jnp.exp2((top_e - top) * SCALE2), 0.0)
        inverse = 1.0 / (weight_l + weight_e * sum_e)
        out_l = local_ref[columns_of(head), queries].astype(jnp.float32)
        out = out_l * (weight_l * inverse) + out_e * (weight_e * scale_e * inverse)
        return out.T.astype(jnp.bfloat16)

    def finish(part, head, scores, biases, values):
        out, top, total = softmax_out(scores, biases, values)
        return merge(part, head, out, top, 1.0, total)

    results = band_jobs(True, 2, q_ref, kv_ref, bias_ref[...], finish)
    for part in range(STRIDE // BLOCK):
        queries = slice(part * BLOCK, (part + 1) * BLOCK)
        for head in range(2):
            top, total = stats(earlier_ref, 2, head, queries)
            out = earlier_ref[columns_of(head), queries].astype(jnp.float32)
            results[part, 2 + head] = merge(part, 2 + head, out, top, total, total)

    def store(ref, half):
        for part in range(2):
            for head in range(4):
                rows = slice(part * BLOCK, (part + 1) * BLOCK)
                ref[rows, columns_of(head)] = results[2 * half + part, head]

    @pl.when(core == 0)
    def _():
        store(same_ref, 0)
        store(cross_ref, 1)

    @pl.when(core == 1)
    def _():
        store(same_ref, 1)
        store(cross_ref, 0)


def complete(flags, query, keyval, local, earlier):
    inputs = [query, keyval, local, earlier]
    return pl.pallas_call(
        complete_kernel,
        grid_spec=pltpu.PrefetchScalarGridSpec(
            num_scalar_prefetch=1,
            grid=(1,),
            in_specs=[pl.BlockSpec(value.shape, lambda j, c: (0, 0)) for value in inputs],
            out_specs=[
                pl.BlockSpec((HALF, HALF), lambda j, c: (0, c[0])),
                pl.BlockSpec((HALF, HALF), lambda j, c: (0, 0)),
            ],
            scratch_shapes=[pltpu.VMEM((BLOCK, BLOCK), jnp.float32)],
        ),
        out_shape=[
            jax.ShapeDtypeStruct((HALF, 2 * HEADS * HEAD), jnp.bfloat16),
            jax.ShapeDtypeStruct((HALF, HALF), jnp.bfloat16),
        ],
        compiler_params=params(),
        cost_estimate=cost(COMPLETE_COST),
        name="complete",
    )(flags, *inputs)


def place_kernel(flags_ref, cross_ref, columns_ref, _, o_ref):
    @pl.when(pl.program_id(0) == 0)
    def _():
        o_ref[...] = cross_ref[...]

    @pl.when(pl.program_id(0) > 0)
    def _():
        o_ref[...] = columns_ref[...]


def place(flags, cross, col_out, result):
    return pl.pallas_call(
        place_kernel,
        grid_spec=pltpu.PrefetchScalarGridSpec(
            num_scalar_prefetch=1,
            grid=(3,),
            in_specs=[
                pl.BlockSpec((HALF, HALF), lambda j, c: (0, 0)),
                pl.BlockSpec((HALF, HALF), lambda j, c: (0, jnp.maximum(j - 1, 0))),
                pl.BlockSpec(memory_space=pl.ANY),
            ],
            out_specs=pl.BlockSpec((HALF, HALF), lambda j, c: (0, jnp.where(j == 0, 1 - c[0], 1 + j))),
        ),
        out_shape=jax.ShapeDtypeStruct(result.shape, jnp.bfloat16),
        input_output_aliases={3: 0},
        compiler_params=params(),
        cost_estimate=cost(1),
        name="place",
    )(flags, cross, col_out, result)


def column_kernel(group, q_ref, k_ref, v_ref, o_ref, bias_ref):
    parts = HALF // BLOCK
    heads = q_ref.shape[1] // HEAD

    @pl.when(pl.program_id(0) == 0)
    def _():
        kpos = lax.broadcasted_iota(jnp.int32, (BLOCK, BLOCK), 0)
        qpos = lax.broadcasted_iota(jnp.int32, (BLOCK, BLOCK), 1)
        column = ((qpos - kpos) & (group - 1)) == 0
        bias_ref[0] = jnp.where(column, 0.0, NEG)
        bias_ref[1] = jnp.where(column & (kpos <= qpos), 0.0, NEG)

    values_t = v_ref[...].astype(jnp.float32).T.astype(jnp.bfloat16)

    def spans(part):
        return [(block * BLOCK, (block + 1) * BLOCK) for block in range(part + 1)]

    def columns(head):
        return slice(head * HEAD, (head + 1) * HEAD)

    def start(part, head):
        query = q_ref[part * BLOCK : (part + 1) * BLOCK, columns(head)]
        return score_blocks(query, k_ref, columns(head), spans(part))

    def finish(part, head, scores):
        values = [values_t[columns(head), low:high] for low, high in spans(part)]
        biases = [bias_ref[1 if block == part else 0] for block in range(part + 1)]
        out, _, total = softmax_out(scores, biases, values)
        out = out * (1.0 / total)
        o_ref[part * BLOCK : (part + 1) * BLOCK, columns(head)] = out.T.astype(jnp.bfloat16)

    pipelined([(part, head) for part in range(parts) for head in range(heads)], 2, start, finish)


def column_attention(projected, group):
    rows = projected.shape[0]
    heads = 4
    steps = HEADS // heads
    spec = lambda third: pl.BlockSpec((rows, heads * HEAD), lambda j: (0, third * steps + j))
    return pl.pallas_call(
        functools.partial(column_kernel, group),
        grid=(steps,),
        in_specs=[spec(0), spec(1), spec(2)],
        out_specs=pl.BlockSpec((rows, heads * HEAD), lambda j: (0, j)),
        out_shape=jax.ShapeDtypeStruct((rows, HEADS * HEAD), jnp.bfloat16),
        scratch_shapes=[pltpu.VMEM((2, BLOCK, BLOCK), jnp.float32)],
        compiler_params=params(),
        cost_estimate=cost(6),
        name="column_attention",
    )(projected, projected, projected)


def in_hbm(value):
    return pltpu.with_memory_space_constraint(value, pltpu.HBM)


def after(value, *others):
    return lax.optimization_barrier((value,) + others)[0]


def on_device(tokens, w_row, w_column):
    count = lax.axis_size("seq")
    chips = count // 2
    rank = lax.axis_index("seq")
    core = (rank % 2).astype(jnp.int32)
    core_arr = core.reshape(1)
    flags = jnp.stack([core, (rank >= 2).astype(jnp.int32)])
    group = HALF // chips
    same_core = [list(range(0, count, 2)), list(range(1, count, 2))]

    def exchange(value):
        width = value.shape[1]
        value = lax.all_to_all(
            value.reshape(chips, group, width), "seq", split_axis=0, concat_axis=0,
            axis_index_groups=same_core, tiled=True,
        )
        return value.reshape(HALF, width)

    def swapped(value):
        return lax.ppermute(value, "seq", [(d, d ^ 1) for d in range(count)])

    def to_next(value):
        return lax.ppermute(value, "seq", [(d, d + 2) for d in range(count - 2)])

    w_row = in_hbm(w_row)
    columns = exchange(tokens)
    sibling = swapped(tokens)
    kv_a, kv_b, q_a, q_b = project(core_arr, tokens, sibling, w_row)
    previous_kv_a = to_next(kv_a)
    next_q_b = lax.ppermute(q_b, "seq", [(d, d - 2) for d in range(2, count)])
    local = band_part(False, q_a, kv_a, q_b, kv_b, estimate=LOCAL_COST)
    columns = after(columns, local)
    col_proj = jnp.dot(columns, w_column, preferred_element_type=jnp.float32).astype(jnp.bfloat16)
    sent_b = band_part(True, after(next_q_b, col_proj), kv_b, estimate=B_COST)
    earlier_b = to_next(sent_b)
    col_out = column_attention(after(col_proj, sent_b), group)
    result, cross = complete(flags, q_a, after(previous_kv_a, col_out), local, earlier_b)
    return place(flags, swapped(cross), exchange(col_out), result)


def solution(mesh):
    in_specs = (P("seq", None), P(), P())
    out_specs = P("seq", None)
    return jax.shard_map(
        on_device, mesh=mesh, in_specs=in_specs, out_specs=out_specs, check_vma=False
    )
```

time: 106 us -> 95.9 us (0.905)
  waiting for transfers between devices: 24.7 us -> 15.3 us
  starting transfers between devices: 34.6 us -> 32.3 us
    ppermute x1, waiting for transfers between devices: 13.9 us -> 0.01 us  [on_device(): next_q_b = lax.ppermute(q_b, 'seq', [(d, d - 2) for d in range(2, count)])]
    all_to_all x2, waiting for transfers between devices: 9.65 us -> 15.3 us  [exchange(): lax.all_to_all(value.reshape(chips, group, width), 'seq', split_axis=0, c...]
    ppermute x1 -> x0, starting transfers between devices: 2.34 us -> none  [on_device(): lax.ppermute(sent_cross, 'seq', [(d, d + 2 ^ 1) for d in range(count - 2)])]
    ppermute x3 -> x2, waiting for transfers between devices: 1.15 us -> 0.01 us  [swapped(): return lax.ppermute(value, 'seq', [(d, d ^ 1) for d in range(count)])]
    pallas_call x1, Pallas kernels: 10.1 us -> 11.2 us  [project(): pl.pallas_call(project_kernel, grid_spec=pltpu.PrefetchScalarGridSpec(num...]
    pallas_call x5 -> x4, Pallas kernels: 17.6 us -> 17.6 us  [the longest x2 9.79 us: band_part(): pl.pallas_call(functools.partial(band_kernel, earlier, pairs), grid=(pair...]
  transfers between devices with their start and end apart: 9 -> 7, of which waited for: 3 -> 2; matrix products, arithmetic and copies ran while one was open for 10% -> 11% of each run, Pallas kernels for 31% -> 35%
where the time goes in v5:
time: 95.9 us; the launch traced here: 95.5 us
  Pallas kernels  35.6 us (37%)
  starting transfers between devices  32.3 us (34%)
  waiting for transfers between devices  15.3 us (16%)
  matrix products  10.3 us (11%)
  local copies, waits for them, and re-layouts  1.83 us (2%)
    all_to_all x2, starting transfers between devices, exchange(): lax.all_to_all(value.reshape(chips, group, width), 'seq', split_axis=0, c...  22.1 us
    all_to_all x2, waiting for transfers between devices, exchange(): lax.all_to_all(value.reshape(chips, group, width), 'seq', split_axis=0, c...  15.3 us
    pallas_call x1, Pallas kernels, project(): pl.pallas_call(project_kernel, grid_spec=pltpu.PrefetchScalarGridSpec(num...  11.2 us
    dot_general x1, matrix products, on_device(): jnp.dot(columns, w_column, preferred_element_type=jnp.float32)  10.3 us
    pallas_call x2, Pallas kernels, band_part(): pl.pallas_call(functools.partial(band_kernel, earlier, pairs), grid=(pair...  9.79 us
    ppermute x2, starting transfers between devices, to_next(): return lax.ppermute(value, 'seq', [(d, d + 2) for d in range(count - 2)])  9 us
    pallas_call x1, Pallas kernels, column_attention(): pl.pallas_call(functools.partial(column_kernel, group), grid=(steps,), in...  6.81 us
    pallas_call x1, Pallas kernels, complete(): pl.pallas_call(complete_kernel, grid_spec=pltpu.PrefetchScalarGridSpec(nu...  5.53 us
  transfers between devices with their start and end apart: 7, of which 2 were waited for; matrix products, arithmetic and copies ran while one was open for 11% of the time, Pallas kernels for 35%

profile of v5, /device:TPU:0, one launch (start us, length us, event | category | flops | bytes accessed | tf_op | source)
XLA Modules:
  0.0 95.5 jit_solution(15265256518677043001)
XLA Ops:
  0.0 0.0 collective-permute-start
  0.0 0.0 copy-start
  0.0 11.9 %all-to-all-start = ((bf16[64,8,2048]{2,1,0:T(8,128)(2,1)}), bf16[64,8,2048]{2,1,0:T(8,128)(2,1)}, u32[]{:S(2)}, u32[]{:S(2)}) async-start(bf16[64,8,2048]{2,1,0:T(8,128)(2,1)} %bitcast.8), calls=%async_computation | async-start | bytes 4194304 | tf_op jit(solution)/shard_map/all_to_all | solution.py:386
  11.9 0.1 pad_add_fusion.flags_ref
  12.0 0.0 collective-permute-done.sibling_ref
  12.0 0.0 copy-done
  12.0 11.2 %project.1 = (bf16[2048,256]{1,0:T(8,128)(2,1)}, bf16[2048,256]{1,0:T(8,128)(2,1)S(1)}, bf16[1024,256]{1,0:T(8,128)(2,1)S(1)}, bf16[1024,256]{1,0:T(8,128)(2,1)}) custom-call(s32[1]{0:T(128)} %bitcast.core_ref, bf16[512,2048]{1,0:T(8,128)(2,1)S(1)} %copy-done, bf16[512,2048]{1,0:T(8,128)(2,1)} %collective-permute-done.sibling_ref, bf16[2048,3072]{1,0:T(8,128)(2,1)} %w_ref.1), custom_call_target="tpu_custom_call" | custom-call | flops 500000000 | bytes 16384 | tf_op jit(solution)/shard_map/project/pallas_call | solution.py:62
  23.2 1.3 %collective-permute-start.2 = (bf16[1024,256]{1,0:T(8,128)(2,1)}, bf16[1024,256]{1,0:T(8,128)(2,1)S(1)}, u32[]{:S(2)}, u32[]{:S(2)}) collective-permute-start(bf16[1024,256]{1,0:T(8,128)(2,1)} %get-tuple-element.17.refs_2_), channel_id=1, source_target_pairs={{2,0},{3,1},{4,2},{5,3},{6,4},{7,5},{8,6},{9,7},{10,8},{11,9},{12,... | collective-permute-start | bytes 1572872 | tf_op jit(solution)/shard_map/ppermute | solution.py:403
  24.5 5.5 %collective-permute-start.1 = (bf16[2048,256]{1,0:T(8,128)(2,1)}, bf16[2048,256]{1,0:T(8,128)(2,1)}, u32[]{:S(2)}, u32[]{:S(2)}) collective-permute-start(bf16[2048,256]{1,0:T(8,128)(2,1)} %get-tuple-element.16.refs_1_), channel_id=1, source_target_pairs={{0,2},{1,3},{2,4},{3,5},{4,6},{5,7},{6,8},{7,9},{8,10},{9,11},{10,... | collective-permute-start | bytes 3145736 | tf_op jit(solution)/shard_map/ppermute | solution.py:396
  30.0 6.6 %band_local.1.local_ref = bf16[544,1024]{1,0:T(8,128)(2,1)S(1)} custom-call(bf16[1024,256]{1,0:T(8,128)(2,1)S(1)} %get-tuple-element.15.refs_0_.q_ref, bf16[2048,256]{1,0:T(8,128)(2,1)} %get-tuple-element.16.refs_1_, bf16[1024,256]{1,0:T(8,128)(2,1)} %get-tuple-element.17.refs_2_, bf16[2048,256]{1,0:T(8,128)(2,1)S(1)} %get-tuple-element.18.refs_3_.refs_1_), custom_call_target="tpu_custom_call" | custom-call | flops 500000000 | bytes 16384 | tf_op jit(solution)/shard_map/band_local/pallas_call | solution.py:193
  36.6 0.0 copy-start.1
  36.6 1.0 %copy-done.1 = bf16[544,1024]{1,0:T(8,128)(2,1)} copy-done((bf16[544,1024]{1,0:T(8,128)(2,1)}, bf16[544,1024]{1,0:T(8,128)(2,1)S(1)}, u32[]{:S(2)}) %copy-start.1) | copy-done | bytes 1114136
  37.6 0.0 copy-start.3
  37.6 0.8 copy-done.3
  38.5 3.3 %all-to-all-done = bf16[64,8,2048]{2,1,0:T(8,128)(2,1)} async-done(((bf16[64,8,2048]{2,1,0:T(8,128)(2,1)}), bf16[64,8,2048]{2,1,0:T(8,128)(2,1)}, u32[]{:S(2)}, u32[]{:S(2)}) %all-to-all-start) | async-done | bytes 2097184 | tf_op jit(solution)/shard_map/all_to_all | solution.py:386
  41.7 10.3 %convolution_convert_fusion.q_ref.k_ref.v_ref = bf16[512,3072]{1,0:T(8,128)(2,1)S(1)} fusion(bf16[512,2048]{1,0:T(8,128)(2,1)} %bitcast.3, bf16[2048,3072]{1,0:T(8,128)(2,1)} %param.5), kind=kOutput, calls=%fused_computation | convolution fusion | flops 6444023808 | bytes 17825792 | tf_op jit(solution)/shard_map/dot_general | solution.py:406
  52.0 0.0 collective-permute-done.2.refs_0_
  52.0 3.2 %band_earlier.1 = bf16[272,1024]{1,0:T(8,128)(2,1)} custom-call(bf16[1024,256]{1,0:T(8,128)(2,1)S(1)} %collective-permute-done.2.refs_0_, bf16[2048,256]{1,0:T(8,128)(2,1)S(1)} %get-tuple-element.18.refs_3_.refs_1_), custom_call_target="tpu_custom_call" | custom-call | flops 500000000 | bytes 16384 | tf_op jit(solution)/shard_map/band_earlier/pallas_call | solution.py:193
  55.2 3.5 %collective-permute-start.3 = (bf16[272,1024]{1,0:T(8,128)(2,1)}, bf16[272,1024]{1,0:T(8,128)(2,1)}, u32[]{:S(2)}, u32[]{:S(2)}) collective-permute-start(bf16[272,1024]{1,0:T(8,128)(2,1)} %band_earlier.1), channel_id=1, source_target_pairs={{0,2},{1,3},{2,4},{3,5},{4,6},{5,7},{6,8},{7,9},{8,10},{9,11},{10,... | collective-permute-start | bytes 1671176 | tf_op jit(solution)/shard_map/ppermute | solution.py:396
  58.7 6.8 %column_attention.1 = bf16[512,1024]{1,0:T(8,128)(2,1)} custom-call(bf16[512,3072]{1,0:T(8,128)(2,1)S(1)} %convolution_convert_fusion.q_ref.k_ref.v_ref, bf16[512,3072]{1,0:T(8,128)(2,1)S(1)} %convolution_convert_fusion.q_ref.k_ref.v_ref, bf16[512,3072]{1,0:T(8,128)(2,1)S(1)} %convolution_convert_fusion.q_ref.k_ref.v_ref), custom_call_target="tpu_custom_call" | custom-call | flops 6000000000 | bytes 16384 | tf_op jit(solution)/shard_map/column_attention/pallas_call | solution.py:353
  65.5 0.0 copy-start.2
  65.5 0.0 copy-start.4
  65.5 10.2 %all-to-all-start.1 = ((bf16[64,8,1024]{2,1,0:T(8,128)(2,1)}), bf16[64,8,1024]{2,1,0:T(8,128)(2,1)S(1)}, u32[]{:S(2)}, u32[]{:S(2)}) async-start(bf16[64,8,1024]{2,1,0:T(8,128)(2,1)} %bitcast.4), calls=%async_computation.1 | async-start | bytes 2097152 | tf_op jit(solution)/shard_map/all_to_all | solution.py:386
  75.7 0.0 collective-permute-done.1.kv_ref
  75.7 0.0 collective-permute-done.3.earlier_ref
  75.7 0.0 copy-done.2
  75.7 0.0 copy-done.4
  75.7 5.5 %complete.1 = (bf16[512,2048]{1,0:T(8,128)(2,1)}, bf16[512,512]{1,0:T(8,128)(2,1)}) custom-call(s32[2]{0:T(128)S(1)} %pad_add_fusion.flags_ref, bf16[1024,256]{1,0:T(8,128)(2,1)S(1)} %copy-done.4, bf16[2048,256]{1,0:T(8,128)(2,1)} %collective-permute-done.1.kv_ref, bf16[544,1024]{1,0:T(8,128)(2,1)S(1)} %copy-done.2, ...), custom_call_target="tpu_custom_call" | custom-call | flops 20000000000 | bytes 16384 | tf_op jit(solution)/shard_map/complete/pallas_call | solution.py:261
  81.2 0.0 collective-permute-start.4
  81.2 12.0 %all-to-all-done.1 = bf16[64,8,1024]{2,1,0:T(8,128)(2,1)S(1)} async-done(((bf16[64,8,1024]{2,1,0:T(8,128)(2,1)}), bf16[64,8,1024]{2,1,0:T(8,128)(2,1)S(1)}, u32[]{:S(2)}, u32[]{:S(2)}) %all-to-all-start.1) | async-done | bytes 1048608 | tf_op jit(solution)/shard_map/all_to_all | solution.py:386
  93.2 0.0 collective-permute-done.4.cross_ref
  93.2 2.3 %place.1 = bf16[512,2048]{1,0:T(8,128)(2,1)} custom-call(s32[2]{0:T(128)S(1)} %pad_add_fusion.flags_ref, bf16[512,512]{1,0:T(8,128)(2,1)S(1)} %collective-permute-done.4.cross_ref, bf16[512,1024]{1,0:T(8,128)(2,1)S(1)} %bitcast.9, bf16[512,2048]{1,0:T(8,128)(2,1)} %get-tuple-element.24._), custom_call_target="tpu_custom_call", output_to_operand_aliasing={{}: (3, {})} | custom-call | flops 1000000000 | bytes 16384 | tf_op jit(solution)/shard_map/place/pallas_call | solution.py:294
Async XLA Ops:
  0.0 12.0 %collective-permute-start = (bf16[512,2048]{1,0:T(8,128)(2,1)}, bf16[512,2048]{1,0:T(8,128)(2,1)}, u32[]{:S(2)}, u32[]{:S(2)}) collective-permute-start(bf16[512,2048]{1,0:T(8,128)(2,1)} %own_ref.1), channel_id=1, source_target_pairs={{0,1},{1,0},{2,3},{3,2},{4,5},{5,4},{6,7},{7,6},{8,9},{9,8},{10,11... | collective-permute-start | bytes 6291464 | tf_op jit(solution)/shard_map/ppermute | solution.py:393
  0.0 12.0 %copy-start = (bf16[512,2048]{1,0:T(8,128)(2,1)S(1)}, bf16[512,2048]{1,0:T(8,128)(2,1)}, u32[]{:S(2)}) copy-start(bf16[512,2048]{1,0:T(8,128)(2,1)} %own_ref.1) | copy-start | bytes 6291460
  0.0 41.7 %all-to-all-start = ((bf16[64,8,2048]{2,1,0:T(8,128)(2,1)}), bf16[64,8,2048]{2,1,0:T(8,128)(2,1)}, u32[]{:S(2)}, u32[]{:S(2)}) async-start(bf16[64,8,2048]{2,1,0:T(8,128)(2,1)} %bitcast.8), calls=%async_computation | async-start | bytes 4194304 | tf_op jit(solution)/shard_map/all_to_all | solution.py:386
  23.2 28.8 %collective-permute-start.2 = (bf16[1024,256]{1,0:T(8,128)(2,1)}, bf16[1024,256]{1,0:T(8,128)(2,1)S(1)}, u32[]{:S(2)}, u32[]{:S(2)}) collective-permute-start(bf16[1024,256]{1,0:T(8,128)(2,1)} %get-tuple-element.17.refs_2_), channel_id=1, source_target_pairs={{2,0},{3,1},{4,2},{5,3},{6,4},{7,5},{8,6},{9,7},{10,8},{11,9},{12,... | collective-permute-start | bytes 1572872 | tf_op jit(solution)/shard_map/ppermute | solution.py:403
  24.5 51.2 %collective-permute-start.1 = (bf16[2048,256]{1,0:T(8,128)(2,1)}, bf16[2048,256]{1,0:T(8,128)(2,1)}, u32[]{:S(2)}, u32[]{:S(2)}) collective-permute-start(bf16[2048,256]{1,0:T(8,128)(2,1)} %get-tuple-element.16.refs_1_), channel_id=1, source_target_pairs={{0,2},{1,3},{2,4},{3,5},{4,6},{5,7},{6,8},{7,9},{8,10},{9,11},{10,... | collective-permute-start | bytes 3145736 | tf_op jit(solution)/shard_map/ppermute | solution.py:396
  36.6 1.0 %copy-start.1 = (bf16[544,1024]{1,0:T(8,128)(2,1)}, bf16[544,1024]{1,0:T(8,128)(2,1)S(1)}, u32[]{:S(2)}) copy-start(bf16[544,1024]{1,0:T(8,128)(2,1)S(1)} %band_local.1.local_ref) | copy-start | bytes 3342340
  37.6 0.8 copy-start.3
  55.2 20.5 %collective-permute-start.3 = (bf16[272,1024]{1,0:T(8,128)(2,1)}, bf16[272,1024]{1,0:T(8,128)(2,1)}, u32[]{:S(2)}, u32[]{:S(2)}) collective-permute-start(bf16[272,1024]{1,0:T(8,128)(2,1)} %band_earlier.1), channel_id=1, source_target_pairs={{0,2},{1,3},{2,4},{3,5},{4,6},{5,7},{6,8},{7,9},{8,10},{9,11},{10,... | collective-permute-start | bytes 1671176 | tf_op jit(solution)/shard_map/ppermute | solution.py:396
  65.5 10.2 %copy-start.2 = (bf16[544,1024]{1,0:T(8,128)(2,1)S(1)}, bf16[544,1024]{1,0:T(8,128)(2,1)}, u32[]{:S(2)}) copy-start(bf16[544,1024]{1,0:T(8,128)(2,1)} %copy-done.1) | copy-start | bytes 3342340
  65.5 10.2 %copy-start.4 = (bf16[1024,256]{1,0:T(8,128)(2,1)S(1)}, bf16[1024,256]{1,0:T(8,128)(2,1)}, u32[]{:S(2)}) copy-start(bf16[1024,256]{1,0:T(8,128)(2,1)} %copy-done.3) | copy-start | bytes 1572868
  65.5 27.7 %all-to-all-start.1 = ((bf16[64,8,1024]{2,1,0:T(8,128)(2,1)}), bf16[64,8,1024]{2,1,0:T(8,128)(2,1)S(1)}, u32[]{:S(2)}, u32[]{:S(2)}) async-start(bf16[64,8,1024]{2,1,0:T(8,128)(2,1)} %bitcast.4), calls=%async_computation.1 | async-start | bytes 2097152 | tf_op jit(solution)/shard_map/all_to_all | solution.py:386
  81.2 12.0 %collective-permute-start.4 = (bf16[512,512]{1,0:T(8,128)(2,1)}, bf16[512,512]{1,0:T(8,128)(2,1)S(1)}, u32[]{:S(2)}, u32[]{:S(2)}) collective-permute-start(bf16[512,512]{1,0:T(8,128)(2,1)} %get-tuple-element.23), channel_id=1, source_target_pairs={{0,1},{1,0},{2,3},{3,2},{4,5},{5,4},{6,7},{7,6},{8,9},{9,8},{10,11... | collective-permute-start | bytes 1572872 | tf_op jit(solution)/shard_map/ppermute | solution.py:393

commit v6 on v5

--- a/solution.py
+++ b/solution.py
@@ -71,7 +71,7 @@
             ],
             out_specs=[whole(*shape) for shape in outs],
         ),
-        out_shape=[jax.ShapeDtypeStruct(shape, jnp.bfloat16) for shape in outs],
+        out_shape=[pltpu.HBM(shape, jnp.bfloat16) for shape in outs],
         compiler_params=params(),
         cost_estimate=cost(PROJECT_COST),
         name="project",
@@ -199,7 +199,7 @@
             pltpu.VMEM((2 * pairs, 8, STRIDE), jnp.float32),
             pltpu.VMEM((BLOCK, BLOCK), jnp.float32),
         ],
-        out_shape=jax.ShapeDtypeStruct(payload, jnp.bfloat16),
+        out_shape=pltpu.HBM(payload, jnp.bfloat16),
         compiler_params=params(),
         cost_estimate=cost(estimate),
         name="band_earlier" if earlier else "band_local",
@@ -280,28 +280,29 @@
     )(flags, *inputs)
 
 
-def place_kernel(flags_ref, cross_ref, columns_ref, _, o_ref):
-    @pl.when(pl.program_id(0) == 0)
-    def _():
-        o_ref[...] = cross_ref[...]
-
-    @pl.when(pl.program_id(0) > 0)
-    def _():
-        o_ref[...] = columns_ref[...]
+def place_kernel(flags_ref, cross_ref, columns_ref, _, o_ref, sems):
+    first = pl.multiple_of((1 - flags_ref[0]) * HALF, HALF)
+    width = columns_ref.shape[1]
+    copies = [
+        pltpu.make_async_copy(cross_ref, o_ref.at[:, pl.ds(first, HALF)], sems.at[0]),
+        pltpu.make_async_copy(columns_ref, o_ref.at[:, pl.ds(width, width)], sems.at[1]),
+    ]
+    for copy in copies:
+        copy.start()
+    for copy in copies:
+        copy.wait()
 
 
 def place(flags, cross, col_out, result):
+    anywhere = pl.BlockSpec(memory_space=pl.ANY)
     return pl.pallas_call(
         place_kernel,
         grid_spec=pltpu.PrefetchScalarGridSpec(
             num_scalar_prefetch=1,
-            grid=(3,),
-            in_specs=[
-                pl.BlockSpec((HALF, HALF), lambda j, c: (0, 0)),
-                pl.BlockSpec((HALF, HALF), lambda j, c: (0, jnp.maximum(j - 1, 0))),
-                pl.BlockSpec(memory_space=pl.ANY),
-            ],
-            out_specs=pl.BlockSpec((HALF, HALF), lambda j, c: (0, jnp.where(j == 0, 1 - c[0], 1 + j))),
+            grid=(1,),
+            in_specs=[anywhere] * 3,
+            out_specs=anywhere,
+            scratch_shapes=[pltpu.SemaphoreType.DMA((2,))],
         ),
         out_shape=jax.ShapeDtypeStruct(result.shape, jnp.bfloat16),
         input_output_aliases={3: 0},
@@ -317,32 +318,38 @@
 
     @pl.when(pl.program_id(0) == 0)
     def _():
-        kpos = lax.broadcasted_iota(jnp.int32, (BLOCK, BLOCK), 0)
-        qpos = lax.broadcasted_iota(jnp.int32, (BLOCK, BLOCK), 1)
+        qpos = lax.broadcasted_iota(jnp.int32, (BLOCK, BLOCK), 0)
+        kpos = lax.broadcasted_iota(jnp.int32, (BLOCK, BLOCK), 1)
         column = ((qpos - kpos) & (group - 1)) == 0
         bias_ref[0] = jnp.where(column, 0.0, NEG)
         bias_ref[1] = jnp.where(column & (kpos <= qpos), 0.0, NEG)
 
-    values_t = v_ref[...].astype(jnp.float32).T.astype(jnp.bfloat16)
-
-    def spans(part):
-        return [(block * BLOCK, (block + 1) * BLOCK) for block in range(part + 1)]
-
-    def columns(head):
-        return slice(head * HEAD, (head + 1) * HEAD)
+    def rows(block):
+        return slice(block * BLOCK, (block + 1) * BLOCK)
 
     def start(part, head):
-        query = q_ref[part * BLOCK : (part + 1) * BLOCK, columns(head)]
-        return score_blocks(query, k_ref, columns(head), spans(part))
+        query = q_ref[rows(part), columns_of(head)]
+        return [
+            lax.dot_general(
+                query, k_ref[rows(block), columns_of(head)], (((1,), (1,)), ((), ())),
+                preferred_element_type=jnp.float32,
+            )
+            for block in range(part + 1)
+        ]
 
     def finish(part, head, scores):
-        values = [values_t[columns(head), low:high] for low, high in spans(part)]
-        biases = [bias_ref[1 if block == part else 0] for block in range(part + 1)]
-        out, _, total = softmax_out(scores, biases, values)
-        out = out * (1.0 / total)
-        o_ref[part * BLOCK : (part + 1) * BLOCK, columns(head)] = out.T.astype(jnp.bfloat16)
-
-    pipelined([(part, head) for part in range(parts) for head in range(heads)], 2, start, finish)
+        scores = [s + bias_ref[1 if block == part else 0] for block, s in enumerate(scores)]
+        top = jnp.max(functools.reduce(jnp.maximum, scores), axis=1, keepdims=True)
+        out = 0.0
+        for block, s in enumerate(scores):
+            values = v_ref[rows(block), columns_of(head)]
+            values = jnp.concatenate([values, jnp.ones_like(values)], axis=1)
+            expd = jnp.exp2((s - top) * SCALE2).astype(jnp.bfloat16)
+            out = out + jnp.dot(expd, values, preferred_element_type=jnp.float32)
+        out = out[:, :HEAD] * (1.0 / out[:, HEAD:])
+        o_ref[rows(part), columns_of(head)] = out.astype(jnp.bfloat16)
+
+    pipelined([(part, head) for part in range(parts) for head in range(heads)], 4, start, finish)
 
 
 def column_attention(projected, group):
@@ -399,6 +406,7 @@
     columns = exchange(tokens)
     sibling = swapped(tokens)
     kv_a, kv_b, q_a, q_b = project(core_arr, tokens, sibling, w_row)
+    kv_a, kv_b, q_a, q_b = [in_hbm(value) for value in (kv_a, kv_b, q_a, q_b)]
     previous_kv_a = to_next(kv_a)
     next_q_b = lax.ppermute(q_b, "seq", [(d, d - 2) for d in range(2, count)])
     local = band_part(False, q_a, kv_a, q_b, kv_b, estimate=LOCAL_COST)
@@ -407,7 +415,7 @@
     sent_b = band_part(True, after(next_q_b, col_proj), kv_b, estimate=B_COST)
     earlier_b = to_next(sent_b)
     col_out = column_attention(after(col_proj, sent_b), group)
-    result, cross = complete(flags, q_a, after(previous_kv_a, col_out), local, earlier_b)
+    result, cross = complete(flags, q_a, after(previous_kv_a, col_out), in_hbm(local), earlier_b)
     return place(flags, swapped(cross), exchange(col_out), result)
 
 

time: 95.9 us -> 94.9 us (0.990)
    pallas_call x2, Pallas kernels: 9.79 us -> 12.6 us  [band_part(): pl.pallas_call(functools.partial(band_kernel, earlier, pairs), grid=(pair...]
    pallas_call x1, Pallas kernels: 6.81 us -> 4.05 us  [column_attention(): pl.pallas_call(functools.partial(column_kernel, group), grid=(steps,), in...]
    ppermute x2, starting transfers between devices: 9 us -> 7.49 us  [to_next(): return lax.ppermute(value, 'seq', [(d, d + 2) for d in range(count - 2)])]
  transfers between devices with their start and end apart: 7 -> 7, of which waited for: 2 -> 2; matrix products, arithmetic and copies ran while one was open for 11% -> 11% of each run, Pallas kernels for 35% -> 36%
where the time goes in v6:
time: 94.9 us; the launch traced here: 94.5 us
  Pallas kernels  35.8 us (38%)
  starting transfers between devices  31.6 us (33%)
  waiting for transfers between devices  14.7 us (15%)
  matrix products  10.3 us (11%)
  local copies, waits for them, and re-layouts  1.78 us (2%)
    all_to_all x2, starting transfers between devices, exchange(): lax.all_to_all(value.reshape(chips, group, width), 'seq', split_axis=0, c...  22.8 us
    all_to_all x2, waiting for transfers between devices, exchange(): lax.all_to_all(value.reshape(chips, group, width), 'seq', split_axis=0, c...  14.7 us
    pallas_call x2, Pallas kernels, band_part(): pl.pallas_call(functools.partial(band_kernel, earlier, pairs), grid=(pair...  12.6 us
    pallas_call x1, Pallas kernels, project(): pl.pallas_call(project_kernel, grid_spec=pltpu.PrefetchScalarGridSpec(num...  11.7 us
    dot_general x1, matrix products, on_device(): jnp.dot(columns, w_column, preferred_element_type=jnp.float32)  10.3 us
    ppermute x2, starting transfers between devices, to_next(): return lax.ppermute(value, 'seq', [(d, d + 2) for d in range(count - 2)])  7.49 us
    pallas_call x1, Pallas kernels, complete(): pl.pallas_call(complete_kernel, grid_spec=pltpu.PrefetchScalarGridSpec(nu...  5.68 us
    pallas_call x1, Pallas kernels, column_attention(): pl.pallas_call(functools.partial(column_kernel, group), grid=(steps,), in...  4.05 us
  transfers between devices with their start and end apart: 7, of which 2 were waited for; matrix products, arithmetic and copies ran while one was open for 11% of the time, Pallas kernels for 36%

profile of v6, /device:TPU:0, one launch (start us, length us, event | category | flops | bytes accessed | tf_op | source)
XLA Modules:
  0.0 94.5 jit_solution(13296449358877137684)
XLA Ops:
  0.0 0.0 collective-permute-start
  0.0 0.0 copy-start
  0.0 11.9 %all-to-all-start = ((bf16[64,8,2048]{2,1,0:T(8,128)(2,1)}), bf16[64,8,2048]{2,1,0:T(8,128)(2,1)}, u32[]{:S(2)}, u32[]{:S(2)}) async-start(bf16[64,8,2048]{2,1,0:T(8,128)(2,1)} %bitcast.8), calls=%async_computation | async-start | bytes 4194304 | tf_op jit(solution)/shard_map/all_to_all | solution.py:393
  11.9 0.1 pad_add_fusion.flags_ref
  12.0 0.0 collective-permute-done.sibling_ref
  12.0 0.0 copy-done
  12.0 11.7 %project.1 = (bf16[2048,256]{1,0:T(8,128)(2,1)}, bf16[2048,256]{1,0:T(8,128)(2,1)}, bf16[1024,256]{1,0:T(8,128)(2,1)}, bf16[1024,256]{1,0:T(8,128)(2,1)}) custom-call(s32[1]{0:T(128)} %bitcast.core_ref, bf16[512,2048]{1,0:T(8,128)(2,1)S(1)} %copy-done, bf16[512,2048]{1,0:T(8,128)(2,1)} %collective-permute-done.sibling_ref, bf16[2048,3072]{1,0:T(8,128)(2,1)} %w_ref.1), custom_call_target="tpu_custom_call" | custom-call | flops 500000000 | bytes 16384 | tf_op jit(solution)/shard_map/project/pallas_call | solution.py:62
  23.7 1.3 %collective-permute-start.2 = (bf16[1024,256]{1,0:T(8,128)(2,1)}, bf16[1024,256]{1,0:T(8,128)(2,1)S(1)}, u32[]{:S(2)}, u32[]{:S(2)}) collective-permute-start(bf16[1024,256]{1,0:T(8,128)(2,1)} %get-tuple-element.17.refs_2_), channel_id=1, source_target_pairs={{2,0},{3,1},{4,2},{5,3},{6,4},{7,5},{8,6},{9,7},{10,8},{11,9},{12,... | collective-permute-start | bytes 1572872 | tf_op jit(solution)/shard_map/ppermute | solution.py:411
  25.0 4.8 %collective-permute-start.1 = (bf16[2048,256]{1,0:T(8,128)(2,1)}, bf16[2048,256]{1,0:T(8,128)(2,1)S(1)}, u32[]{:S(2)}, u32[]{:S(2)}) collective-permute-start(bf16[2048,256]{1,0:T(8,128)(2,1)} %get-tuple-element.16.refs_1_), channel_id=1, source_target_pairs={{0,2},{1,3},{2,4},{3,5},{4,6},{5,7},{6,8},{7,9},{8,10},{9,11},{10,... | collective-permute-start | bytes 3145736 | tf_op jit(solution)/shard_map/ppermute | solution.py:403
  29.8 8.1 %band_local.1.local_ref = bf16[544,1024]{1,0:T(8,128)(2,1)} custom-call(bf16[1024,256]{1,0:T(8,128)(2,1)} %get-tuple-element.15.refs_0_.q_ref, bf16[2048,256]{1,0:T(8,128)(2,1)} %get-tuple-element.16.refs_1_, bf16[1024,256]{1,0:T(8,128)(2,1)} %get-tuple-element.17.refs_2_, bf16[2048,256]{1,0:T(8,128)(2,1)} %get-tuple-element.18.refs_3_.refs_1_), custom_call_target="tpu_custom_call" | custom-call | flops 500000000 | bytes 16384 | tf_op jit(solution)/shard_map/band_local/pallas_call | solution.py:193
  37.9 3.8 %all-to-all-done = bf16[64,8,2048]{2,1,0:T(8,128)(2,1)} async-done(((bf16[64,8,2048]{2,1,0:T(8,128)(2,1)}), bf16[64,8,2048]{2,1,0:T(8,128)(2,1)}, u32[]{:S(2)}, u32[]{:S(2)}) %all-to-all-start) | async-done | bytes 2097184 | tf_op jit(solution)/shard_map/all_to_all | solution.py:393
  41.7 10.3 %convolution_convert_fusion.q_ref.k_ref.v_ref = bf16[512,3072]{1,0:T(8,128)(2,1)S(1)} fusion(bf16[512,2048]{1,0:T(8,128)(2,1)} %bitcast.3, bf16[2048,3072]{1,0:T(8,128)(2,1)} %param.5), kind=kOutput, calls=%fused_computation | convolution fusion | flops 6444023808 | bytes 17825792 | tf_op jit(solution)/shard_map/dot_general | solution.py:414
  52.0 0.0 collective-permute-done.2.refs_0_
  52.0 0.0 copy-start.1
  52.0 0.8 copy-done.1
  52.8 4.5 %band_earlier.1 = bf16[272,1024]{1,0:T(8,128)(2,1)} custom-call(bf16[1024,256]{1,0:T(8,128)(2,1)} %copy-done.1, bf16[2048,256]{1,0:T(8,128)(2,1)} %get-tuple-element.18.refs_3_.refs_1_), custom_call_target="tpu_custom_call" | custom-call | flops 500000000 | bytes 16384 | tf_op jit(solution)/shard_map/band_earlier/pallas_call | solution.py:193
  57.3 2.7 %collective-permute-start.3 = (bf16[272,1024]{1,0:T(8,128)(2,1)}, bf16[272,1024]{1,0:T(8,128)(2,1)S(1)}, u32[]{:S(2)}, u32[]{:S(2)}) collective-permute-start(bf16[272,1024]{1,0:T(8,128)(2,1)} %band_earlier.1), channel_id=1, source_target_pairs={{0,2},{1,3},{2,4},{3,5},{4,6},{5,7},{6,8},{7,9},{8,10},{9,11},{10,... | collective-permute-start | bytes 1671176 | tf_op jit(solution)/shard_map/ppermute | solution.py:403
  60.0 4.1 %column_attention.1 = bf16[512,1024]{1,0:T(8,128)(2,1)} custom-call(bf16[512,3072]{1,0:T(8,128)(2,1)S(1)} %convolution_convert_fusion.q_ref.k_ref.v_ref, bf16[512,3072]{1,0:T(8,128)(2,1)S(1)} %convolution_convert_fusion.q_ref.k_ref.v_ref, bf16[512,3072]{1,0:T(8,128)(2,1)S(1)} %convolution_convert_fusion.q_ref.k_ref.v_ref), custom_call_target="tpu_custom_call" | custom-call | flops 6000000000 | bytes 16384 | tf_op jit(solution)/shard_map/column_attention/pallas_call | solution.py:360
  64.1 10.9 %all-to-all-start.1 = ((bf16[64,8,1024]{2,1,0:T(8,128)(2,1)}), bf16[64,8,1024]{2,1,0:T(8,128)(2,1)S(1)}, u32[]{:S(2)}, u32[]{:S(2)}) async-start(bf16[64,8,1024]{2,1,0:T(8,128)(2,1)} %bitcast.4), calls=%async_computation.1 | async-start | bytes 2097152 | tf_op jit(solution)/shard_map/all_to_all | solution.py:393
  75.0 0.0 collective-permute-done.1.kv_ref
  75.0 0.0 copy-start.2
  75.0 0.0 collective-permute-done.3.earlier_ref
  75.1 1.0 %copy-done.2 = bf16[2048,256]{1,0:T(8,128)(2,1)} copy-done((bf16[2048,256]{1,0:T(8,128)(2,1)}, bf16[2048,256]{1,0:T(8,128)(2,1)S(1)}, u32[]{:S(2)}) %copy-start.2) | copy-done | bytes 1048600
  76.0 5.7 %complete.1 = (bf16[512,2048]{1,0:T(8,128)(2,1)}, bf16[512,512]{1,0:T(8,128)(2,1)S(1)}) custom-call(s32[2]{0:T(128)S(1)} %pad_add_fusion.flags_ref, bf16[1024,256]{1,0:T(8,128)(2,1)} %get-tuple-element.15.refs_0_.q_ref, bf16[2048,256]{1,0:T(8,128)(2,1)} %copy-done.2, bf16[544,1024]{1,0:T(8,128)(2,1)} %band_local.1.local_ref, ...), custom_call_target="tpu_custom_call" | custom-call | flops 20000000000 | bytes 16384 | tf_op jit(solution)/shard_map/complete/pallas_call | solution.py:261
  81.7 0.0 collective-permute-start.4
  81.7 10.9 %all-to-all-done.1 = bf16[64,8,1024]{2,1,0:T(8,128)(2,1)S(1)} async-done(((bf16[64,8,1024]{2,1,0:T(8,128)(2,1)}), bf16[64,8,1024]{2,1,0:T(8,128)(2,1)S(1)}, u32[]{:S(2)}, u32[]{:S(2)}) %all-to-all-start.1) | async-done | bytes 1048608 | tf_op jit(solution)/shard_map/all_to_all | solution.py:393
  92.6 0.0 collective-permute-done.4.cross_ref
  92.6 1.7 %place.1 = bf16[512,2048]{1,0:T(8,128)(2,1)} custom-call(s32[2]{0:T(128)S(1)} %pad_add_fusion.flags_ref, bf16[512,512]{1,0:T(8,128)(2,1)S(1)} %collective-permute-done.4.cross_ref, bf16[512,1024]{1,0:T(8,128)(2,1)S(1)} %bitcast.9, bf16[512,2048]{1,0:T(8,128)(2,1)} %get-tuple-element.24._), custom_call_target="tpu_custom_call", output_to_operand_aliasing={{}: (3, {})} | custom-call | flops 1000000000 | bytes 16384 | tf_op jit(solution)/shard_map/place/pallas_call | solution.py:298
Async XLA Ops:
  0.0 12.0 %collective-permute-start = (bf16[512,2048]{1,0:T(8,128)(2,1)}, bf16[512,2048]{1,0:T(8,128)(2,1)}, u32[]{:S(2)}, u32[]{:S(2)}) collective-permute-start(bf16[512,2048]{1,0:T(8,128)(2,1)} %own_ref.1), channel_id=1, source_target_pairs={{0,1},{1,0},{2,3},{3,2},{4,5},{5,4},{6,7},{7,6},{8,9},{9,8},{10,11... | collective-permute-start | bytes 6291464 | tf_op jit(solution)/shard_map/ppermute | solution.py:400
  0.0 12.0 %copy-start = (bf16[512,2048]{1,0:T(8,128)(2,1)S(1)}, bf16[512,2048]{1,0:T(8,128)(2,1)}, u32[]{:S(2)}) copy-start(bf16[512,2048]{1,0:T(8,128)(2,1)} %own_ref.1) | copy-start | bytes 6291460
  0.0 41.7 %all-to-all-start = ((bf16[64,8,2048]{2,1,0:T(8,128)(2,1)}), bf16[64,8,2048]{2,1,0:T(8,128)(2,1)}, u32[]{:S(2)}, u32[]{:S(2)}) async-start(bf16[64,8,2048]{2,1,0:T(8,128)(2,1)} %bitcast.8), calls=%async_computation | async-start | bytes 4194304 | tf_op jit(solution)/shard_map/all_to_all | solution.py:393
  23.7 28.3 %collective-permute-start.2 = (bf16[1024,256]{1,0:T(8,128)(2,1)}, bf16[1024,256]{1,0:T(8,128)(2,1)S(1)}, u32[]{:S(2)}, u32[]{:S(2)}) collective-permute-start(bf16[1024,256]{1,0:T(8,128)(2,1)} %get-tuple-element.17.refs_2_), channel_id=1, source_target_pairs={{2,0},{3,1},{4,2},{5,3},{6,4},{7,5},{8,6},{9,7},{10,8},{11,9},{12,... | collective-permute-start | bytes 1572872 | tf_op jit(solution)/shard_map/ppermute | solution.py:411
  25.0 50.0 %collective-permute-start.1 = (bf16[2048,256]{1,0:T(8,128)(2,1)}, bf16[2048,256]{1,0:T(8,128)(2,1)S(1)}, u32[]{:S(2)}, u32[]{:S(2)}) collective-permute-start(bf16[2048,256]{1,0:T(8,128)(2,1)} %get-tuple-element.16.refs_1_), channel_id=1, source_target_pairs={{0,2},{1,3},{2,4},{3,5},{4,6},{5,7},{6,8},{7,9},{8,10},{9,11},{10,... | collective-permute-start | bytes 3145736 | tf_op jit(solution)/shard_map/ppermute | solution.py:403
  52.0 0.8 copy-start.1
  57.3 17.7 %collective-permute-start.3 = (bf16[272,1024]{1,0:T(8,128)(2,1)}, bf16[272,1024]{1,0:T(8,128)(2,1)S(1)}, u32[]{:S(2)}, u32[]{:S(2)}) collective-permute-start(bf16[272,1024]{1,0:T(8,128)(2,1)} %band_earlier.1), channel_id=1, source_target_pairs={{0,2},{1,3},{2,4},{3,5},{4,6},{5,7},{6,8},{7,9},{8,10},{9,11},{10,... | collective-permute-start | bytes 1671176 | tf_op jit(solution)/shard_map/ppermute | solution.py:403
  64.1 28.5 %all-to-all-start.1 = ((bf16[64,8,1024]{2,1,0:T(8,128)(2,1)}), bf16[64,8,1024]{2,1,0:T(8,128)(2,1)S(1)}, u32[]{:S(2)}, u32[]{:S(2)}) async-start(bf16[64,8,1024]{2,1,0:T(8,128)(2,1)} %bitcast.4), calls=%async_computation.1 | async-start | bytes 2097152 | tf_op jit(solution)/shard_map/all_to_all | solution.py:393
  75.0 1.0 %copy-start.2 = (bf16[2048,256]{1,0:T(8,128)(2,1)}, bf16[2048,256]{1,0:T(8,128)(2,1)S(1)}, u32[]{:S(2)}) copy-start(bf16[2048,256]{1,0:T(8,128)(2,1)S(1)} %collective-permute-done.1.kv_ref) | copy-start | bytes 3145732
  81.7 10.9 %collective-permute-start.4 = (bf16[512,512]{1,0:T(8,128)(2,1)S(1)}, bf16[512,512]{1,0:T(8,128)(2,1)S(1)}, u32[]{:S(2)}, u32[]{:S(2)}) collective-permute-start(bf16[512,512]{1,0:T(8,128)(2,1)S(1)} %get-tuple-element.23), channel_id=1, source_target_pairs={{0,1},{1,0},{2,3},{3,2},{4,5},{5,4},{6,7},{7,6},{8,9},{9,8},{10,11... | collective-permute-start | bytes 1572872 | tf_op jit(solution)/shard_map/ppermute | solution.py:400

commit v7 on v6

--- a/solution.py
+++ b/solution.py
@@ -71,7 +71,7 @@
             ],
             out_specs=[whole(*shape) for shape in outs],
         ),
-        out_shape=[pltpu.HBM(shape, jnp.bfloat16) for shape in outs],
+        out_shape=[jax.ShapeDtypeStruct(shape, jnp.bfloat16) for shape in outs],
         compiler_params=params(),
         cost_estimate=cost(PROJECT_COST),
         name="project",
@@ -199,7 +199,7 @@
             pltpu.VMEM((2 * pairs, 8, STRIDE), jnp.float32),
             pltpu.VMEM((BLOCK, BLOCK), jnp.float32),
         ],
-        out_shape=pltpu.HBM(payload, jnp.bfloat16),
+        out_shape=(jax.ShapeDtypeStruct if earlier else pltpu.HBM)(payload, jnp.bfloat16),
         compiler_params=params(),
         cost_estimate=cost(estimate),
         name="band_earlier" if earlier else "band_local",
@@ -406,10 +406,9 @@
     columns = exchange(tokens)
     sibling = swapped(tokens)
     kv_a, kv_b, q_a, q_b = project(core_arr, tokens, sibling, w_row)
-    kv_a, kv_b, q_a, q_b = [in_hbm(value) for value in (kv_a, kv_b, q_a, q_b)]
-    previous_kv_a = to_next(kv_a)
-    next_q_b = lax.ppermute(q_b, "seq", [(d, d - 2) for d in range(2, count)])
     local = band_part(False, q_a, kv_a, q_b, kv_b, estimate=LOCAL_COST)
+    previous_kv_a = to_next(after(kv_a, local))
+    next_q_b = lax.ppermute(after(q_b, local), "seq", [(d, d - 2) for d in range(2, count)])
     columns = after(columns, local)
     col_proj = jnp.dot(columns, w_column, preferred_element_type=jnp.float32).astype(jnp.bfloat16)
     sent_b = band_part(True, after(next_q_b, col_proj), kv_b, estimate=B_COST)

time: 94.9 us -> 108 us (1.14)
  waiting for transfers between devices: 14.7 us -> 32.2 us
  Pallas kernels: 35.8 us -> 30.1 us
    ppermute x2, waiting for transfers between devices: 0.01 us -> 13 us  [to_next(): return lax.ppermute(value, 'seq', [(d, d + 2) for d in range(count - 2)])]
    all_to_all x2, waiting for transfers between devices: 14.7 us -> 19.2 us  [exchange(): lax.all_to_all(value.reshape(chips, group, width), 'seq', split_axis=0, c...]
    pallas_call x2, Pallas kernels: 12.6 us -> 8.62 us  [band_part(): pl.pallas_call(functools.partial(band_kernel, earlier, pairs), grid=(pair...]
    pallas_call x1, Pallas kernels: 11.7 us -> 10 us  [project(): pl.pallas_call(project_kernel, grid_spec=pltpu.PrefetchScalarGridSpec(num...]
    unnamed x6 -> x10, local copies, waits for them, and re-layouts: 1.78 us -> 2.57 us
  transfers between devices with their start and end apart: 7 -> 7, of which waited for: 2 -> 3; matrix products, arithmetic and copies ran while one was open for 11% -> 10% of each run, Pallas kernels for 36% -> 27%
where the time goes in v7:
time: 108 us; the launch traced here: 107 us
  waiting for transfers between devices  32.2 us (30%)
  starting transfers between devices  31.7 us (29%)
  Pallas kernels  30.1 us (28%)
  matrix products  10.3 us (10%)
  local copies, waits for them, and re-layouts  2.57 us (2%)
    all_to_all x2, starting transfers between devices, exchange(): lax.all_to_all(value.reshape(chips, group, width), 'seq', split_axis=0, c...  22.9 us
    all_to_all x2, waiting for transfers between devices, exchange(): lax.all_to_all(value.reshape(chips, group, width), 'seq', split_axis=0, c...  19.2 us
    ppermute x2, waiting for transfers between devices, to_next(): return lax.ppermute(value, 'seq', [(d, d + 2) for d in range(count - 2)])  13 us
    dot_general x1, matrix products, on_device(): jnp.dot(columns, w_column, preferred_element_type=jnp.float32)  10.3 us
    pallas_call x1, Pallas kernels, project(): pl.pallas_call(project_kernel, grid_spec=pltpu.PrefetchScalarGridSpec(num...  10 us
    pallas_call x2, Pallas kernels, band_part(): pl.pallas_call(functools.partial(band_kernel, earlier, pairs), grid=(pair...  8.62 us
    ppermute x2, starting transfers between devices, to_next(): return lax.ppermute(value, 'seq', [(d, d + 2) for d in range(count - 2)])  7.47 us
    pallas_call x1, Pallas kernels, complete(): pl.pallas_call(complete_kernel, grid_spec=pltpu.PrefetchScalarGridSpec(nu...  5.7 us
  transfers between devices with their start and end apart: 7, of which 3 were waited for; matrix products, arithmetic and copies ran while one was open for 10% of the time, Pallas kernels for 27%

profile of v7, /device:TPU:0, one launch (start us, length us, event | category | flops | bytes accessed | tf_op | source)
XLA Modules:
  0.0 107.1 jit_solution(6475863446188716164)
XLA Ops:
  0.0 0.0 collective-permute-start
  0.0 0.0 copy-start
  0.0 11.9 %all-to-all-start = ((bf16[64,8,2048]{2,1,0:T(8,128)(2,1)}), bf16[64,8,2048]{2,1,0:T(8,128)(2,1)}, u32[]{:S(2)}, u32[]{:S(2)}) async-start(bf16[64,8,2048]{2,1,0:T(8,128)(2,1)} %bitcast.8), calls=%async_computation | async-start | bytes 4194304 | tf_op jit(solution)/shard_map/all_to_all | solution.py:393
  11.9 0.1 pad_add_fusion.flags_ref
  12.0 0.0 collective-permute-done.sibling_ref
  12.0 0.0 copy-done
  12.0 10.0 %project.1 = (bf16[2048,256]{1,0:T(8,128)(2,1)S(1)}, bf16[2048,256]{1,0:T(8,128)(2,1)S(1)}, bf16[1024,256]{1,0:T(8,128)(2,1)S(1)}, bf16[1024,256]{1,0:T(8,128)(2,1)S(1)}) custom-call(s32[1]{0:T(128)} %bitcast.core_ref, bf16[512,2048]{1,0:T(8,128)(2,1)S(1)} %copy-done, bf16[512,2048]{1,0:T(8,128)(2,1)} %collective-permute-done.sibling_ref, ...), custom_call_target="tpu_custom_call" | custom-call | flops 500000000 | bytes 16384 | tf_op jit(solution)/shard_map/project/pallas_call | solution.py:62
  22.1 6.3 %band_local.1.local_ref = bf16[544,1024]{1,0:T(8,128)(2,1)} custom-call(bf16[1024,256]{1,0:T(8,128)(2,1)S(1)} %get-tuple-element.17.refs_0_.q_ref, bf16[2048,256]{1,0:T(8,128)(2,1)S(1)} %get-tuple-element.21.refs_1_, bf16[1024,256]{1,0:T(8,128)(2,1)S(1)} %get-tuple-element.23.refs_2_, bf16[2048,256]{1,0:T(8,128)(2,1)S(1)} %get-tuple-element.20.refs_3_.refs_1_), custom_call_target="tpu_custom_call" | custom-call | flops 500000000 | bytes 16384 | tf_op jit(solution)/shard_map/band_local/pallas_call | solution.py:193
  28.3 0.0 copy-start.1
  28.3 1.0 copy-done.1
  29.3 0.0 copy-start.2
  29.3 0.8 copy-done.2
  30.1 0.0 copy-start.4
  30.1 0.8 copy-done.4
  30.9 10.8 %all-to-all-done = bf16[64,8,2048]{2,1,0:T(8,128)(2,1)} async-done(((bf16[64,8,2048]{2,1,0:T(8,128)(2,1)}), bf16[64,8,2048]{2,1,0:T(8,128)(2,1)}, u32[]{:S(2)}, u32[]{:S(2)}) %all-to-all-start) | async-done | bytes 2097184 | tf_op jit(solution)/shard_map/all_to_all | solution.py:393
  41.7 1.3 %collective-permute-start.2 = (bf16[1024,256]{1,0:T(8,128)(2,1)}, bf16[1024,256]{1,0:T(8,128)(2,1)S(1)}, u32[]{:S(2)}, u32[]{:S(2)}) collective-permute-start(bf16[1024,256]{1,0:T(8,128)(2,1)} %copy-done.4), channel_id=1, source_target_pairs={{2,0},{3,1},{4,2},{5,3},{6,4},{7,5},{8,6},{9,7},{10,8},{11,9},{12,... | collective-permute-start | bytes 1572872 | tf_op jit(solution)/shard_map/ppermute | solution.py:411
  43.0 5.6 %collective-permute-start.1 = (bf16[2048,256]{1,0:T(8,128)(2,1)}, bf16[2048,256]{1,0:T(8,128)(2,1)}, u32[]{:S(2)}, u32[]{:S(2)}) collective-permute-start(bf16[2048,256]{1,0:T(8,128)(2,1)} %copy-done.1), channel_id=1, source_target_pairs={{0,2},{1,3},{2,4},{3,5},{4,6},{5,7},{6,8},{7,9},{8,10},{9,11},{10,... | collective-permute-start | bytes 3145736 | tf_op jit(solution)/shard_map/ppermute | solution.py:403
  48.6 10.3 %convolution_convert_fusion.q_ref.k_ref.v_ref = bf16[512,3072]{1,0:T(8,128)(2,1)S(1)} fusion(bf16[512,2048]{1,0:T(8,128)(2,1)} %bitcast.3, bf16[2048,3072]{1,0:T(8,128)(2,1)} %param.5), kind=kOutput, calls=%fused_computation | convolution fusion | flops 6444023808 | bytes 17825792 | tf_op jit(solution)/shard_map/dot_general | solution.py:413
  58.8 0.0 collective-permute-done.2.refs_0_
  58.9 2.4 %band_earlier.1 = bf16[272,1024]{1,0:T(8,128)(2,1)S(1)} custom-call(bf16[1024,256]{1,0:T(8,128)(2,1)S(1)} %collective-permute-done.2.refs_0_, bf16[2048,256]{1,0:T(8,128)(2,1)S(1)} %get-tuple-element.20.refs_3_.refs_1_), custom_call_target="tpu_custom_call" | custom-call | flops 500000000 | bytes 16384 | tf_op jit(solution)/shard_map/band_earlier/pallas_call | solution.py:193
  61.2 1.9 %collective-permute-start.3 = (bf16[272,1024]{1,0:T(8,128)(2,1)S(1)}, bf16[272,1024]{1,0:T(8,128)(2,1)S(1)}, u32[]{:S(2)}, u32[]{:S(2)}) collective-permute-start(bf16[272,1024]{1,0:T(8,128)(2,1)S(1)} %band_earlier.1), channel_id=1, source_target_pairs={{0,2},{1,3},{2,4},{3,5},{4,6},{5,7},{6,8},{7,9},{8,10},{9,11},{10,... | collective-permute-start | bytes 1671176 | tf_op jit(solution)/shard_map/ppermute | solution.py:403
  63.1 4.0 %column_attention.1 = bf16[512,1024]{1,0:T(8,128)(2,1)} custom-call(bf16[512,3072]{1,0:T(8,128)(2,1)S(1)} %convolution_convert_fusion.q_ref.k_ref.v_ref, bf16[512,3072]{1,0:T(8,128)(2,1)S(1)} %convolution_convert_fusion.q_ref.k_ref.v_ref, bf16[512,3072]{1,0:T(8,128)(2,1)S(1)} %convolution_convert_fusion.q_ref.k_ref.v_ref), custom_call_target="tpu_custom_call" | custom-call | flops 6000000000 | bytes 16384 | tf_op jit(solution)/shard_map/column_attention/pallas_call | solution.py:360
  67.2 0.0 copy-start.3
  67.2 11.0 %all-to-all-start.1 = ((bf16[64,8,1024]{2,1,0:T(8,128)(2,1)}), bf16[64,8,1024]{2,1,0:T(8,128)(2,1)S(1)}, u32[]{:S(2)}, u32[]{:S(2)}) async-start(bf16[64,8,1024]{2,1,0:T(8,128)(2,1)} %bitcast.4), calls=%async_computation.1 | async-start | bytes 2097152 | tf_op jit(solution)/shard_map/all_to_all | solution.py:393
  78.2 0.0 collective-permute-done.1.kv_ref
  78.2 13.0 %collective-permute-done.3.earlier_ref = bf16[272,1024]{1,0:T(8,128)(2,1)S(1)} collective-permute-done((bf16[272,1024]{1,0:T(8,128)(2,1)S(1)}, bf16[272,1024]{1,0:T(8,128)(2,1)S(1)}, u32[]{:S(2)}, u32[]{:S(2)}) %collective-permute-start.3) | collective-permute-done | bytes 557088 | tf_op jit(solution)/shard_map/ppermute | solution.py:403
  91.2 0.0 copy-done.3
  91.2 5.7 %complete.1 = (bf16[512,2048]{1,0:T(8,128)(2,1)}, bf16[512,512]{1,0:T(8,128)(2,1)}) custom-call(s32[2]{0:T(128)S(1)} %pad_add_fusion.flags_ref, bf16[1024,256]{1,0:T(8,128)(2,1)S(1)} %copy-done.3, bf16[2048,256]{1,0:T(8,128)(2,1)} %collective-permute-done.1.kv_ref, bf16[544,1024]{1,0:T(8,128)(2,1)} %band_local.1.local_ref, ...), custom_call_target="tpu_custom_call" | custom-call | flops 20000000000 | bytes 16384 | tf_op jit(solution)/shard_map/complete/pallas_call | solution.py:261
  96.9 0.0 collective-permute-start.4
  96.9 8.4 %all-to-all-done.1 = bf16[64,8,1024]{2,1,0:T(8,128)(2,1)S(1)} async-done(((bf16[64,8,1024]{2,1,0:T(8,128)(2,1)}), bf16[64,8,1024]{2,1,0:T(8,128)(2,1)S(1)}, u32[]{:S(2)}, u32[]{:S(2)}) %all-to-all-start.1) | async-done | bytes 1048608 | tf_op jit(solution)/shard_map/all_to_all | solution.py:393
  105.3 0.0 collective-permute-done.4.cross_ref
  105.3 1.7 %place.1 = bf16[512,2048]{1,0:T(8,128)(2,1)} custom-call(s32[2]{0:T(128)S(1)} %pad_add_fusion.flags_ref, bf16[512,512]{1,0:T(8,128)(2,1)S(1)} %collective-permute-done.4.cross_ref, bf16[512,1024]{1,0:T(8,128)(2,1)S(1)} %bitcast.9, bf16[512,2048]{1,0:T(8,128)(2,1)} %get-tuple-element.28._), custom_call_target="tpu_custom_call", output_to_operand_aliasing={{}: (3, {})} | custom-call | flops 1000000000 | bytes 16384 | tf_op jit(solution)/shard_map/place/pallas_call | solution.py:298
Async XLA Ops:
  0.0 12.0 %collective-permute-start = (bf16[512,2048]{1,0:T(8,128)(2,1)}, bf16[512,2048]{1,0:T(8,128)(2,1)}, u32[]{:S(2)}, u32[]{:S(2)}) collective-permute-start(bf16[512,2048]{1,0:T(8,128)(2,1)} %own_ref.1), channel_id=1, source_target_pairs={{0,1},{1,0},{2,3},{3,2},{4,5},{5,4},{6,7},{7,6},{8,9},{9,8},{10,11... | collective-permute-start | bytes 6291464 | tf_op jit(solution)/shard_map/ppermute | solution.py:400
  0.0 12.0 %copy-start = (bf16[512,2048]{1,0:T(8,128)(2,1)S(1)}, bf16[512,2048]{1,0:T(8,128)(2,1)}, u32[]{:S(2)}) copy-start(bf16[512,2048]{1,0:T(8,128)(2,1)} %own_ref.1) | copy-start | bytes 6291460
  0.0 41.7 %all-to-all-start = ((bf16[64,8,2048]{2,1,0:T(8,128)(2,1)}), bf16[64,8,2048]{2,1,0:T(8,128)(2,1)}, u32[]{:S(2)}, u32[]{:S(2)}) async-start(bf16[64,8,2048]{2,1,0:T(8,128)(2,1)} %bitcast.8), calls=%async_computation | async-start | bytes 4194304 | tf_op jit(solution)/shard_map/all_to_all | solution.py:393
  28.3 1.0 copy-start.1
  29.3 0.8 copy-start.2
  30.1 0.8 copy-start.4
  41.7 17.1 %collective-permute-start.2 = (bf16[1024,256]{1,0:T(8,128)(2,1)}, bf16[1024,256]{1,0:T(8,128)(2,1)S(1)}, u32[]{:S(2)}, u32[]{:S(2)}) collective-permute-start(bf16[1024,256]{1,0:T(8,128)(2,1)} %copy-done.4), channel_id=1, source_target_pairs={{2,0},{3,1},{4,2},{5,3},{6,4},{7,5},{8,6},{9,7},{10,8},{11,9},{12,... | collective-permute-start | bytes 1572872 | tf_op jit(solution)/shard_map/ppermute | solution.py:411
  43.0 35.2 %collective-permute-start.1 = (bf16[2048,256]{1,0:T(8,128)(2,1)}, bf16[2048,256]{1,0:T(8,128)(2,1)}, u32[]{:S(2)}, u32[]{:S(2)}) collective-permute-start(bf16[2048,256]{1,0:T(8,128)(2,1)} %copy-done.1), channel_id=1, source_target_pairs={{0,2},{1,3},{2,4},{3,5},{4,6},{5,7},{6,8},{7,9},{8,10},{9,11},{10,... | collective-permute-start | bytes 3145736 | tf_op jit(solution)/shard_map/ppermute | solution.py:403
  61.2 30.0 %collective-permute-start.3 = (bf16[272,1024]{1,0:T(8,128)(2,1)S(1)}, bf16[272,1024]{1,0:T(8,128)(2,1)S(1)}, u32[]{:S(2)}, u32[]{:S(2)}) collective-permute-start(bf16[272,1024]{1,0:T(8,128)(2,1)S(1)} %band_earlier.1), channel_id=1, source_target_pairs={{0,2},{1,3},{2,4},{3,5},{4,6},{5,7},{6,8},{7,9},{8,10},{9,11},{10,... | collective-permute-start | bytes 1671176 | tf_op jit(solution)/shard_map/ppermute | solution.py:403
  67.2 24.0 %copy-start.3 = (bf16[1024,256]{1,0:T(8,128)(2,1)S(1)}, bf16[1024,256]{1,0:T(8,128)(2,1)}, u32[]{:S(2)}) copy-start(bf16[1024,256]{1,0:T(8,128)(2,1)} %copy-done.2) | copy-start | bytes 1572868
  67.2 38.1 %all-to-all-start.1 = ((bf16[64,8,1024]{2,1,0:T(8,128)(2,1)}), bf16[64,8,1024]{2,1,0:T(8,128)(2,1)S(1)}, u32[]{:S(2)}, u32[]{:S(2)}) async-start(bf16[64,8,1024]{2,1,0:T(8,128)(2,1)} %bitcast.4), calls=%async_computation.1 | async-start | bytes 2097152 | tf_op jit(solution)/shard_map/all_to_all | solution.py:393
  96.9 8.4 %collective-permute-start.4 = (bf16[512,512]{1,0:T(8,128)(2,1)}, bf16[512,512]{1,0:T(8,128)(2,1)S(1)}, u32[]{:S(2)}, u32[]{:S(2)}) collective-permute-start(bf16[512,512]{1,0:T(8,128)(2,1)} %get-tuple-element.27), channel_id=1, source_target_pairs={{0,1},{1,0},{2,3},{3,2},{4,5},{5,4},{6,7},{7,6},{8,9},{9,8},{10,11... | collective-permute-start | bytes 1572872 | tf_op jit(solution)/shard_map/ppermute | solution.py:400

commit v8 on v7

--- a/solution.py
+++ b/solution.py
@@ -406,9 +406,9 @@
     columns = exchange(tokens)
     sibling = swapped(tokens)
     kv_a, kv_b, q_a, q_b = project(core_arr, tokens, sibling, w_row)
+    previous_kv_a = to_next(kv_a)
+    next_q_b = lax.ppermute(q_b, "seq", [(d, d - 2) for d in range(2, count)])
     local = band_part(False, q_a, kv_a, q_b, kv_b, estimate=LOCAL_COST)
-    previous_kv_a = to_next(after(kv_a, local))
-    next_q_b = lax.ppermute(after(q_b, local), "seq", [(d, d - 2) for d in range(2, count)])
     columns = after(columns, local)
     col_proj = jnp.dot(columns, w_column, preferred_element_type=jnp.float32).astype(jnp.bfloat16)
     sent_b = band_part(True, after(next_q_b, col_proj), kv_b, estimate=B_COST)

time: 108 us -> 91.9 us (0.85)
  waiting for transfers between devices: 32.2 us -> 15.1 us
  Pallas kernels: 30.1 us -> 32.6 us
  local copies, waits for them, and re-layouts: 2.57 us -> 0.82 us
    ppermute x2, waiting for transfers between devices: 13 us -> 0.01 us  [to_next(): return lax.ppermute(value, 'seq', [(d, d + 2) for d in range(count - 2)])]
    all_to_all x2, waiting for transfers between devices: 19.2 us -> 15.1 us  [exchange(): lax.all_to_all(value.reshape(chips, group, width), 'seq', split_axis=0, c...]
    unnamed x10 -> x6, local copies, waits for them, and re-layouts: 2.57 us -> 0.82 us
    pallas_call x2, Pallas kernels: 8.62 us -> 9.96 us  [band_part(): pl.pallas_call(functools.partial(band_kernel, earlier, pairs), grid=(pair...]
    pallas_call x1, Pallas kernels: 10 us -> 11.2 us  [project(): pl.pallas_call(project_kernel, grid_spec=pltpu.PrefetchScalarGridSpec(num...]
  transfers between devices with their start and end apart: 7 -> 7, of which waited for: 3 -> 2; matrix products, arithmetic and copies ran while one was open for 10% -> 11% of each run, Pallas kernels for 27% -> 34%
where the time goes in v8:
time: 91.9 us; the launch traced here: 91.5 us
  Pallas kernels  32.6 us (35%)
  starting transfers between devices  32.3 us (35%)
  waiting for transfers between devices  15.1 us (16%)
  matrix products  10.3 us (11%)
    all_to_all x2, starting transfers between devices, exchange(): lax.all_to_all(value.reshape(chips, group, width), 'seq', split_axis=0, c...  22.8 us
    all_to_all x2, waiting for transfers between devices, exchange(): lax.all_to_all(value.reshape(chips, group, width), 'seq', split_axis=0, c...  15.1 us
    pallas_call x1, Pallas kernels, project(): pl.pallas_call(project_kernel, grid_spec=pltpu.PrefetchScalarGridSpec(num...  11.2 us
    dot_general x1, matrix products, on_device(): jnp.dot(columns, w_column, preferred_element_type=jnp.float32)  10.3 us
    pallas_call x2, Pallas kernels, band_part(): pl.pallas_call(functools.partial(band_kernel, earlier, pairs), grid=(pair...  9.96 us
    ppermute x2, starting transfers between devices, to_next(): return lax.ppermute(value, 'seq', [(d, d + 2) for d in range(count - 2)])  8.28 us
    pallas_call x1, Pallas kernels, complete(): pl.pallas_call(complete_kernel, grid_spec=pltpu.PrefetchScalarGridSpec(nu...  5.7 us
    pallas_call x1, Pallas kernels, column_attention(): pl.pallas_call(functools.partial(column_kernel, group), grid=(steps,), in...  4.05 us
  transfers between devices with their start and end apart: 7, of which 2 were waited for; matrix products, arithmetic and copies ran while one was open for 11% of the time, Pallas kernels for 34%

profile of v8, /device:TPU:0, one launch (start us, length us, event | category | flops | bytes accessed | tf_op | source)
XLA Modules:
  0.0 91.5 jit_solution(17043045171648599061)
XLA Ops:
  0.0 0.0 collective-permute-start
  0.0 0.0 copy-start
  0.0 11.9 %all-to-all-start = ((bf16[64,8,2048]{2,1,0:T(8,128)(2,1)}), bf16[64,8,2048]{2,1,0:T(8,128)(2,1)}, u32[]{:S(2)}, u32[]{:S(2)}) async-start(bf16[64,8,2048]{2,1,0:T(8,128)(2,1)} %bitcast.8), calls=%async_computation | async-start | bytes 4194304 | tf_op jit(solution)/shard_map/all_to_all | solution.py:393
  11.9 0.1 pad_add_fusion.flags_ref
  12.0 0.0 collective-permute-done.sibling_ref
  12.0 0.0 copy-done
  12.0 11.2 %project.1 = (bf16[2048,256]{1,0:T(8,128)(2,1)}, bf16[2048,256]{1,0:T(8,128)(2,1)S(1)}, bf16[1024,256]{1,0:T(8,128)(2,1)S(1)}, bf16[1024,256]{1,0:T(8,128)(2,1)}) custom-call(s32[1]{0:T(128)} %bitcast.core_ref, bf16[512,2048]{1,0:T(8,128)(2,1)S(1)} %copy-done, bf16[512,2048]{1,0:T(8,128)(2,1)} %collective-permute-done.sibling_ref, bf16[2048,3072]{1,0:T(8,128)(2,1)} %w_ref.1), custom_call_target="tpu_custom_call" | custom-call | flops 500000000 | bytes 16384 | tf_op jit(solution)/shard_map/project/pallas_call | solution.py:62
  23.2 1.3 %collective-permute-start.2 = (bf16[1024,256]{1,0:T(8,128)(2,1)}, bf16[1024,256]{1,0:T(8,128)(2,1)S(1)}, u32[]{:S(2)}, u32[]{:S(2)}) collective-permute-start(bf16[1024,256]{1,0:T(8,128)(2,1)} %get-tuple-element.17.refs_2_), channel_id=1, source_target_pairs={{2,0},{3,1},{4,2},{5,3},{6,4},{7,5},{8,6},{9,7},{10,8},{11,9},{12,... | collective-permute-start | bytes 1572872 | tf_op jit(solution)/shard_map/ppermute | solution.py:410
  24.5 5.6 %collective-permute-start.1 = (bf16[2048,256]{1,0:T(8,128)(2,1)}, bf16[2048,256]{1,0:T(8,128)(2,1)}, u32[]{:S(2)}, u32[]{:S(2)}) collective-permute-start(bf16[2048,256]{1,0:T(8,128)(2,1)} %get-tuple-element.16.refs_1_), channel_id=1, source_target_pairs={{0,2},{1,3},{2,4},{3,5},{4,6},{5,7},{6,8},{7,9},{8,10},{9,11},{10,... | collective-permute-start | bytes 3145736 | tf_op jit(solution)/shard_map/ppermute | solution.py:403
  30.1 7.6 %band_local.1.local_ref = bf16[544,1024]{1,0:T(8,128)(2,1)} custom-call(bf16[1024,256]{1,0:T(8,128)(2,1)S(1)} %get-tuple-element.15.refs_0_.q_ref, bf16[2048,256]{1,0:T(8,128)(2,1)} %get-tuple-element.16.refs_1_, bf16[1024,256]{1,0:T(8,128)(2,1)} %get-tuple-element.17.refs_2_, bf16[2048,256]{1,0:T(8,128)(2,1)S(1)} %get-tuple-element.18.refs_3_.refs_1_), custom_call_target="tpu_custom_call" | custom-call | flops 500000000 | bytes 16384 | tf_op jit(solution)/shard_map/band_local/pallas_call | solution.py:193
  37.7 0.0 copy-start.1
  37.7 0.8 copy-done.1
  38.5 3.3 %all-to-all-done = bf16[64,8,2048]{2,1,0:T(8,128)(2,1)} async-done(((bf16[64,8,2048]{2,1,0:T(8,128)(2,1)}), bf16[64,8,2048]{2,1,0:T(8,128)(2,1)}, u32[]{:S(2)}, u32[]{:S(2)}) %all-to-all-start) | async-done | bytes 2097184 | tf_op jit(solution)/shard_map/all_to_all | solution.py:393
  41.7 10.3 %convolution_convert_fusion.q_ref.k_ref.v_ref = bf16[512,3072]{1,0:T(8,128)(2,1)S(1)} fusion(bf16[512,2048]{1,0:T(8,128)(2,1)} %bitcast.3, bf16[2048,3072]{1,0:T(8,128)(2,1)} %param.5), kind=kOutput, calls=%fused_computation | convolution fusion | flops 6444023808 | bytes 17825792 | tf_op jit(solution)/shard_map/dot_general | solution.py:413
  52.0 0.0 collective-permute-done.2.refs_0_
  52.0 2.4 %band_earlier.1 = bf16[272,1024]{1,0:T(8,128)(2,1)S(1)} custom-call(bf16[1024,256]{1,0:T(8,128)(2,1)S(1)} %collective-permute-done.2.refs_0_, bf16[2048,256]{1,0:T(8,128)(2,1)S(1)} %get-tuple-element.18.refs_3_.refs_1_), custom_call_target="tpu_custom_call" | custom-call | flops 500000000 | bytes 16384 | tf_op jit(solution)/shard_map/band_earlier/pallas_call | solution.py:193
  54.4 2.7 %collective-permute-start.3 = (bf16[272,1024]{1,0:T(8,128)(2,1)S(1)}, bf16[272,1024]{1,0:T(8,128)(2,1)S(1)}, u32[]{:S(2)}, u32[]{:S(2)}) collective-permute-start(bf16[272,1024]{1,0:T(8,128)(2,1)S(1)} %band_earlier.1), channel_id=1, source_target_pairs={{0,2},{1,3},{2,4},{3,5},{4,6},{5,7},{6,8},{7,9},{8,10},{9,11},{10,... | collective-permute-start | bytes 1671176 | tf_op jit(solution)/shard_map/ppermute | solution.py:403
  57.1 4.1 %column_attention.1 = bf16[512,1024]{1,0:T(8,128)(2,1)} custom-call(bf16[512,3072]{1,0:T(8,128)(2,1)S(1)} %convolution_convert_fusion.q_ref.k_ref.v_ref, bf16[512,3072]{1,0:T(8,128)(2,1)S(1)} %convolution_convert_fusion.q_ref.k_ref.v_ref, bf16[512,3072]{1,0:T(8,128)(2,1)S(1)} %convolution_convert_fusion.q_ref.k_ref.v_ref), custom_call_target="tpu_custom_call" | custom-call | flops 6000000000 | bytes 16384 | tf_op jit(solution)/shard_map/column_attention/pallas_call | solution.py:360
  61.2 0.0 copy-start.2
  61.2 10.9 %all-to-all-start.1 = ((bf16[64,8,1024]{2,1,0:T(8,128)(2,1)}), bf16[64,8,1024]{2,1,0:T(8,128)(2,1)S(1)}, u32[]{:S(2)}, u32[]{:S(2)}) async-start(bf16[64,8,1024]{2,1,0:T(8,128)(2,1)} %bitcast.4), calls=%async_computation.1 | async-start | bytes 2097152 | tf_op jit(solution)/shard_map/all_to_all | solution.py:393
  72.0 0.0 collective-permute-done.1.kv_ref
  72.0 0.0 collective-permute-done.3.earlier_ref
  72.0 0.0 copy-done.2
  72.1 5.7 %complete.1 = (bf16[512,2048]{1,0:T(8,128)(2,1)}, bf16[512,512]{1,0:T(8,128)(2,1)}) custom-call(s32[2]{0:T(128)S(1)} %pad_add_fusion.flags_ref, bf16[1024,256]{1,0:T(8,128)(2,1)S(1)} %copy-done.2, bf16[2048,256]{1,0:T(8,128)(2,1)} %collective-permute-done.1.kv_ref, bf16[544,1024]{1,0:T(8,128)(2,1)} %band_local.1.local_ref, ...), custom_call_target="tpu_custom_call" | custom-call | flops 20000000000 | bytes 16384 | tf_op jit(solution)/shard_map/complete/pallas_call | solution.py:261
  77.8 0.0 collective-permute-start.4
  77.8 11.9 %all-to-all-done.1 = bf16[64,8,1024]{2,1,0:T(8,128)(2,1)S(1)} async-done(((bf16[64,8,1024]{2,1,0:T(8,128)(2,1)}), bf16[64,8,1024]{2,1,0:T(8,128)(2,1)S(1)}, u32[]{:S(2)}, u32[]{:S(2)}) %all-to-all-start.1) | async-done | bytes 1048608 | tf_op jit(solution)/shard_map/all_to_all | solution.py:393
  89.6 0.0 collective-permute-done.4.cross_ref
  89.6 1.7 %place.1 = bf16[512,2048]{1,0:T(8,128)(2,1)} custom-call(s32[2]{0:T(128)S(1)} %pad_add_fusion.flags_ref, bf16[512,512]{1,0:T(8,128)(2,1)S(1)} %collective-permute-done.4.cross_ref, bf16[512,1024]{1,0:T(8,128)(2,1)S(1)} %bitcast.9, bf16[512,2048]{1,0:T(8,128)(2,1)} %get-tuple-element.24._), custom_call_target="tpu_custom_call", output_to_operand_aliasing={{}: (3, {})} | custom-call | flops 1000000000 | bytes 16384 | tf_op jit(solution)/shard_map/place/pallas_call | solution.py:298
Async XLA Ops:
  0.0 12.0 %collective-permute-start = (bf16[512,2048]{1,0:T(8,128)(2,1)}, bf16[512,2048]{1,0:T(8,128)(2,1)}, u32[]{:S(2)}, u32[]{:S(2)}) collective-permute-start(bf16[512,2048]{1,0:T(8,128)(2,1)} %own_ref.1), channel_id=1, source_target_pairs={{0,1},{1,0},{2,3},{3,2},{4,5},{5,4},{6,7},{7,6},{8,9},{9,8},{10,11... | collective-permute-start | bytes 6291464 | tf_op jit(solution)/shard_map/ppermute | solution.py:400
  0.0 12.0 %copy-start = (bf16[512,2048]{1,0:T(8,128)(2,1)S(1)}, bf16[512,2048]{1,0:T(8,128)(2,1)}, u32[]{:S(2)}) copy-start(bf16[512,2048]{1,0:T(8,128)(2,1)} %own_ref.1) | copy-start | bytes 6291460
  0.0 41.7 %all-to-all-start = ((bf16[64,8,2048]{2,1,0:T(8,128)(2,1)}), bf16[64,8,2048]{2,1,0:T(8,128)(2,1)}, u32[]{:S(2)}, u32[]{:S(2)}) async-start(bf16[64,8,2048]{2,1,0:T(8,128)(2,1)} %bitcast.8), calls=%async_computation | async-start | bytes 4194304 | tf_op jit(solution)/shard_map/all_to_all | solution.py:393
  23.2 28.8 %collective-permute-start.2 = (bf16[1024,256]{1,0:T(8,128)(2,1)}, bf16[1024,256]{1,0:T(8,128)(2,1)S(1)}, u32[]{:S(2)}, u32[]{:S(2)}) collective-permute-start(bf16[1024,256]{1,0:T(8,128)(2,1)} %get-tuple-element.17.refs_2_), channel_id=1, source_target_pairs={{2,0},{3,1},{4,2},{5,3},{6,4},{7,5},{8,6},{9,7},{10,8},{11,9},{12,... | collective-permute-start | bytes 1572872 | tf_op jit(solution)/shard_map/ppermute | solution.py:410
  24.5 47.5 %collective-permute-start.1 = (bf16[2048,256]{1,0:T(8,128)(2,1)}, bf16[2048,256]{1,0:T(8,128)(2,1)}, u32[]{:S(2)}, u32[]{:S(2)}) collective-permute-start(bf16[2048,256]{1,0:T(8,128)(2,1)} %get-tuple-element.16.refs_1_), channel_id=1, source_target_pairs={{0,2},{1,3},{2,4},{3,5},{4,6},{5,7},{6,8},{7,9},{8,10},{9,11},{10,... | collective-permute-start | bytes 3145736 | tf_op jit(solution)/shard_map/ppermute | solution.py:403
  37.7 0.8 copy-start.1
  54.4 17.7 %collective-permute-start.3 = (bf16[272,1024]{1,0:T(8,128)(2,1)S(1)}, bf16[272,1024]{1,0:T(8,128)(2,1)S(1)}, u32[]{:S(2)}, u32[]{:S(2)}) collective-permute-start(bf16[272,1024]{1,0:T(8,128)(2,1)S(1)} %band_earlier.1), channel_id=1, source_target_pairs={{0,2},{1,3},{2,4},{3,5},{4,6},{5,7},{6,8},{7,9},{8,10},{9,11},{10,... | collective-permute-start | bytes 1671176 | tf_op jit(solution)/shard_map/ppermute | solution.py:403
  61.2 10.9 %copy-start.2 = (bf16[1024,256]{1,0:T(8,128)(2,1)S(1)}, bf16[1024,256]{1,0:T(8,128)(2,1)}, u32[]{:S(2)}) copy-start(bf16[1024,256]{1,0:T(8,128)(2,1)} %copy-done.1) | copy-start | bytes 1572868
  61.2 28.5 %all-to-all-start.1 = ((bf16[64,8,1024]{2,1,0:T(8,128)(2,1)}), bf16[64,8,1024]{2,1,0:T(8,128)(2,1)S(1)}, u32[]{:S(2)}, u32[]{:S(2)}) async-start(bf16[64,8,1024]{2,1,0:T(8,128)(2,1)} %bitcast.4), calls=%async_computation.1 | async-start | bytes 2097152 | tf_op jit(solution)/shard_map/all_to_all | solution.py:393
  77.8 11.9 %collective-permute-start.4 = (bf16[512,512]{1,0:T(8,128)(2,1)}, bf16[512,512]{1,0:T(8,128)(2,1)S(1)}, u32[]{:S(2)}, u32[]{:S(2)}) collective-permute-start(bf16[512,512]{1,0:T(8,128)(2,1)} %get-tuple-element.23), channel_id=1, source_target_pairs={{0,1},{1,0},{2,3},{3,2},{4,5},{5,4},{6,7},{7,6},{8,9},{9,8},{10,11... | collective-permute-start | bytes 1572872 | tf_op jit(solution)/shard_map/ppermute | solution.py:400

commit v9 on v8

--- a/solution.py
+++ b/solution.py
@@ -312,62 +312,87 @@
     )(flags, cross, col_out, result)
 
 
-def column_kernel(group, q_ref, k_ref, v_ref, o_ref, bias_ref):
+def column_kernel(group, x_hbm, w_hbm, o_ref, x_ref, w_ref, bias_ref, sems, *projected):
     parts = HALF // BLOCK
-    heads = q_ref.shape[1] // HEAD
-
-    @pl.when(pl.program_id(0) == 0)
-    def _():
-        qpos = lax.broadcasted_iota(jnp.int32, (BLOCK, BLOCK), 0)
-        kpos = lax.broadcasted_iota(jnp.int32, (BLOCK, BLOCK), 1)
-        column = ((qpos - kpos) & (group - 1)) == 0
-        bias_ref[0] = jnp.where(column, 0.0, NEG)
-        bias_ref[1] = jnp.where(column & (kpos <= qpos), 0.0, NEG)
+    heads = HEADS // 2
+    width = heads * HEAD
+    load_x = pltpu.make_async_copy(x_hbm, x_ref, sems.at[6])
+    load_x.start()
+    loads = []
+    for index in range(6):
+        half, third = divmod(index, 3)
+        first = third * HEADS * HEAD + half * width
+        load = pltpu.make_async_copy(
+            w_hbm.at[:, first : first + width], w_ref.at[index], sems.at[index]
+        )
+        load.start()
+        loads.append(load)
+
+    qpos = lax.broadcasted_iota(jnp.int32, (BLOCK, BLOCK), 0)
+    kpos = lax.broadcasted_iota(jnp.int32, (BLOCK, BLOCK), 1)
+    column = ((qpos - kpos) & (group - 1)) == 0
+    bias_ref[0] = jnp.where(column, 0.0, NEG)
+    bias_ref[1] = jnp.where(column & (kpos <= qpos), 0.0, NEG)
 
     def rows(block):
         return slice(block * BLOCK, (block + 1) * BLOCK)
 
-    def start(part, head):
-        query = q_ref[rows(part), columns_of(head)]
-        return [
-            lax.dot_general(
-                query, k_ref[rows(block), columns_of(head)], (((1,), (1,)), ((), ())),
-                preferred_element_type=jnp.float32,
-            )
-            for block in range(part + 1)
-        ]
-
-    def finish(part, head, scores):
-        scores = [s + bias_ref[1 if block == part else 0] for block, s in enumerate(scores)]
-        top = jnp.max(functools.reduce(jnp.maximum, scores), axis=1, keepdims=True)
-        out = 0.0
-        for block, s in enumerate(scores):
-            values = v_ref[rows(block), columns_of(head)]
-            values = jnp.concatenate([values, jnp.ones_like(values)], axis=1)
-            expd = jnp.exp2((s - top) * SCALE2).astype(jnp.bfloat16)
-            out = out + jnp.dot(expd, values, preferred_element_type=jnp.float32)
-        out = out[:, :HEAD] * (1.0 / out[:, HEAD:])
-        o_ref[rows(part), columns_of(head)] = out.astype(jnp.bfloat16)
-
-    pipelined([(part, head) for part in range(parts) for head in range(heads)], 4, start, finish)
-
-
-def column_attention(projected, group):
-    rows = projected.shape[0]
-    heads = 4
-    steps = HEADS // heads
-    spec = lambda third: pl.BlockSpec((rows, heads * HEAD), lambda j: (0, third * steps + j))
+    def attend(q_ref, k_ref, v_ref, first):
+        def start(part, head):
+            query = q_ref[rows(part), columns_of(head)]
+            return [
+                lax.dot_general(
+                    query, k_ref[rows(block), columns_of(head)], (((1,), (1,)), ((), ())),
+                    preferred_element_type=jnp.float32,
+                )
+                for block in range(part + 1)
+            ]
+
+        def finish(part, head, scores):
+            scores = [s + bias_ref[1 if block == part else 0] for block, s in enumerate(scores)]
+            top = jnp.max(functools.reduce(jnp.maximum, scores), axis=1, keepdims=True)
+            out = 0.0
+            for block, s in enumerate(scores):
+                values = v_ref[rows(block), columns_of(head)]
+                values = jnp.concatenate([values, jnp.ones_like(values)], axis=1)
+                expd = jnp.exp2((s - top) * SCALE2).astype(jnp.bfloat16)
+                out = out + jnp.dot(expd, values, preferred_element_type=jnp.float32)
+            out = out[:, :HEAD] * (1.0 / out[:, HEAD:])
+            o_ref[rows(part), columns_of(first + head)] = out.astype(jnp.bfloat16)
+
+        jobs = [(part, head) for part in range(parts) for head in range(heads)]
+        pipelined(jobs, 4, start, finish)
+
+    load_x.wait()
+    for index, load in enumerate(loads):
+        load.wait()
+        value = jnp.dot(x_ref[...], w_ref[index], preferred_element_type=jnp.float32)
+        projected[index][...] = value.astype(jnp.bfloat16)
+        if index == 2:
+            attend(*projected[:3], 0)
+    attend(*projected[3:], heads)
+
+
+def column_attention(x, w_column, group):
+    rows, depth = x.shape
+    width = HEADS // 2 * HEAD
+    far = pl.BlockSpec(memory_space=pltpu.HBM)
     return pl.pallas_call(
         functools.partial(column_kernel, group),
-        grid=(steps,),
-        in_specs=[spec(0), spec(1), spec(2)],
-        out_specs=pl.BlockSpec((rows, heads * HEAD), lambda j: (0, j)),
+        in_specs=[far, far],
+        out_specs=pl.BlockSpec(memory_space=pltpu.VMEM),
         out_shape=jax.ShapeDtypeStruct((rows, HEADS * HEAD), jnp.bfloat16),
-        scratch_shapes=[pltpu.VMEM((2, BLOCK, BLOCK), jnp.float32)],
-        compiler_params=params(),
-        cost_estimate=cost(6),
+        scratch_shapes=[
+            pltpu.VMEM((rows, depth), jnp.bfloat16),
+            pltpu.VMEM((6, depth, width), jnp.bfloat16),
+            pltpu.VMEM((2, BLOCK, BLOCK), jnp.float32),
+            pltpu.SemaphoreType.DMA((7,)),
+        ]
+        + [pltpu.VMEM((rows, width), jnp.bfloat16)] * 6,
+        compiler_params=pltpu.CompilerParams(vmem_limit_bytes=44 << 20),
+        cost_estimate=cost(13),
         name="column_attention",
-    )(projected, projected, projected)
+    )(in_hbm(x), in_hbm(w_column))
 
 
 def in_hbm(value):
@@ -410,12 +435,11 @@
     next_q_b = lax.ppermute(q_b, "seq", [(d, d - 2) for d in range(2, count)])
     local = band_part(False, q_a, kv_a, q_b, kv_b, estimate=LOCAL_COST)
     columns = after(columns, local)
-    col_proj = jnp.dot(columns, w_column, preferred_element_type=jnp.float32).astype(jnp.bfloat16)
-    sent_b = band_part(True, after(next_q_b, col_proj), kv_b, estimate=B_COST)
+    col_out = column_attention(columns, w_column, group)
+    sent_b = band_part(True, after(next_q_b, col_out), kv_b, estimate=B_COST)
     earlier_b = to_next(sent_b)
-    col_out = column_attention(after(col_proj, sent_b), group)
     result, cross = complete(flags, q_a, after(previous_kv_a, col_out), in_hbm(local), earlier_b)
-    return place(flags, swapped(cross), exchange(col_out), result)
+    return place(flags, swapped(cross), exchange(after(col_out, sent_b)), result)
 
 
 def solution(mesh):

time: 91.9 us -> 96.2 us (1.047)
  the two profiles are of different devices: /device:TPU:0 before, /device:TPU:9 now
where the time goes in v9:
time: 96.2 us; the launch traced here: 95.8 us
  starting transfers between devices  42.9 us (45%)
  Pallas kernels  41.7 us (43%)
  waiting for transfers between devices  8.96 us (9%)
  local copies, waits for them, and re-layouts  1.86 us (2%)
    all_to_all x2, starting transfers between devices, exchange(): lax.all_to_all(value.reshape(chips, group, width), 'seq', split_axis=0, c...  21.6 us
    pallas_call x1, Pallas kernels, column_attention(): pl.pallas_call(functools.partial(column_kernel, group), in_specs=[far, fa...  13.4 us
    ppermute x2, starting transfers between devices, swapped(): return lax.ppermute(value, 'seq', [(d, d ^ 1) for d in range(count)])  13.1 us
    pallas_call x1, Pallas kernels, project(): pl.pallas_call(project_kernel, grid_spec=pltpu.PrefetchScalarGridSpec(num...  11.2 us
    pallas_call x2, Pallas kernels, band_part(): pl.pallas_call(functools.partial(band_kernel, earlier, pairs), grid=(pair...  9.89 us
    pallas_call x1, Pallas kernels, complete(): pl.pallas_call(complete_kernel, grid_spec=pltpu.PrefetchScalarGridSpec(nu...  5.51 us
    ppermute x1, starting transfers between devices, on_device(): next_q_b = lax.ppermute(q_b, 'seq', [(d, d - 2) for d in range(2, count)])  4.29 us
    ppermute x2, waiting for transfers between devices, to_next(): return lax.ppermute(value, 'seq', [(d, d + 2) for d in range(count - 2)])  4.16 us
  transfers between devices with their start and end apart: 7, of which 3 were waited for; matrix products, arithmetic and copies ran while one was open for 0% of the time, Pallas kernels for 42%

profile of v9, /device:TPU:9, one launch (start us, length us, event | category | flops | bytes accessed | tf_op | source)
XLA Modules:
  0.0 95.8 jit_solution(9513995146854052954)
XLA Ops:
  0.0 0.7 collective-permute-start
  0.7 0.0 copy-start
  0.7 11.2 %all-to-all-start = ((bf16[64,8,2048]{2,1,0:T(8,128)(2,1)}), bf16[64,8,2048]{2,1,0:T(8,128)(2,1)}, u32[]{:S(2)}, u32[]{:S(2)}) async-start(bf16[64,8,2048]{2,1,0:T(8,128)(2,1)} %bitcast.6), calls=%async_computation | async-start | bytes 4194304 | tf_op jit(solution)/shard_map/all_to_all | solution.py:418
  11.9 0.0 collective-permute-done.sibling_ref
  11.9 0.0 copy-done
  11.9 11.2 %project.1 = (bf16[2048,256]{1,0:T(8,128)(2,1)}, bf16[2048,256]{1,0:T(8,128)(2,1)S(1)}, bf16[1024,256]{1,0:T(8,128)(2,1)S(1)}, bf16[1024,256]{1,0:T(8,128)(2,1)}) custom-call(s32[1]{0:T(128)} %bitcast.core_ref, bf16[512,2048]{1,0:T(8,128)(2,1)S(1)} %copy-done, bf16[512,2048]{1,0:T(8,128)(2,1)} %collective-permute-done.sibling_ref, bf16[2048,3072]{1,0:T(8,128)(2,1)} %w_ref.1), custom_call_target="tpu_custom_call" | custom-call | flops 500000000 | bytes 16384 | tf_op jit(solution)/shard_map/project/pallas_call | solution.py:62
  23.1 4.3 %collective-permute-start.2 = (bf16[1024,256]{1,0:T(8,128)(2,1)}, bf16[1024,256]{1,0:T(8,128)(2,1)S(1)}, u32[]{:S(2)}, u32[]{:S(2)}) collective-permute-start(bf16[1024,256]{1,0:T(8,128)(2,1)} %get-tuple-element.17.refs_2_), channel_id=1, source_target_pairs={{2,0},{3,1},{4,2},{5,3},{6,4},{7,5},{8,6},{9,7},{10,8},{11,9},{12,... | collective-permute-start | bytes 1572872 | tf_op jit(solution)/shard_map/ppermute | solution.py:435
  27.4 1.9 %collective-permute-start.1 = (bf16[2048,256]{1,0:T(8,128)(2,1)}, bf16[2048,256]{1,0:T(8,128)(2,1)}, u32[]{:S(2)}, u32[]{:S(2)}) collective-permute-start(bf16[2048,256]{1,0:T(8,128)(2,1)} %get-tuple-element.16.refs_1_), channel_id=1, source_target_pairs={{0,2},{1,3},{2,4},{3,5},{4,6},{5,7},{6,8},{7,9},{8,10},{9,11},{10,... | collective-permute-start | bytes 3145736 | tf_op jit(solution)/shard_map/ppermute | solution.py:428
  29.4 7.6 %band_local.1.local_ref = bf16[544,1024]{1,0:T(8,128)(2,1)} custom-call(bf16[1024,256]{1,0:T(8,128)(2,1)S(1)} %get-tuple-element.15.refs_0_.q_ref, bf16[2048,256]{1,0:T(8,128)(2,1)} %get-tuple-element.16.refs_1_, bf16[1024,256]{1,0:T(8,128)(2,1)} %get-tuple-element.17.refs_2_, bf16[2048,256]{1,0:T(8,128)(2,1)S(1)} %get-tuple-element.18.refs_3_.refs_1_), custom_call_target="tpu_custom_call" | custom-call | flops 500000000 | bytes 16384 | tf_op jit(solution)/shard_map/band_local/pallas_call | solution.py:193
  36.9 0.0 copy-start.1
  36.9 0.8 copy-done.1
  37.8 3.3 %all-to-all-done = bf16[64,8,2048]{2,1,0:T(8,128)(2,1)} async-done(((bf16[64,8,2048]{2,1,0:T(8,128)(2,1)}), bf16[64,8,2048]{2,1,0:T(8,128)(2,1)}, u32[]{:S(2)}, u32[]{:S(2)}) %all-to-all-start) | async-done | bytes 2097184 | tf_op jit(solution)/shard_map/all_to_all | solution.py:418
  41.0 13.4 %column_attention.1 = bf16[512,1024]{1,0:T(8,128)(2,1)} custom-call(bf16[512,2048]{1,0:T(8,128)(2,1)} %bitcast.3.x_hbm, bf16[2048,3072]{1,0:T(8,128)(2,1)} %w_hbm.1), custom_call_target="tpu_custom_call" | custom-call | flops 12999999488 | bytes 16384 | tf_op jit(solution)/shard_map/column_attention/pallas_call | solution.py:380
  54.4 0.0 collective-permute-done.2.refs_0_
  54.4 2.3 %band_earlier.1 = bf16[272,1024]{1,0:T(8,128)(2,1)S(1)} custom-call(bf16[1024,256]{1,0:T(8,128)(2,1)S(1)} %collective-permute-done.2.refs_0_, bf16[2048,256]{1,0:T(8,128)(2,1)S(1)} %get-tuple-element.18.refs_3_.refs_1_), custom_call_target="tpu_custom_call" | custom-call | flops 500000000 | bytes 16384 | tf_op jit(solution)/shard_map/band_earlier/pallas_call | solution.py:193
  56.7 1.9 %collective-permute-start.3 = (bf16[272,1024]{1,0:T(8,128)(2,1)S(1)}, bf16[272,1024]{1,0:T(8,128)(2,1)S(1)}, u32[]{:S(2)}, u32[]{:S(2)}) collective-permute-start(bf16[272,1024]{1,0:T(8,128)(2,1)S(1)} %band_earlier.1), channel_id=1, source_target_pairs={{0,2},{1,3},{2,4},{3,5},{4,6},{5,7},{6,8},{7,9},{8,10},{9,11},{10,... | collective-permute-start | bytes 1671176 | tf_op jit(solution)/shard_map/ppermute | solution.py:428
  58.7 0.1 pad_add_fusion.flags_ref
  58.7 10.4 %all-to-all-start.1 = ((bf16[64,8,1024]{2,1,0:T(8,128)(2,1)}), bf16[64,8,1024]{2,1,0:T(8,128)(2,1)S(1)}, u32[]{:S(2)}, u32[]{:S(2)}) async-start(bf16[64,8,1024]{2,1,0:T(8,128)(2,1)} %bitcast.4), calls=%async_computation.1 | async-start | bytes 2097152 | tf_op jit(solution)/shard_map/all_to_all | solution.py:418
  69.2 0.0 collective-permute-done.1.kv_ref
  69.2 4.2 %collective-permute-done.3.earlier_ref = bf16[272,1024]{1,0:T(8,128)(2,1)S(1)} collective-permute-done((bf16[272,1024]{1,0:T(8,128)(2,1)S(1)}, bf16[272,1024]{1,0:T(8,128)(2,1)S(1)}, u32[]{:S(2)}, u32[]{:S(2)}) %collective-permute-start.3) | collective-permute-done | bytes 557088 | tf_op jit(solution)/shard_map/ppermute | solution.py:428
  73.3 0.0 copy-start.2
  73.3 1.0 %copy-done.2 = bf16[1024,256]{1,0:T(8,128)(2,1)S(1)} copy-done((bf16[1024,256]{1,0:T(8,128)(2,1)S(1)}, bf16[1024,256]{1,0:T(8,128)(2,1)}, u32[]{:S(2)}) %copy-start.2) | copy-done | bytes 524312
  74.4 5.5 %complete.1 = (bf16[512,2048]{1,0:T(8,128)(2,1)}, bf16[512,512]{1,0:T(8,128)(2,1)S(1)}) custom-call(s32[2]{0:T(128)S(1)} %pad_add_fusion.flags_ref, bf16[1024,256]{1,0:T(8,128)(2,1)S(1)} %copy-done.2, bf16[2048,256]{1,0:T(8,128)(2,1)} %collective-permute-done.1.kv_ref, bf16[544,1024]{1,0:T(8,128)(2,1)} %band_local.1.local_ref, ...), custom_call_target="tpu_custom_call" | custom-call | flops 20000000000 | bytes 16384 | tf_op jit(solution)/shard_map/complete/pallas_call | solution.py:261
  79.9 12.5 %collective-permute-start.4 = (bf16[512,512]{1,0:T(8,128)(2,1)S(1)}, bf16[512,512]{1,0:T(8,128)(2,1)S(1)}, u32[]{:S(2)}, u32[]{:S(2)}) collective-permute-start(bf16[512,512]{1,0:T(8,128)(2,1)S(1)} %get-tuple-element.22), channel_id=1, source_target_pairs={{0,1},{1,0},{2,3},{3,2},{4,5},{5,4},{6,7},{7,6},{8,9},{9,8},{10,11... | collective-permute-start | bytes 1572872 | tf_op jit(solution)/shard_map/ppermute | solution.py:425
  92.3 0.0 all-to-all-done.1
  92.4 1.5 %collective-permute-done.4.cross_ref = bf16[512,512]{1,0:T(8,128)(2,1)S(1)} collective-permute-done((bf16[512,512]{1,0:T(8,128)(2,1)S(1)}, bf16[512,512]{1,0:T(8,128)(2,1)S(1)}, u32[]{:S(2)}, u32[]{:S(2)}) %collective-permute-start.4) | collective-permute-done | bytes 524320 | tf_op jit(solution)/shard_map/ppermute | solution.py:425
  93.9 1.7 %place.1 = bf16[512,2048]{1,0:T(8,128)(2,1)} custom-call(s32[2]{0:T(128)S(1)} %pad_add_fusion.flags_ref, bf16[512,512]{1,0:T(8,128)(2,1)S(1)} %collective-permute-done.4.cross_ref, bf16[512,1024]{1,0:T(8,128)(2,1)S(1)} %bitcast.7, bf16[512,2048]{1,0:T(8,128)(2,1)} %get-tuple-element.24._), custom_call_target="tpu_custom_call", output_to_operand_aliasing={{}: (3, {})} | custom-call | flops 1000000000 | bytes 16384 | tf_op jit(solution)/shard_map/place/pallas_call | solution.py:298
Async XLA Ops:
  0.0 11.9 %collective-permute-start = (bf16[512,2048]{1,0:T(8,128)(2,1)}, bf16[512,2048]{1,0:T(8,128)(2,1)}, u32[]{:S(2)}, u32[]{:S(2)}) collective-permute-start(bf16[512,2048]{1,0:T(8,128)(2,1)} %own_ref.1), channel_id=1, source_target_pairs={{0,1},{1,0},{2,3},{3,2},{4,5},{5,4},{6,7},{7,6},{8,9},{9,8},{10,11... | collective-permute-start | bytes 6291464 | tf_op jit(solution)/shard_map/ppermute | solution.py:425
  0.7 11.2 %copy-start = (bf16[512,2048]{1,0:T(8,128)(2,1)S(1)}, bf16[512,2048]{1,0:T(8,128)(2,1)}, u32[]{:S(2)}) copy-start(bf16[512,2048]{1,0:T(8,128)(2,1)} %own_ref.1) | copy-start | bytes 6291460
  0.7 40.3 %all-to-all-start = ((bf16[64,8,2048]{2,1,0:T(8,128)(2,1)}), bf16[64,8,2048]{2,1,0:T(8,128)(2,1)}, u32[]{:S(2)}, u32[]{:S(2)}) async-start(bf16[64,8,2048]{2,1,0:T(8,128)(2,1)} %bitcast.6), calls=%async_computation | async-start | bytes 4194304 | tf_op jit(solution)/shard_map/all_to_all | solution.py:418
  23.1 31.3 %collective-permute-start.2 = (bf16[1024,256]{1,0:T(8,128)(2,1)}, bf16[1024,256]{1,0:T(8,128)(2,1)S(1)}, u32[]{:S(2)}, u32[]{:S(2)}) collective-permute-start(bf16[1024,256]{1,0:T(8,128)(2,1)} %get-tuple-element.17.refs_2_), channel_id=1, source_target_pairs={{2,0},{3,1},{4,2},{5,3},{6,4},{7,5},{8,6},{9,7},{10,8},{11,9},{12,... | collective-permute-start | bytes 1572872 | tf_op jit(solution)/shard_map/ppermute | solution.py:435
  27.4 41.8 %collective-permute-start.1 = (bf16[2048,256]{1,0:T(8,128)(2,1)}, bf16[2048,256]{1,0:T(8,128)(2,1)}, u32[]{:S(2)}, u32[]{:S(2)}) collective-permute-start(bf16[2048,256]{1,0:T(8,128)(2,1)} %get-tuple-element.16.refs_1_), channel_id=1, source_target_pairs={{0,2},{1,3},{2,4},{3,5},{4,6},{5,7},{6,8},{7,9},{8,10},{9,11},{10,... | collective-permute-start | bytes 3145736 | tf_op jit(solution)/shard_map/ppermute | solution.py:428
  36.9 0.8 copy-start.1
  56.7 16.6 %collective-permute-start.3 = (bf16[272,1024]{1,0:T(8,128)(2,1)S(1)}, bf16[272,1024]{1,0:T(8,128)(2,1)S(1)}, u32[]{:S(2)}, u32[]{:S(2)}) collective-permute-start(bf16[272,1024]{1,0:T(8,128)(2,1)S(1)} %band_earlier.1), channel_id=1, source_target_pairs={{0,2},{1,3},{2,4},{3,5},{4,6},{5,7},{6,8},{7,9},{8,10},{9,11},{10,... | collective-permute-start | bytes 1671176 | tf_op jit(solution)/shard_map/ppermute | solution.py:428
  58.7 33.6 %all-to-all-start.1 = ((bf16[64,8,1024]{2,1,0:T(8,128)(2,1)}), bf16[64,8,1024]{2,1,0:T(8,128)(2,1)S(1)}, u32[]{:S(2)}, u32[]{:S(2)}) async-start(bf16[64,8,1024]{2,1,0:T(8,128)(2,1)} %bitcast.4), calls=%async_computation.1 | async-start | bytes 2097152 | tf_op jit(solution)/shard_map/all_to_all | solution.py:418
  73.3 1.0 %copy-start.2 = (bf16[1024,256]{1,0:T(8,128)(2,1)S(1)}, bf16[1024,256]{1,0:T(8,128)(2,1)}, u32[]{:S(2)}) copy-start(bf16[1024,256]{1,0:T(8,128)(2,1)} %copy-done.1) | copy-start | bytes 1572868
  79.9 14.0 %collective-permute-start.4 = (bf16[512,512]{1,0:T(8,128)(2,1)S(1)}, bf16[512,512]{1,0:T(8,128)(2,1)S(1)}, u32[]{:S(2)}, u32[]{:S(2)}) collective-permute-start(bf16[512,512]{1,0:T(8,128)(2,1)S(1)} %get-tuple-element.22), channel_id=1, source_target_pairs={{0,1},{1,0},{2,3},{3,2},{4,5},{5,4},{6,7},{7,6},{8,9},{9,8},{10,11... | collective-permute-start | bytes 1572872 | tf_op jit(solution)/shard_map/ppermute | solution.py:425

commit v10 on v8

--- a/solution.py
+++ b/solution.py
@@ -312,18 +312,15 @@
     )(flags, cross, col_out, result)
 
 
-def column_kernel(group, q_ref, k_ref, v_ref, o_ref, bias_ref):
-    parts = HALF // BLOCK
-    heads = q_ref.shape[1] // HEAD
-
-    @pl.when(pl.program_id(0) == 0)
-    def _():
-        qpos = lax.broadcasted_iota(jnp.int32, (BLOCK, BLOCK), 0)
-        kpos = lax.broadcasted_iota(jnp.int32, (BLOCK, BLOCK), 1)
-        column = ((qpos - kpos) & (group - 1)) == 0
-        bias_ref[0] = jnp.where(column, 0.0, NEG)
-        bias_ref[1] = jnp.where(column & (kpos <= qpos), 0.0, NEG)
-
+def column_bias(group, bias_ref):
+    qpos = lax.broadcasted_iota(jnp.int32, (BLOCK, BLOCK), 0)
+    kpos = lax.broadcasted_iota(jnp.int32, (BLOCK, BLOCK), 1)
+    column = ((qpos - kpos) & (group - 1)) == 0
+    bias_ref[0] = jnp.where(column, 0.0, NEG)
+    bias_ref[1] = jnp.where(column & (kpos <= qpos), 0.0, NEG)
+
+
+def column_attend(q_ref, k_ref, v_ref, bias_ref, o_ref):
     def rows(block):
         return slice(block * BLOCK, (block + 1) * BLOCK)
 
@@ -349,25 +346,79 @@
         out = out[:, :HEAD] * (1.0 / out[:, HEAD:])
         o_ref[rows(part), columns_of(head)] = out.astype(jnp.bfloat16)
 
-    pipelined([(part, head) for part in range(parts) for head in range(heads)], 4, start, finish)
-
-
-def column_attention(projected, group):
-    rows = projected.shape[0]
-    heads = 4
-    steps = HEADS // heads
-    spec = lambda third: pl.BlockSpec((rows, heads * HEAD), lambda j: (0, third * steps + j))
+    jobs = [(part, head) for part in range(HALF // BLOCK) for head in range(HEADS // 2)]
+    pipelined(jobs, 4, start, finish)
+
+
+def column_kernel(
+    group, x_hbm, w_hbm, o_ref, q_ref, k_ref, v_ref, x_ref, w_ref, bias_ref, sems, *projected
+):
+    width = HEADS // 2 * HEAD
+    load_x = pltpu.make_async_copy(x_hbm, x_ref, sems.at[6])
+    load_x.start()
+    loads = []
+    for index in range(6):
+        half, third = divmod(index, 3)
+        first = third * HEADS * HEAD + half * width
+        load = pltpu.make_async_copy(
+            w_hbm.at[:, first : first + width], w_ref.at[index], sems.at[index]
+        )
+        load.start()
+        loads.append(load)
+    column_bias(group, bias_ref)
+    load_x.wait()
+    for load, ref, block in zip(loads, projected + (q_ref, k_ref, v_ref), range(6)):
+        load.wait()
+        value = jnp.dot(x_ref[...], w_ref[block], preferred_element_type=jnp.float32)
+        ref[...] = value.astype(jnp.bfloat16)
+    column_attend(*projected, bias_ref, o_ref)
+
+
+def column_first(x, w_column, group):
+    rows, depth = x.shape
+    width = HEADS // 2 * HEAD
+    far = pl.BlockSpec(memory_space=pltpu.HBM)
+    half = pl.BlockSpec((rows, width), lambda j: (0, 0))
+    part = jax.ShapeDtypeStruct((rows, width), jnp.bfloat16)
     return pl.pallas_call(
         functools.partial(column_kernel, group),
-        grid=(steps,),
-        in_specs=[spec(0), spec(1), spec(2)],
-        out_specs=pl.BlockSpec((rows, heads * HEAD), lambda j: (0, j)),
-        out_shape=jax.ShapeDtypeStruct((rows, HEADS * HEAD), jnp.bfloat16),
+        grid=(1,),
+        in_specs=[far, far],
+        out_specs=[half] * 4,
+        out_shape=[jax.ShapeDtypeStruct((rows, HEADS * HEAD), jnp.bfloat16)] + [part] * 3,
+        scratch_shapes=[
+            pltpu.VMEM((rows, depth), jnp.bfloat16),
+            pltpu.VMEM((6, depth, width), jnp.bfloat16),
+            pltpu.VMEM((2, BLOCK, BLOCK), jnp.float32),
+            pltpu.SemaphoreType.DMA((7,)),
+        ]
+        + [pltpu.VMEM((rows, width), jnp.bfloat16)] * 3,
+        compiler_params=pltpu.CompilerParams(vmem_limit_bytes=44 << 20),
+        cost_estimate=cost(11),
+        name="column_first",
+    )(in_hbm(x), in_hbm(w_column))
+
+
+def column_rest_kernel(group, q_ref, k_ref, v_ref, _, o_ref, bias_ref):
+    column_bias(group, bias_ref)
+    column_attend(q_ref, k_ref, v_ref, bias_ref, o_ref)
+
+
+def column_rest(query, keys, values, first, group):
+    rows, width = query.shape
+    whole = pl.BlockSpec((rows, width), lambda j: (0, 0))
+    return pl.pallas_call(
+        functools.partial(column_rest_kernel, group),
+        grid=(1,),
+        in_specs=[whole] * 3 + [pl.BlockSpec(memory_space=pl.ANY)],
+        out_specs=pl.BlockSpec((rows, width), lambda j: (0, 1)),
+        out_shape=jax.ShapeDtypeStruct(first.shape, jnp.bfloat16),
+        input_output_aliases={3: 0},
         scratch_shapes=[pltpu.VMEM((2, BLOCK, BLOCK), jnp.float32)],
         compiler_params=params(),
         cost_estimate=cost(6),
-        name="column_attention",
-    )(projected, projected, projected)
+        name="column_rest",
+    )(query, keys, values, first)
 
 
 def in_hbm(value):
@@ -410,10 +461,10 @@
     next_q_b = lax.ppermute(q_b, "seq", [(d, d - 2) for d in range(2, count)])
     local = band_part(False, q_a, kv_a, q_b, kv_b, estimate=LOCAL_COST)
     columns = after(columns, local)
-    col_proj = jnp.dot(columns, w_column, preferred_element_type=jnp.float32).astype(jnp.bfloat16)
-    sent_b = band_part(True, after(next_q_b, col_proj), kv_b, estimate=B_COST)
+    col_first, *projected = column_first(columns, w_column, group)
+    sent_b = band_part(True, after(next_q_b, col_first), kv_b, estimate=B_COST)
     earlier_b = to_next(sent_b)
-    col_out = column_attention(after(col_proj, sent_b), group)
+    col_out = column_rest(after(projected[0], sent_b), *projected[1:], col_first, group)
     result, cross = complete(flags, q_a, after(previous_kv_a, col_out), in_hbm(local), earlier_b)
     return place(flags, swapped(cross), exchange(col_out), result)
 

time: 91.9 us -> 92 us (level)
  matrix products: 10.3 us -> 0 us
  Pallas kernels: 32.6 us -> 42.7 us
    dot_general x1 -> x0, matrix products: 10.3 us -> none  [on_device(): jnp.dot(columns, w_column, preferred_element_type=jnp.float32)]
    pallas_call x1 -> x2, Pallas kernels: 4.05 us -> 14.3 us  [the longest x1 12 us: column_first(): pl.pallas_call(functools.partial(column_kernel, group), grid=(1,), in_spe...]
  transfers between devices with their start and end apart: 7 -> 7, of which waited for: 2 -> 2; matrix products, arithmetic and copies ran while one was open for 11% -> 0% of each run, Pallas kernels for 34% -> 45%
where the time goes in v10:
time: 92 us; the launch traced here: 91.6 us
  Pallas kernels  42.7 us (46%)
  starting transfers between devices  32.3 us (35%)
  waiting for transfers between devices  15.4 us (17%)
    all_to_all x2, starting transfers between devices, exchange(): lax.all_to_all(value.reshape(chips, group, width), 'seq', split_axis=0, c...  22.5 us
    all_to_all x2, waiting for transfers between devices, exchange(): lax.all_to_all(value.reshape(chips, group, width), 'seq', split_axis=0, c...  15.4 us
    pallas_call x1, Pallas kernels, column_first(): pl.pallas_call(functools.partial(column_kernel, group), grid=(1,), in_spe...  12 us
    pallas_call x1, Pallas kernels, project(): pl.pallas_call(project_kernel, grid_spec=pltpu.PrefetchScalarGridSpec(num...  11.2 us
    pallas_call x2, Pallas kernels, band_part(): pl.pallas_call(functools.partial(band_kernel, earlier, pairs), grid=(pair...  9.86 us
    ppermute x2, starting transfers between devices, to_next(): return lax.ppermute(value, 'seq', [(d, d + 2) for d in range(count - 2)])  8.5 us
    pallas_call x1, Pallas kernels, complete(): pl.pallas_call(complete_kernel, grid_spec=pltpu.PrefetchScalarGridSpec(nu...  5.67 us
    pallas_call x1, Pallas kernels, column_rest(): pl.pallas_call(functools.partial(column_rest_kernel, group), grid=(1,), i...  2.29 us
  transfers between devices with their start and end apart: 7, of which 2 were waited for; matrix products, arithmetic and copies ran while one was open for 0% of the time, Pallas kernels for 45%

profile of v10, /device:TPU:0, one launch (start us, length us, event | category | flops | bytes accessed | tf_op | source)
XLA Modules:
  0.0 91.6 jit_solution(15277494036295121794)
XLA Ops:
  0.0 0.0 collective-permute-start
  0.0 0.0 copy-start
  0.0 11.9 %all-to-all-start = ((bf16[64,8,2048]{2,1,0:T(8,128)(2,1)}), bf16[64,8,2048]{2,1,0:T(8,128)(2,1)}, u32[]{:S(2)}, u32[]{:S(2)}) async-start(bf16[64,8,2048]{2,1,0:T(8,128)(2,1)} %bitcast.6), calls=%async_computation | async-start | bytes 4194304 | tf_op jit(solution)/shard_map/all_to_all | solution.py:444
  11.9 0.1 pad_add_fusion.flags_ref
  12.0 0.0 collective-permute-done.sibling_ref
  12.0 0.0 copy-done
  12.0 11.2 %project.1 = (bf16[2048,256]{1,0:T(8,128)(2,1)}, bf16[2048,256]{1,0:T(8,128)(2,1)S(1)}, bf16[1024,256]{1,0:T(8,128)(2,1)S(1)}, bf16[1024,256]{1,0:T(8,128)(2,1)}) custom-call(s32[1]{0:T(128)} %bitcast.core_ref, bf16[512,2048]{1,0:T(8,128)(2,1)S(1)} %copy-done, bf16[512,2048]{1,0:T(8,128)(2,1)} %collective-permute-done.sibling_ref, bf16[2048,3072]{1,0:T(8,128)(2,1)} %w_ref.1), custom_call_target="tpu_custom_call" | custom-call | flops 500000000 | bytes 16384 | tf_op jit(solution)/shard_map/project/pallas_call | solution.py:62
  23.2 1.3 %collective-permute-start.2 = (bf16[1024,256]{1,0:T(8,128)(2,1)}, bf16[1024,256]{1,0:T(8,128)(2,1)S(1)}, u32[]{:S(2)}, u32[]{:S(2)}) collective-permute-start(bf16[1024,256]{1,0:T(8,128)(2,1)} %get-tuple-element.21.refs_2_), channel_id=1, source_target_pairs={{2,0},{3,1},{4,2},{5,3},{6,4},{7,5},{8,6},{9,7},{10,8},{11,9},{12,... | collective-permute-start | bytes 1572872 | tf_op jit(solution)/shard_map/ppermute | solution.py:461
  24.5 5.6 %collective-permute-start.1 = (bf16[2048,256]{1,0:T(8,128)(2,1)}, bf16[2048,256]{1,0:T(8,128)(2,1)}, u32[]{:S(2)}, u32[]{:S(2)}) collective-permute-start(bf16[2048,256]{1,0:T(8,128)(2,1)} %get-tuple-element.20.refs_1_), channel_id=1, source_target_pairs={{0,2},{1,3},{2,4},{3,5},{4,6},{5,7},{6,8},{7,9},{8,10},{9,11},{10,... | collective-permute-start | bytes 3145736 | tf_op jit(solution)/shard_map/ppermute | solution.py:454
  30.1 7.6 %band_local.1.local_ref = bf16[544,1024]{1,0:T(8,128)(2,1)} custom-call(bf16[1024,256]{1,0:T(8,128)(2,1)S(1)} %get-tuple-element.19.refs_0_.q_ref, bf16[2048,256]{1,0:T(8,128)(2,1)} %get-tuple-element.20.refs_1_, bf16[1024,256]{1,0:T(8,128)(2,1)} %get-tuple-element.21.refs_2_, bf16[2048,256]{1,0:T(8,128)(2,1)S(1)} %get-tuple-element.22.refs_3_.refs_1_), custom_call_target="tpu_custom_call" | custom-call | flops 500000000 | bytes 16384 | tf_op jit(solution)/shard_map/band_local/pallas_call | solution.py:193
  37.6 0.0 copy-start.1
  37.6 0.8 copy-done.1
  38.5 3.3 %all-to-all-done = bf16[64,8,2048]{2,1,0:T(8,128)(2,1)} async-done(((bf16[64,8,2048]{2,1,0:T(8,128)(2,1)}), bf16[64,8,2048]{2,1,0:T(8,128)(2,1)}, u32[]{:S(2)}, u32[]{:S(2)}) %all-to-all-start) | async-done | bytes 2097184 | tf_op jit(solution)/shard_map/all_to_all | solution.py:444
  41.7 12.0 %column_first.1 = (bf16[512,1024]{1,0:T(8,128)(2,1)}, bf16[512,512]{1,0:T(8,128)(2,1)S(1)}, bf16[512,512]{1,0:T(8,128)(2,1)S(1)}, bf16[512,512]{1,0:T(8,128)(2,1)S(1)}) custom-call(bf16[512,2048]{1,0:T(8,128)(2,1)} %bitcast.3.x_hbm, bf16[2048,3072]{1,0:T(8,128)(2,1)} %w_hbm.1), custom_call_target="tpu_custom_call" | custom-call | flops 11000000512 | bytes 16384 | tf_op jit(solution)/shard_map/column_first/pallas_call | solution.py:383
  53.7 0.0 collective-permute-done.2.refs_0_
  53.7 2.3 %band_earlier.1 = bf16[272,1024]{1,0:T(8,128)(2,1)S(1)} custom-call(bf16[1024,256]{1,0:T(8,128)(2,1)S(1)} %collective-permute-done.2.refs_0_, bf16[2048,256]{1,0:T(8,128)(2,1)S(1)} %get-tuple-element.22.refs_3_.refs_1_), custom_call_target="tpu_custom_call" | custom-call | flops 500000000 | bytes 16384 | tf_op jit(solution)/shard_map/band_earlier/pallas_call | solution.py:193
  56.0 2.9 %collective-permute-start.3 = (bf16[272,1024]{1,0:T(8,128)(2,1)S(1)}, bf16[272,1024]{1,0:T(8,128)(2,1)S(1)}, u32[]{:S(2)}, u32[]{:S(2)}) collective-permute-start(bf16[272,1024]{1,0:T(8,128)(2,1)S(1)} %band_earlier.1), channel_id=1, source_target_pairs={{0,2},{1,3},{2,4},{3,5},{4,6},{5,7},{6,8},{7,9},{8,10},{9,11},{10,... | collective-permute-start | bytes 1671176 | tf_op jit(solution)/shard_map/ppermute | solution.py:454
  59.0 2.3 %column_rest.1 = bf16[512,1024]{1,0:T(8,128)(2,1)} custom-call(bf16[512,512]{1,0:T(8,128)(2,1)S(1)} %get-tuple-element.27.q_ref, bf16[512,512]{1,0:T(8,128)(2,1)S(1)} %get-tuple-element.28.k_ref, bf16[512,512]{1,0:T(8,128)(2,1)S(1)} %get-tuple-element.29.v_ref, bf16[512,1024]{1,0:T(8,128)(2,1)} %get-tuple-element.25._), custom_call_target="tpu_custom_call", output_to_operand_aliasing={{}: (3, {})} | custom-call | flops 6000000000 | bytes 16384 | tf_op jit(solution)/shard_map/column_rest/pallas_call | solution.py:410
  61.2 0.0 copy-start.2
  61.3 10.6 %all-to-all-start.1 = ((bf16[64,8,1024]{2,1,0:T(8,128)(2,1)}), bf16[64,8,1024]{2,1,0:T(8,128)(2,1)S(1)}, u32[]{:S(2)}, u32[]{:S(2)}) async-start(bf16[64,8,1024]{2,1,0:T(8,128)(2,1)} %bitcast.4), calls=%async_computation.1 | async-start | bytes 2097152 | tf_op jit(solution)/shard_map/all_to_all | solution.py:444
  71.9 0.0 collective-permute-done.1.kv_ref
  71.9 0.0 collective-permute-done.3.earlier_ref
  71.9 0.0 copy-done.2
  71.9 5.7 %complete.1 = (bf16[512,2048]{1,0:T(8,128)(2,1)}, bf16[512,512]{1,0:T(8,128)(2,1)}) custom-call(s32[2]{0:T(128)S(1)} %pad_add_fusion.flags_ref, bf16[1024,256]{1,0:T(8,128)(2,1)S(1)} %copy-done.2, bf16[2048,256]{1,0:T(8,128)(2,1)} %collective-permute-done.1.kv_ref, bf16[544,1024]{1,0:T(8,128)(2,1)} %band_local.1.local_ref, ...), custom_call_target="tpu_custom_call" | custom-call | flops 20000000000 | bytes 16384 | tf_op jit(solution)/shard_map/complete/pallas_call | solution.py:261
  77.6 0.0 collective-permute-start.4
  77.6 12.1 %all-to-all-done.1 = bf16[64,8,1024]{2,1,0:T(8,128)(2,1)S(1)} async-done(((bf16[64,8,1024]{2,1,0:T(8,128)(2,1)}), bf16[64,8,1024]{2,1,0:T(8,128)(2,1)S(1)}, u32[]{:S(2)}, u32[]{:S(2)}) %all-to-all-start.1) | async-done | bytes 1048608 | tf_op jit(solution)/shard_map/all_to_all | solution.py:444
  89.7 0.0 collective-permute-done.4.cross_ref
  89.7 1.7 %place.1 = bf16[512,2048]{1,0:T(8,128)(2,1)} custom-call(s32[2]{0:T(128)S(1)} %pad_add_fusion.flags_ref, bf16[512,512]{1,0:T(8,128)(2,1)S(1)} %collective-permute-done.4.cross_ref, bf16[512,1024]{1,0:T(8,128)(2,1)S(1)} %bitcast.7, bf16[512,2048]{1,0:T(8,128)(2,1)} %get-tuple-element.32._), custom_call_target="tpu_custom_call", output_to_operand_aliasing={{}: (3, {})} | custom-call | flops 1000000000 | bytes 16384 | tf_op jit(solution)/shard_map/place/pallas_call | solution.py:298
Async XLA Ops:
  0.0 12.0 %collective-permute-start = (bf16[512,2048]{1,0:T(8,128)(2,1)}, bf16[512,2048]{1,0:T(8,128)(2,1)}, u32[]{:S(2)}, u32[]{:S(2)}) collective-permute-start(bf16[512,2048]{1,0:T(8,128)(2,1)} %own_ref.1), channel_id=1, source_target_pairs={{0,1},{1,0},{2,3},{3,2},{4,5},{5,4},{6,7},{7,6},{8,9},{9,8},{10,11... | collective-permute-start | bytes 6291464 | tf_op jit(solution)/shard_map/ppermute | solution.py:451
  0.0 12.0 %copy-start = (bf16[512,2048]{1,0:T(8,128)(2,1)S(1)}, bf16[512,2048]{1,0:T(8,128)(2,1)}, u32[]{:S(2)}) copy-start(bf16[512,2048]{1,0:T(8,128)(2,1)} %own_ref.1) | copy-start | bytes 6291460
  0.0 41.7 %all-to-all-start = ((bf16[64,8,2048]{2,1,0:T(8,128)(2,1)}), bf16[64,8,2048]{2,1,0:T(8,128)(2,1)}, u32[]{:S(2)}, u32[]{:S(2)}) async-start(bf16[64,8,2048]{2,1,0:T(8,128)(2,1)} %bitcast.6), calls=%async_computation | async-start | bytes 4194304 | tf_op jit(solution)/shard_map/all_to_all | solution.py:444
  23.2 30.5 %collective-permute-start.2 = (bf16[1024,256]{1,0:T(8,128)(2,1)}, bf16[1024,256]{1,0:T(8,128)(2,1)S(1)}, u32[]{:S(2)}, u32[]{:S(2)}) collective-permute-start(bf16[1024,256]{1,0:T(8,128)(2,1)} %get-tuple-element.21.refs_2_), channel_id=1, source_target_pairs={{2,0},{3,1},{4,2},{5,3},{6,4},{7,5},{8,6},{9,7},{10,8},{11,9},{12,... | collective-permute-start | bytes 1572872 | tf_op jit(solution)/shard_map/ppermute | solution.py:461
  24.5 47.4 %collective-permute-start.1 = (bf16[2048,256]{1,0:T(8,128)(2,1)}, bf16[2048,256]{1,0:T(8,128)(2,1)}, u32[]{:S(2)}, u32[]{:S(2)}) collective-permute-start(bf16[2048,256]{1,0:T(8,128)(2,1)} %get-tuple-element.20.refs_1_), channel_id=1, source_target_pairs={{0,2},{1,3},{2,4},{3,5},{4,6},{5,7},{6,8},{7,9},{8,10},{9,11},{10,... | collective-permute-start | bytes 3145736 | tf_op jit(solution)/shard_map/ppermute | solution.py:454
  37.6 0.8 copy-start.1
  56.0 15.9 %collective-permute-start.3 = (bf16[272,1024]{1,0:T(8,128)(2,1)S(1)}, bf16[272,1024]{1,0:T(8,128)(2,1)S(1)}, u32[]{:S(2)}, u32[]{:S(2)}) collective-permute-start(bf16[272,1024]{1,0:T(8,128)(2,1)S(1)} %band_earlier.1), channel_id=1, source_target_pairs={{0,2},{1,3},{2,4},{3,5},{4,6},{5,7},{6,8},{7,9},{8,10},{9,11},{10,... | collective-permute-start | bytes 1671176 | tf_op jit(solution)/shard_map/ppermute | solution.py:454
  61.2 10.7 %copy-start.2 = (bf16[1024,256]{1,0:T(8,128)(2,1)S(1)}, bf16[1024,256]{1,0:T(8,128)(2,1)}, u32[]{:S(2)}) copy-start(bf16[1024,256]{1,0:T(8,128)(2,1)} %copy-done.1) | copy-start | bytes 1572868
  61.3 28.5 %all-to-all-start.1 = ((bf16[64,8,1024]{2,1,0:T(8,128)(2,1)}), bf16[64,8,1024]{2,1,0:T(8,128)(2,1)S(1)}, u32[]{:S(2)}, u32[]{:S(2)}) async-start(bf16[64,8,1024]{2,1,0:T(8,128)(2,1)} %bitcast.4), calls=%async_computation.1 | async-start | bytes 2097152 | tf_op jit(solution)/shard_map/all_to_all | solution.py:444
  77.6 12.1 %collective-permute-start.4 = (bf16[512,512]{1,0:T(8,128)(2,1)}, bf16[512,512]{1,0:T(8,128)(2,1)S(1)}, u32[]{:S(2)}, u32[]{:S(2)}) collective-permute-start(bf16[512,512]{1,0:T(8,128)(2,1)} %get-tuple-element.31), channel_id=1, source_target_pairs={{0,1},{1,0},{2,3},{3,2},{4,5},{5,4},{6,7},{7,6},{8,9},{9,8},{10,11... | collective-permute-start | bytes 1572872 | tf_op jit(solution)/shard_map/ppermute | solution.py:451

commit v11 on v8

--- a/solution.py
+++ b/solution.py
@@ -280,12 +280,19 @@
     )(flags, *inputs)
 
 
-def place_kernel(flags_ref, cross_ref, columns_ref, _, o_ref, sems):
-    first = pl.multiple_of((1 - flags_ref[0]) * HALF, HALF)
-    width = columns_ref.shape[1]
+def place_kernel(flags_ref, values_ref, _, o_ref, sems, *, cross):
+    width = values_ref.shape[1]
+    if cross:
+        first = pl.multiple_of((1 - flags_ref[0]) * HALF, HALF)
+    else:
+        first = width
+    count = sems.shape[0]
+    rows = [pl.ds(index * (HALF // count), HALF // count) for index in range(count)]
     copies = [
-        pltpu.make_async_copy(cross_ref, o_ref.at[:, pl.ds(first, HALF)], sems.at[0]),
-        pltpu.make_async_copy(columns_ref, o_ref.at[:, pl.ds(width, width)], sems.at[1]),
+        pltpu.make_async_copy(
+            values_ref.at[part, :], o_ref.at[part, pl.ds(first, width)], sems.at[index]
+        )
+        for index, part in enumerate(rows)
     ]
     for copy in copies:
         copy.start()
@@ -293,23 +300,23 @@
         copy.wait()
 
 
-def place(flags, cross, col_out, result):
+def place(flags, values, result, cross):
     anywhere = pl.BlockSpec(memory_space=pl.ANY)
     return pl.pallas_call(
-        place_kernel,
+        functools.partial(place_kernel, cross=cross),
         grid_spec=pltpu.PrefetchScalarGridSpec(
             num_scalar_prefetch=1,
             grid=(1,),
-            in_specs=[anywhere] * 3,
+            in_specs=[anywhere] * 2,
             out_specs=anywhere,
-            scratch_shapes=[pltpu.SemaphoreType.DMA((2,))],
+            scratch_shapes=[pltpu.SemaphoreType.DMA((8,))],
         ),
         out_shape=jax.ShapeDtypeStruct(result.shape, jnp.bfloat16),
-        input_output_aliases={3: 0},
+        input_output_aliases={2: 0},
         compiler_params=params(),
         cost_estimate=cost(1),
-        name="place",
-    )(flags, cross, col_out, result)
+        name="place_cross" if cross else "place_columns",
+    )(flags, values, result)
 
 
 def column_kernel(group, q_ref, k_ref, v_ref, o_ref, bias_ref):
@@ -415,7 +422,8 @@
     earlier_b = to_next(sent_b)
     col_out = column_attention(after(col_proj, sent_b), group)
     result, cross = complete(flags, q_a, after(previous_kv_a, col_out), in_hbm(local), earlier_b)
-    return place(flags, swapped(cross), exchange(col_out), result)
+    result = place(flags, swapped(cross), result, True)
+    return place(flags, exchange(col_out), result, False)
 
 
 def solution(mesh):

time: 91.9 us -> 92 us (level)
  waiting for transfers between devices: 15.1 us -> 13.6 us
  Pallas kernels: 32.6 us -> 33.9 us
    all_to_all x2, waiting for transfers between devices: 15.1 us -> 11.7 us  [exchange(): lax.all_to_all(value.reshape(chips, group, width), 'seq', split_axis=0, c...]
    ppermute x2, waiting for transfers between devices: 0.01 us -> 1.91 us  [swapped(): return lax.ppermute(value, 'seq', [(d, d ^ 1) for d in range(count)])]
    pallas_call x1 -> x2, Pallas kernels: 1.7 us -> 2.95 us  [place(): pl.pallas_call(functools.partial(place_kernel, cross=cross), grid_spec=pl...]
  transfers between devices with their start and end apart: 7 -> 7, of which waited for: 2 -> 3; matrix products, arithmetic and copies ran while one was open for 11% -> 11% of each run, Pallas kernels for 34% -> 35%
where the time goes in v11:
time: 92 us; the launch traced here: 91.6 us
  Pallas kernels  33.9 us (37%)
  starting transfers between devices  32.6 us (35%)
  waiting for transfers between devices  13.6 us (15%)
  matrix products  10.3 us (11%)
    all_to_all x2, starting transfers between devices, exchange(): lax.all_to_all(value.reshape(chips, group, width), 'seq', split_axis=0, c...  23 us
    all_to_all x2, waiting for transfers between devices, exchange(): lax.all_to_all(value.reshape(chips, group, width), 'seq', split_axis=0, c...  11.7 us
    pallas_call x1, Pallas kernels, project(): pl.pallas_call(project_kernel, grid_spec=pltpu.PrefetchScalarGridSpec(num...  11.4 us
    dot_general x1, matrix products, on_device(): jnp.dot(columns, w_column, preferred_element_type=jnp.float32)  10.3 us
    pallas_call x2, Pallas kernels, band_part(): pl.pallas_call(functools.partial(band_kernel, earlier, pairs), grid=(pair...  9.95 us
    ppermute x2, starting transfers between devices, to_next(): return lax.ppermute(value, 'seq', [(d, d + 2) for d in range(count - 2)])  8.28 us
    pallas_call x1, Pallas kernels, complete(): pl.pallas_call(complete_kernel, grid_spec=pltpu.PrefetchScalarGridSpec(nu...  5.54 us
    pallas_call x1, Pallas kernels, column_attention(): pl.pallas_call(functools.partial(column_kernel, group), grid=(steps,), in...  4.05 us
  transfers between devices with their start and end apart: 7, of which 3 were waited for; matrix products, arithmetic and copies ran while one was open for 11% of the time, Pallas kernels for 35%

profile of v11, /device:TPU:0, one launch (start us, length us, event | category | flops | bytes accessed | tf_op | source)
XLA Modules:
  0.0 91.6 jit_solution(8849513045246227456)
XLA Ops:
  0.0 0.0 collective-permute-start
  0.0 0.0 copy-start
  0.0 11.9 %all-to-all-start = ((bf16[64,8,2048]{2,1,0:T(8,128)(2,1)}), bf16[64,8,2048]{2,1,0:T(8,128)(2,1)}, u32[]{:S(2)}, u32[]{:S(2)}) async-start(bf16[64,8,2048]{2,1,0:T(8,128)(2,1)} %bitcast.8), calls=%async_computation | async-start | bytes 4194304 | tf_op jit(solution)/shard_map/all_to_all | solution.py:400
  11.9 0.1 pad_add_fusion.flags_ref
  12.0 0.0 collective-permute-done.sibling_ref
  12.0 0.0 copy-done
  12.0 11.4 %project.1 = (bf16[2048,256]{1,0:T(8,128)(2,1)}, bf16[2048,256]{1,0:T(8,128)(2,1)S(1)}, bf16[1024,256]{1,0:T(8,128)(2,1)S(1)}, bf16[1024,256]{1,0:T(8,128)(2,1)}) custom-call(s32[1]{0:T(128)} %bitcast.core_ref, bf16[512,2048]{1,0:T(8,128)(2,1)S(1)} %copy-done, bf16[512,2048]{1,0:T(8,128)(2,1)} %collective-permute-done.sibling_ref, bf16[2048,3072]{1,0:T(8,128)(2,1)} %w_ref.1), custom_call_target="tpu_custom_call" | custom-call | flops 500000000 | bytes 16384 | tf_op jit(solution)/shard_map/project/pallas_call | solution.py:62
  23.5 1.3 %collective-permute-start.1 = (bf16[1024,256]{1,0:T(8,128)(2,1)}, bf16[1024,256]{1,0:T(8,128)(2,1)S(1)}, u32[]{:S(2)}, u32[]{:S(2)}) collective-permute-start(bf16[1024,256]{1,0:T(8,128)(2,1)} %get-tuple-element.17.refs_2_), channel_id=1, source_target_pairs={{2,0},{3,1},{4,2},{5,3},{6,4},{7,5},{8,6},{9,7},{10,8},{11,9},{12,... | collective-permute-start | bytes 1572872 | tf_op jit(solution)/shard_map/ppermute | solution.py:417
  24.7 5.6 %collective-permute-start.2 = (bf16[2048,256]{1,0:T(8,128)(2,1)}, bf16[2048,256]{1,0:T(8,128)(2,1)}, u32[]{:S(2)}, u32[]{:S(2)}) collective-permute-start(bf16[2048,256]{1,0:T(8,128)(2,1)} %get-tuple-element.16.refs_1_), channel_id=1, source_target_pairs={{0,2},{1,3},{2,4},{3,5},{4,6},{5,7},{6,8},{7,9},{8,10},{9,11},{10,... | collective-permute-start | bytes 3145736 | tf_op jit(solution)/shard_map/ppermute | solution.py:410
  30.3 7.6 %band_local.1.local_ref = bf16[544,1024]{1,0:T(8,128)(2,1)} custom-call(bf16[1024,256]{1,0:T(8,128)(2,1)S(1)} %get-tuple-element.15.refs_0_.q_ref, bf16[2048,256]{1,0:T(8,128)(2,1)} %get-tuple-element.16.refs_1_, bf16[1024,256]{1,0:T(8,128)(2,1)} %get-tuple-element.17.refs_2_, bf16[2048,256]{1,0:T(8,128)(2,1)S(1)} %get-tuple-element.18.refs_3_.refs_1_), custom_call_target="tpu_custom_call" | custom-call | flops 500000000 | bytes 16384 | tf_op jit(solution)/shard_map/band_local/pallas_call | solution.py:193
  37.9 0.0 copy-start.1
  37.9 0.8 copy-done.1
  38.7 3.0 %all-to-all-done = bf16[64,8,2048]{2,1,0:T(8,128)(2,1)} async-done(((bf16[64,8,2048]{2,1,0:T(8,128)(2,1)}), bf16[64,8,2048]{2,1,0:T(8,128)(2,1)}, u32[]{:S(2)}, u32[]{:S(2)}) %all-to-all-start) | async-done | bytes 2097184 | tf_op jit(solution)/shard_map/all_to_all | solution.py:400
  41.7 10.3 %convolution_convert_fusion.q_ref.k_ref.v_ref = bf16[512,3072]{1,0:T(8,128)(2,1)S(1)} fusion(bf16[512,2048]{1,0:T(8,128)(2,1)} %bitcast.3, bf16[2048,3072]{1,0:T(8,128)(2,1)} %param.5), kind=kOutput, calls=%fused_computation | convolution fusion | flops 6444023808 | bytes 17825792 | tf_op jit(solution)/shard_map/dot_general | solution.py:420
  52.0 0.0 collective-permute-done.1.refs_0_
  52.0 2.3 %band_earlier.1 = bf16[272,1024]{1,0:T(8,128)(2,1)S(1)} custom-call(bf16[1024,256]{1,0:T(8,128)(2,1)S(1)} %collective-permute-done.1.refs_0_, bf16[2048,256]{1,0:T(8,128)(2,1)S(1)} %get-tuple-element.18.refs_3_.refs_1_), custom_call_target="tpu_custom_call" | custom-call | flops 500000000 | bytes 16384 | tf_op jit(solution)/shard_map/band_earlier/pallas_call | solution.py:193
  54.4 2.7 %collective-permute-start.3 = (bf16[272,1024]{1,0:T(8,128)(2,1)S(1)}, bf16[272,1024]{1,0:T(8,128)(2,1)S(1)}, u32[]{:S(2)}, u32[]{:S(2)}) collective-permute-start(bf16[272,1024]{1,0:T(8,128)(2,1)S(1)} %band_earlier.1), channel_id=1, source_target_pairs={{0,2},{1,3},{2,4},{3,5},{4,6},{5,7},{6,8},{7,9},{8,10},{9,11},{10,... | collective-permute-start | bytes 1671176 | tf_op jit(solution)/shard_map/ppermute | solution.py:410
  57.1 4.1 %column_attention.1 = bf16[512,1024]{1,0:T(8,128)(2,1)} custom-call(bf16[512,3072]{1,0:T(8,128)(2,1)S(1)} %convolution_convert_fusion.q_ref.k_ref.v_ref, bf16[512,3072]{1,0:T(8,128)(2,1)S(1)} %convolution_convert_fusion.q_ref.k_ref.v_ref, bf16[512,3072]{1,0:T(8,128)(2,1)S(1)} %convolution_convert_fusion.q_ref.k_ref.v_ref), custom_call_target="tpu_custom_call" | custom-call | flops 6000000000 | bytes 16384 | tf_op jit(solution)/shard_map/column_attention/pallas_call | solution.py:367
  61.1 0.0 copy-start.2
  61.1 11.1 %all-to-all-start.1 = ((bf16[64,8,1024]{2,1,0:T(8,128)(2,1)}), bf16[64,8,1024]{2,1,0:T(8,128)(2,1)S(1)}, u32[]{:S(2)}, u32[]{:S(2)}) async-start(bf16[64,8,1024]{2,1,0:T(8,128)(2,1)} %bitcast.4), calls=%async_computation.1 | async-start | bytes 2097152 | tf_op jit(solution)/shard_map/all_to_all | solution.py:400
  72.3 0.0 collective-permute-done.2.kv_ref
  72.3 0.0 collective-permute-done.3.earlier_ref
  72.3 0.0 copy-done.2
  72.3 5.5 %complete.1 = (bf16[512,2048]{1,0:T(8,128)(2,1)}, bf16[512,512]{1,0:T(8,128)(2,1)S(1)}) custom-call(s32[2]{0:T(128)S(1)} %pad_add_fusion.flags_ref, bf16[1024,256]{1,0:T(8,128)(2,1)S(1)} %copy-done.2, bf16[2048,256]{1,0:T(8,128)(2,1)} %collective-permute-done.2.kv_ref, bf16[544,1024]{1,0:T(8,128)(2,1)} %band_local.1.local_ref, ...), custom_call_target="tpu_custom_call" | custom-call | flops 20000000000 | bytes 16384 | tf_op jit(solution)/shard_map/complete/pallas_call | solution.py:261
  77.8 0.0 collective-permute-start.4
  77.8 1.9 %collective-permute-done.4.values_ref = bf16[512,512]{1,0:T(8,128)(2,1)S(1)} collective-permute-done((bf16[512,512]{1,0:T(8,128)(2,1)S(1)}, bf16[512,512]{1,0:T(8,128)(2,1)S(1)}, u32[]{:S(2)}, u32[]{:S(2)}) %collective-permute-start.4) | collective-permute-done | bytes 524320 | tf_op jit(solution)/shard_map/ppermute | solution.py:407
  79.8 1.4 %place_cross.1._ = bf16[512,2048]{1,0:T(8,128)(2,1)} custom-call(s32[2]{0:T(128)S(1)} %pad_add_fusion.flags_ref, bf16[512,512]{1,0:T(8,128)(2,1)S(1)} %collective-permute-done.4.values_ref, bf16[512,2048]{1,0:T(8,128)(2,1)} %get-tuple-element.24._), custom_call_target="tpu_custom_call", output_to_operand_aliasing={{}: (2, {})} | custom-call | flops 1000000000 | bytes 16384 | tf_op jit(solution)/shard_map/place_cross/pallas_call | solution.py:305
  81.2 8.7 %all-to-all-done.1 = bf16[64,8,1024]{2,1,0:T(8,128)(2,1)S(1)} async-done(((bf16[64,8,1024]{2,1,0:T(8,128)(2,1)}), bf16[64,8,1024]{2,1,0:T(8,128)(2,1)S(1)}, u32[]{:S(2)}, u32[]{:S(2)}) %all-to-all-start.1) | async-done | bytes 1048608 | tf_op jit(solution)/shard_map/all_to_all | solution.py:400
  89.9 1.6 %place_columns.1 = bf16[512,2048]{1,0:T(8,128)(2,1)} custom-call(s32[2]{0:T(128)S(1)} %pad_add_fusion.flags_ref, bf16[512,1024]{1,0:T(8,128)(2,1)S(1)} %bitcast.9, bf16[512,2048]{1,0:T(8,128)(2,1)} %place_cross.1._), custom_call_target="tpu_custom_call", output_to_operand_aliasing={{}: (2, {})} | custom-call | flops 1000000000 | bytes 16384 | tf_op jit(solution)/shard_map/place_columns/pallas_call | solution.py:305
Async XLA Ops:
  0.0 12.0 %collective-permute-start = (bf16[512,2048]{1,0:T(8,128)(2,1)}, bf16[512,2048]{1,0:T(8,128)(2,1)}, u32[]{:S(2)}, u32[]{:S(2)}) collective-permute-start(bf16[512,2048]{1,0:T(8,128)(2,1)} %own_ref.1), channel_id=1, source_target_pairs={{0,1},{1,0},{2,3},{3,2},{4,5},{5,4},{6,7},{7,6},{8,9},{9,8},{10,11... | collective-permute-start | bytes 6291464 | tf_op jit(solution)/shard_map/ppermute | solution.py:407
  0.0 12.0 %copy-start = (bf16[512,2048]{1,0:T(8,128)(2,1)S(1)}, bf16[512,2048]{1,0:T(8,128)(2,1)}, u32[]{:S(2)}) copy-start(bf16[512,2048]{1,0:T(8,128)(2,1)} %own_ref.1) | copy-start | bytes 6291460
  0.0 41.7 %all-to-all-start = ((bf16[64,8,2048]{2,1,0:T(8,128)(2,1)}), bf16[64,8,2048]{2,1,0:T(8,128)(2,1)}, u32[]{:S(2)}, u32[]{:S(2)}) async-start(bf16[64,8,2048]{2,1,0:T(8,128)(2,1)} %bitcast.8), calls=%async_computation | async-start | bytes 4194304 | tf_op jit(solution)/shard_map/all_to_all | solution.py:400
  23.5 28.6 %collective-permute-start.1 = (bf16[1024,256]{1,0:T(8,128)(2,1)}, bf16[1024,256]{1,0:T(8,128)(2,1)S(1)}, u32[]{:S(2)}, u32[]{:S(2)}) collective-permute-start(bf16[1024,256]{1,0:T(8,128)(2,1)} %get-tuple-element.17.refs_2_), channel_id=1, source_target_pairs={{2,0},{3,1},{4,2},{5,3},{6,4},{7,5},{8,6},{9,7},{10,8},{11,9},{12,... | collective-permute-start | bytes 1572872 | tf_op jit(solution)/shard_map/ppermute | solution.py:417
  24.7 47.5 %collective-permute-start.2 = (bf16[2048,256]{1,0:T(8,128)(2,1)}, bf16[2048,256]{1,0:T(8,128)(2,1)}, u32[]{:S(2)}, u32[]{:S(2)}) collective-permute-start(bf16[2048,256]{1,0:T(8,128)(2,1)} %get-tuple-element.16.refs_1_), channel_id=1, source_target_pairs={{0,2},{1,3},{2,4},{3,5},{4,6},{5,7},{6,8},{7,9},{8,10},{9,11},{10,... | collective-permute-start | bytes 3145736 | tf_op jit(solution)/shard_map/ppermute | solution.py:410
  37.9 0.8 copy-start.1
  54.4 17.9 %collective-permute-start.3 = (bf16[272,1024]{1,0:T(8,128)(2,1)S(1)}, bf16[272,1024]{1,0:T(8,128)(2,1)S(1)}, u32[]{:S(2)}, u32[]{:S(2)}) collective-permute-start(bf16[272,1024]{1,0:T(8,128)(2,1)S(1)} %band_earlier.1), channel_id=1, source_target_pairs={{0,2},{1,3},{2,4},{3,5},{4,6},{5,7},{6,8},{7,9},{8,10},{9,11},{10,... | collective-permute-start | bytes 1671176 | tf_op jit(solution)/shard_map/ppermute | solution.py:410
  61.1 11.1 %copy-start.2 = (bf16[1024,256]{1,0:T(8,128)(2,1)S(1)}, bf16[1024,256]{1,0:T(8,128)(2,1)}, u32[]{:S(2)}) copy-start(bf16[1024,256]{1,0:T(8,128)(2,1)} %copy-done.1) | copy-start | bytes 1572868
  61.1 28.7 %all-to-all-start.1 = ((bf16[64,8,1024]{2,1,0:T(8,128)(2,1)}), bf16[64,8,1024]{2,1,0:T(8,128)(2,1)S(1)}, u32[]{:S(2)}, u32[]{:S(2)}) async-start(bf16[64,8,1024]{2,1,0:T(8,128)(2,1)} %bitcast.4), calls=%async_computation.1 | async-start | bytes 2097152 | tf_op jit(solution)/shard_map/all_to_all | solution.py:400
  77.8 1.9 %collective-permute-start.4 = (bf16[512,512]{1,0:T(8,128)(2,1)S(1)}, bf16[512,512]{1,0:T(8,128)(2,1)S(1)}, u32[]{:S(2)}, u32[]{:S(2)}) collective-permute-start(bf16[512,512]{1,0:T(8,128)(2,1)S(1)} %get-tuple-element.23), channel_id=1, source_target_pairs={{0,1},{1,0},{2,3},{3,2},{4,5},{5,4},{6,7},{7,6},{8,9},{9,8},{10,11... | collective-permute-start | bytes 1572872 | tf_op jit(solution)/shard_map/ppermute | solution.py:407

commit v12 on v11

--- a/solution.py
+++ b/solution.py
@@ -361,7 +361,7 @@
 
 def column_attention(projected, group):
     rows = projected.shape[0]
-    heads = 4
+    heads = 8
     steps = HEADS // heads
     spec = lambda third: pl.BlockSpec((rows, heads * HEAD), lambda j: (0, third * steps + j))
     return pl.pallas_call(

time: 92 us -> 91.4 us (level)
  no operation moved by 1% of the time
where the time goes in v12:
time: 91.4 us; the launch traced here: 91 us
  Pallas kernels  33.3 us (36%)
  starting transfers between devices  32.6 us (36%)
  waiting for transfers between devices  13.6 us (15%)
  matrix products  10.3 us (11%)
    all_to_all x2, starting transfers between devices, exchange(): lax.all_to_all(value.reshape(chips, group, width), 'seq', split_axis=0, c...  23 us
    all_to_all x2, waiting for transfers between devices, exchange(): lax.all_to_all(value.reshape(chips, group, width), 'seq', split_axis=0, c...  11.7 us
    pallas_call x1, Pallas kernels, project(): pl.pallas_call(project_kernel, grid_spec=pltpu.PrefetchScalarGridSpec(num...  11.4 us
    dot_general x1, matrix products, on_device(): jnp.dot(columns, w_column, preferred_element_type=jnp.float32)  10.3 us
    pallas_call x2, Pallas kernels, band_part(): pl.pallas_call(functools.partial(band_kernel, earlier, pairs), grid=(pair...  9.95 us
    ppermute x2, starting transfers between devices, to_next(): return lax.ppermute(value, 'seq', [(d, d + 2) for d in range(count - 2)])  8.28 us
    pallas_call x1, Pallas kernels, complete(): pl.pallas_call(complete_kernel, grid_spec=pltpu.PrefetchScalarGridSpec(nu...  5.54 us
    pallas_call x1, Pallas kernels, column_attention(): pl.pallas_call(functools.partial(column_kernel, group), grid=(steps,), in...  3.42 us
  transfers between devices with their start and end apart: 7, of which 3 were waited for; matrix products, arithmetic and copies ran while one was open for 11% of the time, Pallas kernels for 35%

profile of v12, /device:TPU:0, one launch (start us, length us, event | category | flops | bytes accessed | tf_op | source)
XLA Modules:
  0.0 91.0 jit_solution(16303111296509840305)
XLA Ops:
  0.0 0.0 collective-permute-start
  0.0 0.0 copy-start
  0.0 11.9 %all-to-all-start = ((bf16[64,8,2048]{2,1,0:T(8,128)(2,1)}), bf16[64,8,2048]{2,1,0:T(8,128)(2,1)}, u32[]{:S(2)}, u32[]{:S(2)}) async-start(bf16[64,8,2048]{2,1,0:T(8,128)(2,1)} %bitcast.8), calls=%async_computation | async-start | bytes 4194304 | tf_op jit(solution)/shard_map/all_to_all | solution.py:400
  11.9 0.1 pad_add_fusion.flags_ref
  12.0 0.0 collective-permute-done.sibling_ref
  12.0 0.0 copy-done
  12.0 11.4 %project.1 = (bf16[2048,256]{1,0:T(8,128)(2,1)}, bf16[2048,256]{1,0:T(8,128)(2,1)S(1)}, bf16[1024,256]{1,0:T(8,128)(2,1)S(1)}, bf16[1024,256]{1,0:T(8,128)(2,1)}) custom-call(s32[1]{0:T(128)} %bitcast.core_ref, bf16[512,2048]{1,0:T(8,128)(2,1)S(1)} %copy-done, bf16[512,2048]{1,0:T(8,128)(2,1)} %collective-permute-done.sibling_ref, bf16[2048,3072]{1,0:T(8,128)(2,1)} %w_ref.1), custom_call_target="tpu_custom_call" | custom-call | flops 500000000 | bytes 16384 | tf_op jit(solution)/shard_map/project/pallas_call | solution.py:62
  23.5 1.3 %collective-permute-start.1 = (bf16[1024,256]{1,0:T(8,128)(2,1)}, bf16[1024,256]{1,0:T(8,128)(2,1)S(1)}, u32[]{:S(2)}, u32[]{:S(2)}) collective-permute-start(bf16[1024,256]{1,0:T(8,128)(2,1)} %get-tuple-element.17.refs_2_), channel_id=1, source_target_pairs={{2,0},{3,1},{4,2},{5,3},{6,4},{7,5},{8,6},{9,7},{10,8},{11,9},{12,... | collective-permute-start | bytes 1572872 | tf_op jit(solution)/shard_map/ppermute | solution.py:417
  24.7 5.6 %collective-permute-start.2 = (bf16[2048,256]{1,0:T(8,128)(2,1)}, bf16[2048,256]{1,0:T(8,128)(2,1)}, u32[]{:S(2)}, u32[]{:S(2)}) collective-permute-start(bf16[2048,256]{1,0:T(8,128)(2,1)} %get-tuple-element.16.refs_1_), channel_id=1, source_target_pairs={{0,2},{1,3},{2,4},{3,5},{4,6},{5,7},{6,8},{7,9},{8,10},{9,11},{10,... | collective-permute-start | bytes 3145736 | tf_op jit(solution)/shard_map/ppermute | solution.py:410
  30.3 7.6 %band_local.1.local_ref = bf16[544,1024]{1,0:T(8,128)(2,1)} custom-call(bf16[1024,256]{1,0:T(8,128)(2,1)S(1)} %get-tuple-element.15.refs_0_.q_ref, bf16[2048,256]{1,0:T(8,128)(2,1)} %get-tuple-element.16.refs_1_, bf16[1024,256]{1,0:T(8,128)(2,1)} %get-tuple-element.17.refs_2_, bf16[2048,256]{1,0:T(8,128)(2,1)S(1)} %get-tuple-element.18.refs_3_.refs_1_), custom_call_target="tpu_custom_call" | custom-call | flops 500000000 | bytes 16384 | tf_op jit(solution)/shard_map/band_local/pallas_call | solution.py:193
  37.9 0.0 copy-start.1
  37.9 0.8 copy-done.1
  38.7 3.0 %all-to-all-done = bf16[64,8,2048]{2,1,0:T(8,128)(2,1)} async-done(((bf16[64,8,2048]{2,1,0:T(8,128)(2,1)}), bf16[64,8,2048]{2,1,0:T(8,128)(2,1)}, u32[]{:S(2)}, u32[]{:S(2)}) %all-to-all-start) | async-done | bytes 2097184 | tf_op jit(solution)/shard_map/all_to_all | solution.py:400
  41.7 10.3 %convolution_convert_fusion.q_ref.k_ref.v_ref = bf16[512,3072]{1,0:T(8,128)(2,1)S(1)} fusion(bf16[512,2048]{1,0:T(8,128)(2,1)} %bitcast.3, bf16[2048,3072]{1,0:T(8,128)(2,1)} %param.5), kind=kOutput, calls=%fused_computation | convolution fusion | flops 6444023808 | bytes 17825792 | tf_op jit(solution)/shard_map/dot_general | solution.py:420
  52.0 0.0 collective-permute-done.1.refs_0_
  52.0 2.3 %band_earlier.1 = bf16[272,1024]{1,0:T(8,128)(2,1)S(1)} custom-call(bf16[1024,256]{1,0:T(8,128)(2,1)S(1)} %collective-permute-done.1.refs_0_, bf16[2048,256]{1,0:T(8,128)(2,1)S(1)} %get-tuple-element.18.refs_3_.refs_1_), custom_call_target="tpu_custom_call" | custom-call | flops 500000000 | bytes 16384 | tf_op jit(solution)/shard_map/band_earlier/pallas_call | solution.py:193
  54.4 2.7 %collective-permute-start.3 = (bf16[272,1024]{1,0:T(8,128)(2,1)S(1)}, bf16[272,1024]{1,0:T(8,128)(2,1)S(1)}, u32[]{:S(2)}, u32[]{:S(2)}) collective-permute-start(bf16[272,1024]{1,0:T(8,128)(2,1)S(1)} %band_earlier.1), channel_id=1, source_target_pairs={{0,2},{1,3},{2,4},{3,5},{4,6},{5,7},{6,8},{7,9},{8,10},{9,11},{10,... | collective-permute-start | bytes 1671176 | tf_op jit(solution)/shard_map/ppermute | solution.py:410
  57.1 3.4 %column_attention.1 = bf16[512,1024]{1,0:T(8,128)(2,1)} custom-call(bf16[512,3072]{1,0:T(8,128)(2,1)S(1)} %convolution_convert_fusion.q_ref.k_ref.v_ref, bf16[512,3072]{1,0:T(8,128)(2,1)S(1)} %convolution_convert_fusion.q_ref.k_ref.v_ref, bf16[512,3072]{1,0:T(8,128)(2,1)S(1)} %convolution_convert_fusion.q_ref.k_ref.v_ref), custom_call_target="tpu_custom_call" | custom-call | flops 6000000000 | bytes 16384 | tf_op jit(solution)/shard_map/column_attention/pallas_call | solution.py:367
  60.5 0.0 copy-start.2
  60.5 11.1 %all-to-all-start.1 = ((bf16[64,8,1024]{2,1,0:T(8,128)(2,1)}), bf16[64,8,1024]{2,1,0:T(8,128)(2,1)S(1)}, u32[]{:S(2)}, u32[]{:S(2)}) async-start(bf16[64,8,1024]{2,1,0:T(8,128)(2,1)} %bitcast.4), calls=%async_computation.1 | async-start | bytes 2097152 | tf_op jit(solution)/shard_map/all_to_all | solution.py:400
  71.6 0.0 collective-permute-done.2.kv_ref
  71.7 0.0 collective-permute-done.3.earlier_ref
  71.7 0.0 copy-done.2
  71.7 5.5 %complete.1 = (bf16[512,2048]{1,0:T(8,128)(2,1)}, bf16[512,512]{1,0:T(8,128)(2,1)S(1)}) custom-call(s32[2]{0:T(128)S(1)} %pad_add_fusion.flags_ref, bf16[1024,256]{1,0:T(8,128)(2,1)S(1)} %copy-done.2, bf16[2048,256]{1,0:T(8,128)(2,1)} %collective-permute-done.2.kv_ref, bf16[544,1024]{1,0:T(8,128)(2,1)} %band_local.1.local_ref, ...), custom_call_target="tpu_custom_call" | custom-call | flops 20000000000 | bytes 16384 | tf_op jit(solution)/shard_map/complete/pallas_call | solution.py:261
  77.2 0.0 collective-permute-start.4
  77.2 1.9 %collective-permute-done.4.values_ref = bf16[512,512]{1,0:T(8,128)(2,1)S(1)} collective-permute-done((bf16[512,512]{1,0:T(8,128)(2,1)S(1)}, bf16[512,512]{1,0:T(8,128)(2,1)S(1)}, u32[]{:S(2)}, u32[]{:S(2)}) %collective-permute-start.4) | collective-permute-done | bytes 524320 | tf_op jit(solution)/shard_map/ppermute | solution.py:407
  79.1 1.4 %place_cross.1._ = bf16[512,2048]{1,0:T(8,128)(2,1)} custom-call(s32[2]{0:T(128)S(1)} %pad_add_fusion.flags_ref, bf16[512,512]{1,0:T(8,128)(2,1)S(1)} %collective-permute-done.4.values_ref, bf16[512,2048]{1,0:T(8,128)(2,1)} %get-tuple-element.24._), custom_call_target="tpu_custom_call", output_to_operand_aliasing={{}: (2, {})} | custom-call | flops 1000000000 | bytes 16384 | tf_op jit(solution)/shard_map/place_cross/pallas_call | solution.py:305
  80.5 8.7 %all-to-all-done.1 = bf16[64,8,1024]{2,1,0:T(8,128)(2,1)S(1)} async-done(((bf16[64,8,1024]{2,1,0:T(8,128)(2,1)}), bf16[64,8,1024]{2,1,0:T(8,128)(2,1)S(1)}, u32[]{:S(2)}, u32[]{:S(2)}) %all-to-all-start.1) | async-done | bytes 1048608 | tf_op jit(solution)/shard_map/all_to_all | solution.py:400
  89.2 1.6 %place_columns.1 = bf16[512,2048]{1,0:T(8,128)(2,1)} custom-call(s32[2]{0:T(128)S(1)} %pad_add_fusion.flags_ref, bf16[512,1024]{1,0:T(8,128)(2,1)S(1)} %bitcast.9, bf16[512,2048]{1,0:T(8,128)(2,1)} %place_cross.1._), custom_call_target="tpu_custom_call", output_to_operand_aliasing={{}: (2, {})} | custom-call | flops 1000000000 | bytes 16384 | tf_op jit(solution)/shard_map/place_columns/pallas_call | solution.py:305
Async XLA Ops:
  0.0 12.0 %collective-permute-start = (bf16[512,2048]{1,0:T(8,128)(2,1)}, bf16[512,2048]{1,0:T(8,128)(2,1)}, u32[]{:S(2)}, u32[]{:S(2)}) collective-permute-start(bf16[512,2048]{1,0:T(8,128)(2,1)} %own_ref.1), channel_id=1, source_target_pairs={{0,1},{1,0},{2,3},{3,2},{4,5},{5,4},{6,7},{7,6},{8,9},{9,8},{10,11... | collective-permute-start | bytes 6291464 | tf_op jit(solution)/shard_map/ppermute | solution.py:407
  0.0 12.0 %copy-start = (bf16[512,2048]{1,0:T(8,128)(2,1)S(1)}, bf16[512,2048]{1,0:T(8,128)(2,1)}, u32[]{:S(2)}) copy-start(bf16[512,2048]{1,0:T(8,128)(2,1)} %own_ref.1) | copy-start | bytes 6291460
  0.0 41.7 %all-to-all-start = ((bf16[64,8,2048]{2,1,0:T(8,128)(2,1)}), bf16[64,8,2048]{2,1,0:T(8,128)(2,1)}, u32[]{:S(2)}, u32[]{:S(2)}) async-start(bf16[64,8,2048]{2,1,0:T(8,128)(2,1)} %bitcast.8), calls=%async_computation | async-start | bytes 4194304 | tf_op jit(solution)/shard_map/all_to_all | solution.py:400
  23.5 28.6 %collective-permute-start.1 = (bf16[1024,256]{1,0:T(8,128)(2,1)}, bf16[1024,256]{1,0:T(8,128)(2,1)S(1)}, u32[]{:S(2)}, u32[]{:S(2)}) collective-permute-start(bf16[1024,256]{1,0:T(8,128)(2,1)} %get-tuple-element.17.refs_2_), channel_id=1, source_target_pairs={{2,0},{3,1},{4,2},{5,3},{6,4},{7,5},{8,6},{9,7},{10,8},{11,9},{12,... | collective-permute-start | bytes 1572872 | tf_op jit(solution)/shard_map/ppermute | solution.py:417
  24.7 46.9 %collective-permute-start.2 = (bf16[2048,256]{1,0:T(8,128)(2,1)}, bf16[2048,256]{1,0:T(8,128)(2,1)}, u32[]{:S(2)}, u32[]{:S(2)}) collective-permute-start(bf16[2048,256]{1,0:T(8,128)(2,1)} %get-tuple-element.16.refs_1_), channel_id=1, source_target_pairs={{0,2},{1,3},{2,4},{3,5},{4,6},{5,7},{6,8},{7,9},{8,10},{9,11},{10,... | collective-permute-start | bytes 3145736 | tf_op jit(solution)/shard_map/ppermute | solution.py:410
  37.9 0.8 copy-start.1
  54.4 17.3 %collective-permute-start.3 = (bf16[272,1024]{1,0:T(8,128)(2,1)S(1)}, bf16[272,1024]{1,0:T(8,128)(2,1)S(1)}, u32[]{:S(2)}, u32[]{:S(2)}) collective-permute-start(bf16[272,1024]{1,0:T(8,128)(2,1)S(1)} %band_earlier.1), channel_id=1, source_target_pairs={{0,2},{1,3},{2,4},{3,5},{4,6},{5,7},{6,8},{7,9},{8,10},{9,11},{10,... | collective-permute-start | bytes 1671176 | tf_op jit(solution)/shard_map/ppermute | solution.py:410
  60.5 11.1 %copy-start.2 = (bf16[1024,256]{1,0:T(8,128)(2,1)S(1)}, bf16[1024,256]{1,0:T(8,128)(2,1)}, u32[]{:S(2)}) copy-start(bf16[1024,256]{1,0:T(8,128)(2,1)} %copy-done.1) | copy-start | bytes 1572868
  60.5 28.7 %all-to-all-start.1 = ((bf16[64,8,1024]{2,1,0:T(8,128)(2,1)}), bf16[64,8,1024]{2,1,0:T(8,128)(2,1)S(1)}, u32[]{:S(2)}, u32[]{:S(2)}) async-start(bf16[64,8,1024]{2,1,0:T(8,128)(2,1)} %bitcast.4), calls=%async_computation.1 | async-start | bytes 2097152 | tf_op jit(solution)/shard_map/all_to_all | solution.py:400
  77.2 1.9 %collective-permute-start.4 = (bf16[512,512]{1,0:T(8,128)(2,1)S(1)}, bf16[512,512]{1,0:T(8,128)(2,1)S(1)}, u32[]{:S(2)}, u32[]{:S(2)}) collective-permute-start(bf16[512,512]{1,0:T(8,128)(2,1)S(1)} %get-tuple-element.23), channel_id=1, source_target_pairs={{0,1},{1,0},{2,3},{3,2},{4,5},{5,4},{6,7},{7,6},{8,9},{9,8},{10,11... | collective-permute-start | bytes 1572872 | tf_op jit(solution)/shard_map/ppermute | solution.py:407
